TPU v7x, 256 devices: a whole 4x4x8 slice. The times are simulated.
256 devices in a mesh: slab: 32 (over x, y, core), cross: 8 (over z).
Axes of the slice: x: 4, y: 4, z: 8, core: 2. Of those that a mesh axis runs over, the one named last changes fastest.
Arguments:
- velocity: float32 [3, 128, 32, 128], P(None, 'slab', 'cross'), may hold values from -6 to 6
- acceleration: float32 [3, 128, 32, 128], P(None, 'slab', 'cross'), may hold values from -6 to 6
- grad_coef: float32 [3, 128, 32, 128], P(None, 'slab', 'cross'), may hold values from -6 to 6
- density_dev: float32 [128, 32, 128], P('slab', 'cross'), may hold values from -3 to 3
- self_weight: float32 [128, 32, 128], P('slab', 'cross'), may hold values from 0.5 to 4
- self_tiles: float32 [128, 32, 128, 128], P('slab', 'cross'), may hold values from -0.015625 to 0
- edge_tiles: float32 [128, 32, 4, 128, 128], P('slab', 'cross'), may hold values from -0.015625 to 0
- tile_count: int32 [128, 32], P('slab', 'cross'), may hold values from 1 to 4
- tile_offset: int32 [128, 32, 4], P('slab', 'cross'), may hold values from 0 to 3, as said below
- ghost_owner: int32 [32], P('cross'), may hold values from 0 to 3, as said below
- ghost_mirror: int32 [32, 128], P('cross'), may hold values from 0 to 127, as said below
- ghost_gain: float32 [32, 128], P('cross'), may hold values from 0.5 to 2
Outputs:
- pressure: float32 [128, 32, 128], P('slab', 'cross')
- residual: float32 [128, 32, 128], P('slab', 'cross')
Inputs may be any that keep to these rules, and one draw needn't show every extreme that they name: `tile_offset`: in every block row the 4 codes are all different. `ghost_owner`: each aligned group of 4 entries is a permutation of 0 to 3. `ghost_mirror`: each row is a permutation of 0 to 127.
All inputs are finite; a program needn't handle non-finite values.
Results may differ from a plain program's by a relative error of at most 0.0003.
Values sent between devices are 32-bit elements; how exact they have to be, the bound alone decides.
No kernel may reach another device: no remote copies, remote signals or barrier semaphores. Data moves between devices by JAX's collectives and lax.ppermute only.
A program may use at most 128 MiB of HBM per device.

v0:
```python
import jax
import jax.numpy as jnp
from jax import lax
from jax.sharding import PartitionSpec as P

ITERS = 2


time_step = 0.5
shift_rows = (0, 1, 1, 1)
shift_cols = (1, -1, 0, 1)
highest = lax.Precision.HIGHEST


def from_behind(value, axis, steps):
    count = lax.axis_size(axis)
    initial, last = (max(0, -steps), min(count, count - steps))
    return lax.ppermute(value, axis, [(source, source + steps) for source in range(initial, last)])


def slot_weights(tile_count, tile_offset):
    slot_count = tile_offset.shape[-1]
    live_mask = (
        lax.broadcasted_iota(jnp.int32, tile_offset.shape, tile_offset.ndim - 1)
        < tile_count[..., None]
    ).astype(jnp.float32)
    onehot = (tile_offset[..., None] == jnp.arange(slot_count, dtype=jnp.int32)).astype(jnp.float32)
    return onehot * live_mask[..., None]


def per_device(
    velocity,
    acceleration,
    grad_coef,
    density_dev,
    self_weight,
    self_tiles,
    edge_tiles,
    tile_count,
    tile_offset,
    ghost_owner,
    ghost_mirror,
    ghost_gain,
):
    row_count, col_count, block_len = self_weight.shape
    weights = slot_weights(tile_count, tile_offset)
    on_wall = lax.axis_index("slab") == lax.axis_size("slab") - 1

    def coupling(vector_in):
        east_column = from_behind(vector_in[:, 0], "cross", -1)
        west_column = from_behind(vector_in[:, col_count - 1], "cross", 1)
        widened = jnp.concatenate([west_column[:, None], vector_in, east_column[:, None]], axis=1)
        below_row = from_behind(widened[0], "slab", -1)
        padded = jnp.concatenate(
            [jnp.zeros((1, col_count + 2, block_len), jnp.float32), widened, below_row[None]],
            axis=0,
        )
        neighbours = jnp.stack(
            [
                padded[
                    1 + step_row : 1 + step_row + row_count, 1 + step_col : 1 + step_col + col_count
                ]
                for step_row, step_col in zip(shift_rows, shift_cols)
            ],
            axis=2,
        )
        result = jnp.einsum("abij,abj->abi", self_tiles, vector_in, precision=highest)
        result = result + jnp.einsum("abji,abj->abi", self_tiles, vector_in, precision=highest)
        picked = jnp.einsum("abko,abon->abkn", weights, neighbours, precision=highest)
        result = result + jnp.einsum("abkij,abkj->abi", edge_tiles, picked, precision=highest)
        transposed = jnp.einsum("abkji,abj->abki", edge_tiles, vector_in, precision=highest)
        spread = jnp.einsum("abko,abkn->abon", weights, transposed, precision=highest)
        buffer = jnp.zeros((row_count + 2, col_count + 2, block_len), jnp.float32)
        for slot_index, (step_row, step_col) in enumerate(zip(shift_rows, shift_cols)):
            buffer = buffer.at[
                1 + step_row : 1 + step_row + row_count, 1 + step_col : 1 + step_col + col_count
            ].add(spread[:, :, slot_index])
        from_west = from_behind(buffer[:, col_count + 1], "cross", 1)
        from_east = from_behind(buffer[:, 0], "cross", -1)
        buffer = buffer.at[:, 1].add(from_west)
        buffer = buffer.at[:, col_count].add(from_east)
        from_north = from_behind(buffer[row_count + 1, 1 : col_count + 1], "slab", 1)
        buffer = buffer.at[1, 1 : col_count + 1].add(from_north)
        result = result + buffer[1 : row_count + 1, 1 : col_count + 1]
        wall_row = vector_in[row_count - 1]
        mirrored = wall_row[ghost_owner[:, None], ghost_mirror]
        returned = (
            jnp.zeros_like(wall_row)
            .at[ghost_owner[:, None], ghost_mirror]
            .add(ghost_gain * wall_row)
        )
        ghost_term = jnp.where(on_wall, -(ghost_gain * mirrored + returned), 0.0)
        return result.at[row_count - 1].add(ghost_term)

    ustar = velocity + time_step * acceleration
    source = density_dev / (time_step * time_step) - jnp.sum(grad_coef * ustar, axis=0) / time_step
    degree = -coupling(jnp.ones_like(self_weight))
    diagonal = self_weight + degree
    columns = jnp.arange(col_count, dtype=jnp.int32)
    fixed_point = (
        (ghost_owner == columns)[:, None]
        & (ghost_mirror == jnp.arange(block_len, dtype=jnp.int32)[None, :])
    ).astype(jnp.float32)
    jacobi = diagonal + 2.0 * jnp.diagonal(self_tiles, axis1=2, axis2=3)
    jacobi = jacobi.at[row_count - 1].add(jnp.where(on_wall, -2.0 * ghost_gain * fixed_point, 0.0))
    pressure = jnp.zeros_like(source)
    residual = source

    def inner(left, right):
        return lax.psum(jnp.sum(left * right), ("slab", "cross"))

    scaled = residual / jacobi
    direction = scaled
    norm_now = inner(residual, scaled)
    for iteration in range(ITERS):
        applied = diagonal * direction + coupling(direction)
        step_size = norm_now / inner(direction, applied)
        pressure = pressure + step_size * direction
        residual = residual - step_size * applied
        if iteration + 1 < ITERS:
            scaled = residual / jacobi
            norm_next = inner(residual, scaled)
            direction = scaled + norm_next / norm_now * direction
            norm_now = norm_next
    return (pressure, residual)


def solution(mesh):
    in_specs = (
        P(None, "slab", "cross", None),
        P(None, "slab", "cross", None),
        P(None, "slab", "cross", None),
        P("slab", "cross", None),
        P("slab", "cross", None),
        P("slab", "cross", None, None),
        P("slab", "cross", None, None, None),
        P("slab", "cross"),
        P("slab", "cross", None),
        P("cross"),
        P("cross", None),
        P("cross", None),
    )
    out_specs = (P("slab", "cross", None), P("slab", "cross", None))
    return jax.shard_map(
        per_device, mesh=mesh, in_specs=in_specs, out_specs=out_specs, check_vma=False
    )
```

profile of v0, /device:TPU:1, one launch (start us, length us, event | category | flops | bytes accessed | tf_op | source)
XLA Modules:
  0.0 445.4 jit_solution(9102112146553521204)
XLA Ops:
  2.1 5.0 %collective-permute-start.1 = (f32[4,128]{1,0:T(4,128)S(1)}, f32[4,128]{1,0:T(4,128)S(1)}, u32[]{:S(2)}, u32[]{:S(2)}) collective-permute-start(f32[4,128]{1,0:T(4,128)S(1)} %broadcast.357), channel_id=1, source_target_pairs={{0,1},{1,2},{2,3},{3,4},{4,5},{5,6},{6,7},{8,9},{9,10},{10,11},{11... | collective-permute-start | bytes 6152 | tf_op jit(solution)/shard_map/ppermute | solution.py:18
  7.9 4.3 fusion.83
  12.8 3.5 collective-permute-start.3
  20.6 4.7 %gather_fusion = f32[512]{0:T(512)S(1)} fusion(f32[4,128]{1,0:T(4,128)S(1)} %broadcast.357, s32[512]{0:T(512)S(1)} %get-tuple-element.348), kind=kCustom, calls=%fused_computation | custom fusion | bytes 8192 | tf_op jit(solution)/shard_map/gather | solution.py:86
  25.3 16.6 %copy.103 = f32[4,4,128,128]{1,0,3,2:T(4,128)} copy(f32[4,4,128,128]{3,2,1,0:T(8,128)S(1)} %copy-done) | data formatting | bytes 2097152 | tf_op args[5]
  41.9 1.9 gather_fusion.1
  43.9 22.6 %scatter_fusion = f32[4,128]{1,0:T(4,128)S(1)} fusion(f32[4,128]{1,0:T(4,128)S(1)} %bitcast_multiply_fusion.2, s32[512]{0:T(512)S(1)} %get-tuple-element.347, f32[512]{0:T(512)S(1)} %bitcast.250), kind=kCustom, calls=%fused_computation.4 | custom fusion | flops 512 | bytes 10240 | tf_op jit(solution)/shard_map/scatter-add | solution.py:90
  66.7 4.4 collective-permute-start.5
  71.1 1.9 collective-permute-start.2
  73.1 2.9 collective-permute-done.2
  76.4 5.3 %fusion.82 = f32[4,4,1,128,1]{3,2,4,1,0:T(1,128)S(1)} fusion(f32[4,4,4,128,1]{3,4,2,1,0:T(1,128)S(1)} %bitcast.251, f32[4,4,4,128,128]{4,3,2,1,0:T(8,128)} %param.68), kind=kOutput, calls=%fused_computation.192 | convolution fusion | flops 12582912 | bytes 4235264 | tf_op jit(solution)/shard_map/abkij,abkj->abi/dot_general | solution.py:70
  83.1 1.7 fusion.55
  84.8 4.7 %gather_fusion.2 = f32[512]{0:T(512)S(1)} fusion(f32[4,128]{1,0:T(4,128)S(1)} %bitcast.231, s32[512]{0:T(512)S(1)} %get-tuple-element.348), kind=kCustom, calls=%fused_computation.2 | custom fusion | bytes 8192 | tf_op jit(solution)/shard_map/gather | solution.py:86
  89.5 22.6 %scatter_fusion.1 = f32[4,128]{1,0:T(4,128)S(1)} fusion(f32[4,128]{1,0:T(4,128)S(1)} %get-tuple-element.352, s32[512]{0:T(512)S(1)} %get-tuple-element.347, f32[512]{0:T(512)S(1)} %get-tuple-element.351), kind=kCustom, calls=%fused_computation.5 | custom fusion | flops 512 | bytes 10240 | tf_op jit(solution)/shard_map/scatter-add | solution.py:90
  113.4 4.9 %collective-permute-start.7 = (f32[4,128]{1,0:T(4,128)S(1)}, f32[4,128]{1,0:T(4,128)S(1)}, u32[]{:S(2)}, u32[]{:S(2)}) collective-permute-start(f32[4,128]{1,0:T(4,128)S(1)} %get-tuple-element.345), channel_id=1, source_target_pairs={{0,1},{1,2},{2,3},{3,4},{4,5},{5,6},{6,7},{8,9},{9,10},{10,11},{11... | collective-permute-start | bytes 6152 | tf_op jit(solution)/shard_map/ppermute | solution.py:18
  118.3 4.3 fusion.45
  123.4 4.7 %collective-permute-start.9 = (f32[6,128]{1,0:T(8,128)S(1)}, f32[6,128]{1,0:T(8,128)S(1)}, u32[]{:S(2)}, u32[]{:S(2)}) collective-permute-start(f32[6,128]{1,0:T(8,128)S(1)} %slice_bitcast_fusion.9), channel_id=1, source_target_pairs={{0,1},{1,2},{2,3},{3,4},{4,5},{5,6},{6,7},{8,9},{9,10},{10,11},{11... | collective-permute-start | bytes 9224 | tf_op jit(solution)/shard_map/ppermute | solution.py:18
  128.1 1.9 collective-permute-start.8
  134.8 4.5 %collective-permute-start.11 = (f32[4,128]{1,0:T(4,128)S(1)}, f32[4,128]{1,0:T(4,128)S(1)}, u32[]{:S(2)}, u32[]{:S(2)}) collective-permute-start(f32[4,128]{1,0:T(4,128)S(1)} %get-tuple-element.334), channel_id=1, source_target_pairs={{0,8},{8,16},{16,24},{24,32},{32,40},{40,48},{48,56},{56,64},{64,7... | collective-permute-start | bytes 6152 | tf_op jit(solution)/shard_map/ppermute | solution.py:18
  139.3 5.3 %fusion.84 = f32[4,4,1,128,1]{3,2,4,1,0:T(1,128)S(1)} fusion(f32[4,4,4,128,1]{3,4,2,1,0:T(1,128)S(1)} %bitcast.239, f32[4,4,4,128,128]{4,3,2,1,0:T(8,128)} %param.68), kind=kOutput, calls=%fused_computation.194 | convolution fusion | flops 12582912 | bytes 4235264 | tf_op jit(solution)/shard_map/abkij,abkj->abi/dot_general | solution.py:70
  145.3 83.3 %all-reduce.4 = (f32[]{:T(128)}, f32[]{:T(128)}) all-reduce(f32[]{:T(128)} %get-tuple-element.309, f32[]{:T(128)} %get-tuple-element.308), channel_id=1, replica_groups=mesh['slab'=32,'cross'=8] {'slab','cross'}, use_global_device_ids=true, to_apply=%region_3.0 | all-reduce | flops 2 | bytes 16 | tf_op jit(solution)/shard_map/psum | solution.py:110
  230.6 72.8 %psum.30 = f32[]{:T(128)} all-reduce(f32[]{:T(128)} %get-tuple-element.312), channel_id=1, replica_groups=mesh['slab'=32,'cross'=8] {'slab','cross'}, use_global_device_ids=true, to_apply=%region_8.0 | all-reduce | flops 1 | bytes 8 | tf_op jit(solution)/shard_map/psum | solution.py:110
  307.5 4.7 %gather_fusion.3 = f32[512]{0:T(512)S(1)} fusion(f32[4,128]{1,0:T(4,128)S(1)} %bitcast.229, s32[512]{0:T(512)S(1)} %get-tuple-element.348), kind=kCustom, calls=%fused_computation.3 | custom fusion | bytes 8192 | tf_op jit(solution)/shard_map/gather | solution.py:86
  313.5 4.3 collective-permute-start.13
  317.8 4.3 fusion.43
  322.9 3.4 collective-permute-start.15
  326.2 22.6 %scatter_fusion.2 = f32[4,128]{1,0:T(4,128)S(1)} fusion(f32[4,128]{1,0:T(4,128)S(1)} %get-tuple-element.350, s32[512]{0:T(512)S(1)} %get-tuple-element.347, f32[512]{0:T(512)S(1)} %get-tuple-element.349), kind=kCustom, calls=%fused_computation.6 | custom fusion | flops 512 | bytes 10240 | tf_op jit(solution)/shard_map/scatter-add | solution.py:90
  348.9 3.4 collective-permute-start.14
  354.9 2.0 collective-permute-done.16
  356.9 3.8 collective-permute-start.17
  360.7 5.3 %fusion.85 = f32[4,4,1,128,1]{3,2,4,1,0:T(1,128)S(1)} fusion(f32[4,4,4,128,1]{3,4,2,1,0:T(1,128)S(1)} %bitcast.240, f32[4,4,4,128,128]{4,3,2,1,0:T(8,128)} %param.68), kind=kOutput, calls=%fused_computation.195 | convolution fusion | flops 12582912 | bytes 4235264 | tf_op jit(solution)/shard_map/abkij,abkj->abi/dot_general | solution.py:70
  366.8 76.1 %psum.31 = f32[]{:T(128)} all-reduce(f32[]{:T(128)} %multiply_reduce_fusion.1), channel_id=1, replica_groups=mesh['slab'=32,'cross'=8] {'slab','cross'}, use_global_device_ids=true, to_apply=%region_11.12 | all-reduce | flops 1 | bytes 8 | tf_op jit(solution)/shard_map/psum | solution.py:110
  (163 shorter events, 26.0 us)
Async XLA Ops:
  0.6 11.6 %copy-start.1 = (s32[4,4,4]{2,1,0:T(4,128)S(1)}, s32[4,4,4]{2,1,0:T(4,128)}, u32[]{:S(2)}) copy-start(s32[4,4,4]{2,1,0:T(4,128)} %param.70) | copy-start | bytes 772
  0.6 17.1 %copy-start = (f32[4,4,128,128]{3,2,1,0:T(8,128)S(1)}, f32[4,4,128,128]{3,2,1,0:T(8,128)}, u32[]{:S(2)}) copy-start(f32[4,4,128,128]{3,2,1,0:T(8,128)} %param.67) | copy-start | bytes 3145732
  0.7 19.8 %copy-start.9 = (s32[4]{0:T(128)S(1)}, s32[4]{0:T(128)}, u32[]{:S(2)}) copy-start(s32[4]{0:T(128)} %param.71) | copy-start | bytes 52
  0.7 19.8 %copy-start.8 = (s32[4,128]{1,0:T(4,128)S(1)}, s32[4,128]{1,0:T(4,128)}, u32[]{:S(2)}) copy-start(s32[4,128]{1,0:T(4,128)} %param.72) | copy-start | bytes 6148
  0.7 65.9 %collective-permute-start = (f32[4,128]{1,0:T(4,128)S(1)}, f32[4,128]{1,0:T(4,128)S(1)}, u32[]{:S(2)}, u32[]{:S(2)}) collective-permute-start(f32[4,128]{1,0:T(4,128)S(1)} %broadcast.357), channel_id=1, source_target_pairs={{1,0},{2,1},{3,2},{4,3},{5,4},{6,5},{7,6},{9,8},{10,9},{11,10},{12... | collective-permute-start | bytes 6152 | tf_op jit(solution)/shard_map/ppermute | solution.py:18
  2.1 69.0 %collective-permute-start.1 = (f32[4,128]{1,0:T(4,128)S(1)}, f32[4,128]{1,0:T(4,128)S(1)}, u32[]{:S(2)}, u32[]{:S(2)}) collective-permute-start(f32[4,128]{1,0:T(4,128)S(1)} %broadcast.357), channel_id=1, source_target_pairs={{0,1},{1,2},{2,3},{3,4},{4,5},{5,6},{6,7},{8,9},{9,10},{10,11},{11... | collective-permute-start | bytes 6152 | tf_op jit(solution)/shard_map/ppermute | solution.py:18
  7.9 17.4 %copy-start.3 = (f32[4,128]{1,0:T(4,128)S(1)}, f32[4,128]{1,0:T(4,128)}, u32[]{:S(2)}) copy-start(f32[4,128]{1,0:T(4,128)} %param.73) | copy-start | bytes 6148
  7.9 17.4 %copy-start.4 = (f32[3,4,4,128]{3,2,1,0:T(4,128)S(1)}, f32[3,4,4,128]{3,2,1,0:T(4,128)}, u32[]{:S(2)}) copy-start(f32[3,4,4,128]{3,2,1,0:T(4,128)} %param.64) | copy-start | bytes 73732
  7.9 17.4 %copy-start.5 = (f32[3,4,4,128]{3,2,1,0:T(4,128)S(1)}, f32[3,4,4,128]{3,2,1,0:T(4,128)}, u32[]{:S(2)}) copy-start(f32[3,4,4,128]{3,2,1,0:T(4,128)} %param.62) | copy-start | bytes 73732
  7.9 17.4 %copy-start.6 = (f32[3,4,4,128]{3,2,1,0:T(4,128)S(1)}, f32[3,4,4,128]{3,2,1,0:T(4,128)}, u32[]{:S(2)}) copy-start(f32[3,4,4,128]{3,2,1,0:T(4,128)} %param.63) | copy-start | bytes 73732
  12.8 53.8 %collective-permute-start.3 = (f32[6,128]{1,0:T(8,128)S(1)}, f32[6,128]{1,0:T(8,128)S(1)}, u32[]{:S(2)}, u32[]{:S(2)}) collective-permute-start(f32[6,128]{1,0:T(8,128)S(1)} %slice_bitcast_fusion.10), channel_id=1, source_target_pairs={{0,1},{1,2},{2,3},{3,4},{4,5},{5,6},{6,7},{8,9},{9,10},{10,11},{11... | collective-permute-start | bytes 9224 | tf_op jit(solution)/shard_map/ppermute | solution.py:18
  16.4 50.2 %collective-permute-start.4 = (f32[6,128]{1,0:T(8,128)S(1)}, f32[6,128]{1,0:T(8,128)S(1)}, u32[]{:S(2)}, u32[]{:S(2)}) collective-permute-start(f32[6,128]{1,0:T(8,128)S(1)} %bitcast.284), channel_id=1, source_target_pairs={{1,0},{2,1},{3,2},{4,3},{5,4},{6,5},{7,6},{9,8},{10,9},{11,10},{12... | collective-permute-start | bytes 9224 | tf_op jit(solution)/shard_map/ppermute | solution.py:18
  43.9 38.0 %copy-start.7 = (f32[4,4,128]{2,1,0:T(4,128)S(1)}, f32[4,4,128]{2,1,0:T(4,128)}, u32[]{:S(2)}) copy-start(f32[4,4,128]{2,1,0:T(4,128)} %param.66) | copy-start | bytes 24580
  43.9 38.1 %copy-start.2 = (f32[4,4,128]{2,1,0:T(4,128)S(1)}, f32[4,4,128]{2,1,0:T(4,128)}, u32[]{:S(2)}) copy-start(f32[4,4,128]{2,1,0:T(4,128)} %param.65) | copy-start | bytes 24580
  66.7 6.4 %collective-permute-start.5 = (f32[4,128]{1,0:T(4,128)S(1)}, f32[4,128]{1,0:T(4,128)S(1)}, u32[]{:S(2)}, u32[]{:S(2)}) collective-permute-start(f32[4,128]{1,0:T(4,128)S(1)} %bitcast.289), channel_id=1, source_target_pairs={{0,8},{8,16},{16,24},{24,32},{32,40},{40,48},{48,56},{56,64},{64,7... | collective-permute-start | bytes 6152 | tf_op jit(solution)/shard_map/ppermute | solution.py:18
  71.1 4.9 %collective-permute-start.2 = (f32[6,128]{1,0:T(8,128)S(1)}, f32[6,128]{1,0:T(8,128)S(1)}, u32[]{:S(2)}, u32[]{:S(2)}) collective-permute-start(f32[6,128]{1,0:T(8,128)S(1)} %fusion.61), channel_id=1, source_target_pairs={{8,0},{16,8},{24,16},{32,24},{40,32},{48,40},{56,48},{64,56},{72,6... | collective-permute-start | bytes 9224 | tf_op jit(solution)/shard_map/ppermute | solution.py:18
  112.1 15.9 %collective-permute-start.6 = (f32[4,128]{1,0:T(4,128)S(1)}, f32[4,128]{1,0:T(4,128)S(1)}, u32[]{:S(2)}, u32[]{:S(2)}) collective-permute-start(f32[4,128]{1,0:T(4,128)S(1)} %get-tuple-element.346), channel_id=1, source_target_pairs={{1,0},{2,1},{3,2},{4,3},{5,4},{6,5},{7,6},{9,8},{10,9},{11,10},{12... | collective-permute-start | bytes 6152 | tf_op jit(solution)/shard_map/ppermute | solution.py:18
  113.4 14.6 %collective-permute-start.7 = (f32[4,128]{1,0:T(4,128)S(1)}, f32[4,128]{1,0:T(4,128)S(1)}, u32[]{:S(2)}, u32[]{:S(2)}) collective-permute-start(f32[4,128]{1,0:T(4,128)S(1)} %get-tuple-element.345), channel_id=1, source_target_pairs={{0,1},{1,2},{2,3},{3,4},{4,5},{5,6},{6,7},{8,9},{9,10},{10,11},{11... | collective-permute-start | bytes 6152 | tf_op jit(solution)/shard_map/ppermute | solution.py:18
  123.4 6.7 %collective-permute-start.9 = (f32[6,128]{1,0:T(8,128)S(1)}, f32[6,128]{1,0:T(8,128)S(1)}, u32[]{:S(2)}, u32[]{:S(2)}) collective-permute-start(f32[6,128]{1,0:T(8,128)S(1)} %slice_bitcast_fusion.9), channel_id=1, source_target_pairs={{0,1},{1,2},{2,3},{3,4},{4,5},{5,6},{6,7},{8,9},{9,10},{10,11},{11... | collective-permute-start | bytes 9224 | tf_op jit(solution)/shard_map/ppermute | solution.py:18
  128.1 4.9 %collective-permute-start.8 = (f32[6,128]{1,0:T(8,128)S(1)}, f32[6,128]{1,0:T(8,128)S(1)}, u32[]{:S(2)}, u32[]{:S(2)}) collective-permute-start(f32[6,128]{1,0:T(8,128)S(1)} %bitcast.285), channel_id=1, source_target_pairs={{8,0},{16,8},{24,16},{32,24},{40,32},{48,40},{56,48},{64,56},{72,6... | collective-permute-start | bytes 9224 | tf_op jit(solution)/shard_map/ppermute | solution.py:18
  130.1 4.6 %collective-permute-start.10 = (f32[6,128]{1,0:T(8,128)S(1)}, f32[6,128]{1,0:T(8,128)S(1)}, u32[]{:S(2)}, u32[]{:S(2)}) collective-permute-start(f32[6,128]{1,0:T(8,128)S(1)} %get-tuple-element.336), channel_id=1, source_target_pairs={{1,0},{2,1},{3,2},{4,3},{5,4},{6,5},{7,6},{9,8},{10,9},{11,10},{12... | collective-permute-start | bytes 9224 | tf_op jit(solution)/shard_map/ppermute | solution.py:18
  134.8 9.8 %collective-permute-start.11 = (f32[4,128]{1,0:T(4,128)S(1)}, f32[4,128]{1,0:T(4,128)S(1)}, u32[]{:S(2)}, u32[]{:S(2)}) collective-permute-start(f32[4,128]{1,0:T(4,128)S(1)} %get-tuple-element.334), channel_id=1, source_target_pairs={{0,8},{8,16},{16,24},{24,32},{32,40},{40,48},{48,56},{56,64},{64,7... | collective-permute-start | bytes 6152 | tf_op jit(solution)/shard_map/ppermute | solution.py:18
  312.2 36.7 %collective-permute-start.12 = (f32[4,128]{1,0:T(4,128)S(1)}, f32[4,128]{1,0:T(4,128)S(1)}, u32[]{:S(2)}, u32[]{:S(2)}) collective-permute-start(f32[4,128]{1,0:T(4,128)S(1)} %get-tuple-element.344), channel_id=1, source_target_pairs={{1,0},{2,1},{3,2},{4,3},{5,4},{6,5},{7,6},{9,8},{10,9},{11,10},{12... | collective-permute-start | bytes 6152 | tf_op jit(solution)/shard_map/ppermute | solution.py:18
  313.5 35.4 %collective-permute-start.13 = (f32[4,128]{1,0:T(4,128)S(1)}, f32[4,128]{1,0:T(4,128)S(1)}, u32[]{:S(2)}, u32[]{:S(2)}) collective-permute-start(f32[4,128]{1,0:T(4,128)S(1)} %get-tuple-element.343), channel_id=1, source_target_pairs={{0,1},{1,2},{2,3},{3,4},{4,5},{5,6},{6,7},{8,9},{9,10},{10,11},{11... | collective-permute-start | bytes 6152 | tf_op jit(solution)/shard_map/ppermute | solution.py:18
  322.9 29.5 %collective-permute-start.15 = (f32[6,128]{1,0:T(8,128)S(1)}, f32[6,128]{1,0:T(8,128)S(1)}, u32[]{:S(2)}, u32[]{:S(2)}) collective-permute-start(f32[6,128]{1,0:T(8,128)S(1)} %slice_bitcast_fusion.7), channel_id=1, source_target_pairs={{0,1},{1,2},{2,3},{3,4},{4,5},{5,6},{6,7},{8,9},{9,10},{10,11},{11... | collective-permute-start | bytes 9224 | tf_op jit(solution)/shard_map/ppermute | solution.py:18
  348.9 5.6 %collective-permute-start.14 = (f32[6,128]{1,0:T(8,128)S(1)}, f32[6,128]{1,0:T(8,128)S(1)}, u32[]{:S(2)}, u32[]{:S(2)}) collective-permute-start(f32[6,128]{1,0:T(8,128)S(1)} %bitcast.286), channel_id=1, source_target_pairs={{8,0},{16,8},{24,16},{32,24},{40,32},{48,40},{56,48},{64,56},{72,6... | collective-permute-start | bytes 9224 | tf_op jit(solution)/shard_map/ppermute | solution.py:18
  352.4 4.5 %collective-permute-start.16 = (f32[6,128]{1,0:T(8,128)S(1)}, f32[6,128]{1,0:T(8,128)S(1)}, u32[]{:S(2)}, u32[]{:S(2)}) collective-permute-start(f32[6,128]{1,0:T(8,128)S(1)} %get-tuple-element.329), channel_id=1, source_target_pairs={{1,0},{2,1},{3,2},{4,3},{5,4},{6,5},{7,6},{9,8},{10,9},{11,10},{12... | collective-permute-start | bytes 9224 | tf_op jit(solution)/shard_map/ppermute | solution.py:18
  356.9 9.1 %collective-permute-start.17 = (f32[4,128]{1,0:T(4,128)S(1)}, f32[4,128]{1,0:T(4,128)S(1)}, u32[]{:S(2)}, u32[]{:S(2)}) collective-permute-start(f32[4,128]{1,0:T(4,128)S(1)} %slice_bitcast_fusion.11), channel_id=1, source_target_pairs={{0,8},{8,16},{16,24},{24,32},{32,40},{40,48},{48,56},{56,64},{64,7... | collective-permute-start | bytes 6152 | tf_op jit(solution)/shard_map/ppermute | solution.py:18
where the time goes:
time: 447 us; the launch traced here: 445 us
  blocking collectives  232 us (52%)
  other arithmetic  71 us (16%)
  starting transfers between devices  53.6 us (12%)
  matrix products  38.4 us (9%)
  local copies, waits for them, and re-layouts  35.6 us (8%)
  waiting for transfers between devices  8.76 us (2%)
  between operations  5.8 us (1%)
    psum x3, blocking collectives, inner(): return lax.psum(jnp.sum(left * right), ('slab', 'cross'))  232 us
    scatter-add x3, other arithmetic, coupling(): returned = jnp.zeros_like(wall_row).at[ghost_owner[:, None], ghost_mirror...  67.9 us
    ppermute x18, starting transfers between devices, from_behind(): lax.ppermute(value, axis, [(source, source + steps) for source in range(i...  53.6 us
    unnamed x28, local copies, waits for them, and re-layouts  17.9 us
    dot_general x3, matrix products, coupling(): jnp.einsum('abkij,abkj->abi', edge_tiles, picked, precision=highest)  15.8 us
    gather x3, local copies, waits for them, and re-layouts, coupling(): mirrored = wall_row[ghost_owner[:, None], ghost_mirror]  14 us
    dot_general x3, matrix products, coupling(): jnp.einsum('abkji,abj->abki', edge_tiles, vector_in, precision=highest)  12.8 us
  transfers between devices with their start and end apart: 18, of which 5 were waited for; matrix products, arithmetic and copies ran while one was open for 22% of the time, Pallas kernels for 0%

commit v1 on v0

v1 whole, which is shorter than its diff:
```python
import functools

import jax
import jax.numpy as jnp
from jax import lax
from jax.experimental import pallas as pl
from jax.experimental.pallas import tpu as pltpu
from jax.sharding import PartitionSpec as P

STRIDE = 8
DUMMY = 7
CODE_STEP = (1, STRIDE - 1, STRIDE, STRIDE + 1)

VMEM = pl.BlockSpec(memory_space=pltpu.VMEM)
SMEM = pl.BlockSpec(memory_space=pltpu.SMEM)
f32 = jnp.float32


def apply_tiles(
    table, mirror_ref, gain_ref, self_ref, edge_ref, p_ref, v_ref, rows, cols, size
):
    lane = lax.broadcasted_iota(jnp.int32, (size, size), 1)
    sub = lax.broadcasted_iota(jnp.int32, (size, size), 0)
    eye = lane == sub
    columns = jnp.transpose(p_ref[...])
    mirror = jnp.transpose(mirror_ref[...])
    gain = jnp.transpose(gain_ref[...])
    lanef = lane.astype(f32)
    sums = jnp.zeros((size, size), f32)
    slots = edge_ref.shape[0] // (rows * cols)
    for r in range(rows):
        for c in range(cols):
            block = r * cols + c
            at = r * STRIDE + c + 1
            down = jnp.broadcast_to(columns[:, at : at + 1], (size, size))
            tile = jnp.where(eye, 0.0, self_ref[block])
            acc = tile * p_ref[at : at + 1, :]
            v_ref[at : at + 1, :] += jnp.sum(tile * down, axis=0, keepdims=True)
            for k in range(slots):
                j = table[block * slots + k]
                tile = edge_ref[block * slots + k]
                acc += tile * p_ref[pl.ds(j, 1), :]
                v_ref[pl.ds(j, 1), :] += jnp.sum(tile * down, axis=0, keepdims=True)
            if r == rows - 1:
                owner = table[rows * cols * slots + c]
                same = jnp.broadcast_to(owner == c, (size, size))
                hit = (lanef == mirror[:, c : c + 1]) & ~(same & eye)
                tile = jnp.where(hit, gain[:, c : c + 1], 0.0)
                j = r * STRIDE + 1 + owner
                acc += tile * p_ref[pl.ds(j, 1), :]
                v_ref[pl.ds(j, 1), :] += jnp.sum(tile * down, axis=0, keepdims=True)
            sums = jnp.where(lane == at, jnp.sum(acc, axis=1, keepdims=True), sums)
    v_ref[...] += jnp.transpose(sums)[: v_ref.shape[0], :]


def pack_sides(v_ref, east_ref, west_ref, rows, cols):
    for r in range(rows + 1):
        east_ref[2 * r : 2 * r + 2, :] = v_ref[r * STRIDE + cols : r * STRIDE + cols + 2, :]
        west_ref[2 * r : 2 * r + 2, :] = v_ref[r * STRIDE : r * STRIDE + 2, :]


def first_kernel(
    rows, cols, table, vel, acc, grad, dens, weight, mirror, gain, self_ref, edge_ref, valid,
    v_out, src_out, east, west, p_ref,
):
    size = p_ref.shape[1]
    p_ref[...] = jnp.zeros_like(p_ref)
    p_ref[: valid.shape[0], :] = valid[...]
    v_out[...] = jnp.zeros_like(v_out)
    src_out[...] = jnp.zeros_like(src_out)
    east[...] = jnp.zeros_like(east)
    west[...] = jnp.zeros_like(west)
    for r in range(rows):
        lo = r * STRIDE + 1
        total = jnp.zeros((cols, size), f32)
        for d in range(3):
            total += grad[d, r] * (vel[d, r] + 0.5 * acc[d, r])
        src = dens[r] / 0.25 - total / 0.5
        src_out[lo : lo + cols, :] = src
        v_out[lo : lo + cols, :] = -weight[r]
        east[2 * (rows + 1) + r : 2 * (rows + 1) + r + 1, :] = src[cols - 1 : cols, :]
        west[2 * (rows + 1) + r : 2 * (rows + 1) + r + 1, :] = src[0:1, :]
    apply_tiles(table, mirror, gain, self_ref, edge_ref, p_ref, v_out, rows, cols, size)
    pack_sides(v_out, east, west, rows, cols)


def second_kernel(
    rows, cols, table, mirror, gain, self_ref, edge_ref, valid, total, src,
    v_out, s_out, jac_out, east, west, p_ref,
):
    size = p_ref.shape[1]
    inside = valid[...] > 0.0
    jac = jnp.where(inside, -total[...], 1.0)
    s = jnp.where(inside, src[...] / jac, 0.0)
    p_ref[...] = jnp.zeros_like(p_ref)
    p_ref[: s.shape[0], :] = s
    s_out[...] = s
    jac_out[...] = jac
    v_out[...] = jnp.zeros_like(v_out)
    east[...] = jnp.zeros_like(east)
    west[...] = jnp.zeros_like(west)
    apply_tiles(table, mirror, gain, self_ref, edge_ref, p_ref, v_out, rows, cols, size)
    pack_sides(v_out, east, west, rows, cols)


def third_kernel(
    rows, cols, table, mirror, gain, self_ref, edge_ref, valid, total, src, s_ref, jac,
    v_out, w_out, east, west, sums_out, p_ref,
):
    size = p_ref.shape[1]
    inside = valid[...] > 0.0
    u = total[...]
    w = jnp.where(inside, u / jac[...], 0.0)
    p_ref[...] = jnp.zeros_like(p_ref)
    p_ref[: w.shape[0], :] = w
    w_out[...] = w
    v_out[...] = jnp.zeros_like(v_out)
    east[...] = jnp.zeros_like(east)
    west[...] = jnp.zeros_like(west)
    apply_tiles(table, mirror, gain, self_ref, edge_ref, p_ref, v_out, rows, cols, size)
    pack_sides(v_out, east, west, rows, cols)
    at = lax.broadcasted_iota(jnp.int32, u.shape, 0)
    column = at % STRIDE
    own = (at < rows * STRIDE) & (column >= 1) & (column <= cols)
    s = s_ref[...]

    def whole(x):
        return jnp.sum(jnp.sum(x, axis=0, keepdims=True), axis=1, keepdims=True)

    sums = (
        whole(jnp.where(own, src[...] * s, 0.0)),
        whole(jnp.where(own, s * u, 0.0)),
        whole(jnp.where(own, w * u, 0.0)),
        whole(w * v_out[...]),
    )
    lane = lax.broadcasted_iota(jnp.int32, (1, size), 1)
    line = jnp.zeros((1, size), f32)
    for k, value in enumerate(sums):
        line = jnp.where(lane == k, value, line)
    sums_out[...] = jnp.broadcast_to(line, sums_out.shape)


def last_kernel(rows, cols, gathered, v, s_ref, jac_ref, w_ref, pressure, residual):
    nu = jnp.sum(gathered[...], axis=0, keepdims=True)
    nu0, nu1, nu2, nu3 = (nu[:, k : k + 1] for k in range(4))
    rho = nu1 / nu0
    a0 = 1.0 / (1.0 + rho)
    norm1 = a0 * a0 * (nu2 - rho * nu1)
    beta = norm1 / nu0
    g = a0 * rho + beta
    cross = g * g * nu1 - 2.0 * g * a0 * nu2 + a0 * a0 * nu3
    sigma = jnp.where(norm1 > 0.0, beta + cross / norm1, 0.0)
    step = 1.0 / (1.0 + sigma)
    rest = sigma * step
    ps, pw = a0 + step * g, -step * a0
    rs, rw, rv = a0 * rho * rest - step * beta, -a0 * rest - step * g, step * a0
    for r in range(rows):
        lo = r * STRIDE + 1
        s, w, jac = s_ref[lo : lo + cols, :], w_ref[lo : lo + cols, :], jac_ref[lo : lo + cols, :]
        pressure[r] = ps * s + pw * w
        residual[r] = jac * (rs * s + rw * w) + rv * v[lo : lo + cols, :]


def shift(value, axis, step):
    count = lax.axis_size(axis)
    return lax.ppermute(value, axis, [(i, (i + step) % count) for i in range(count)])


def per_device(
    velocity,
    acceleration,
    grad_coef,
    density_dev,
    self_weight,
    self_tiles,
    edge_tiles,
    tile_count,
    tile_offset,
    ghost_owner,
    ghost_mirror,
    ghost_gain,
):
    rows, cols, size = self_weight.shape
    slots = tile_offset.shape[-1]
    region = (rows + 1) * STRIDE
    side = STRIDE * pl.cdiv(2 * (rows + 1) + rows, STRIDE)
    slab, cross = lax.axis_index("slab"), lax.axis_index("cross")
    n_slab, n_cross = lax.axis_size("slab"), lax.axis_size("cross")
    has_north, has_south = slab > 0, slab < n_slab - 1
    has_west, has_east = cross > 0, cross < n_cross - 1

    here = (
        jnp.arange(rows, dtype=jnp.int32)[:, None] * STRIDE
        + jnp.arange(cols, dtype=jnp.int32)[None, :]
        + 1
    )
    step = jnp.zeros_like(tile_offset)
    for code, distance in enumerate(CODE_STEP):
        step = jnp.where(tile_offset == code, distance, step)
    live = lax.broadcasted_iota(jnp.int32, tile_offset.shape, 2) < tile_count[..., None]
    target = jnp.where(live, here[..., None] + step, DUMMY)
    table = jnp.concatenate([target.reshape(-1), ghost_owner])
    mirror = jnp.zeros((size, size), f32).at[:cols].set(ghost_mirror.astype(f32))
    gain = jnp.zeros((size, size), f32).at[:cols].set(
        jnp.where(has_south, 0.0, -ghost_gain)
    )
    at = lax.broadcasted_iota(jnp.int32, (region, size), 0)
    column = at % STRIDE
    valid = (
        (column <= cols + 1)
        & ((column > 0) | has_west)
        & ((column <= cols) | has_east)
        & ((at < rows * STRIDE) | has_south)
    ).astype(f32)
    selfs = self_tiles.reshape(rows * cols, size, size)
    edges = edge_tiles.reshape(rows * cols * slots, size, size)

    def call(kernel, shapes, scratch, *operands):
        return pl.pallas_call(
            functools.partial(kernel, rows, cols),
            out_shape=[jax.ShapeDtypeStruct(shape, f32) for shape in shapes],
            in_specs=[SMEM if x is table else VMEM for x in operands],
            out_specs=[VMEM] * len(shapes),
            scratch_shapes=[pltpu.VMEM((size, size), f32)] if scratch else [],
        )(*operands)

    def merge_sides(v, east, west):
        from_west = jnp.where(has_west, shift(east, "cross", 1), 0.0)
        from_east = jnp.where(has_east, shift(west, "cross", -1), 0.0)
        pair = (rows + 1, 2, size)
        gap = jnp.zeros(pair, f32)
        head = 2 * (rows + 1)
        parts = [from_west[:head].reshape(pair), gap, from_east[:head].reshape(pair), gap]
        return (
            v.reshape(rows + 1, STRIDE, size) + jnp.concatenate(parts, axis=1),
            from_west[head : head + rows],
            from_east[head : head + rows],
        )

    v, src, east, west = call(
        first_kernel,
        [(region, size), (region, size), (side, size), (side, size)],
        True,
        table, velocity, acceleration, grad_coef, density_dev, self_weight,
        mirror, gain, selfs, edges, valid,
    )
    total, src_west, src_east = merge_sides(v, east, west)
    src3 = src.reshape(rows + 1, STRIDE, size)
    src3 = src3.at[:rows, 0].set(src_west).at[:rows, cols + 1].set(src_east)
    from_north = shift(total[rows], "slab", 1)
    from_south = shift(jnp.concatenate([total[0], src3[0]], axis=0), "slab", -1)
    total = total.at[0].add(jnp.where(has_north, from_north, 0.0))
    total = total.at[rows].add(from_south[:STRIDE])
    src3 = src3.at[rows].set(from_south[STRIDE:])
    src = src3.reshape(region, size)

    v, s, jac, east, west = call(
        second_kernel,
        [(region, size)] * 3 + [(side, size)] * 2,
        True,
        table, mirror, gain, selfs, edges, valid, total.reshape(region, size), src,
    )
    total, _, _ = merge_sides(v, east, west)
    from_north = shift(total[rows], "slab", 1)
    from_south = shift(total[0], "slab", -1)
    total = total.at[0].add(jnp.where(has_north, from_north, 0.0))
    total = total.at[rows].add(from_south)

    v, w, east, west, sums = call(
        third_kernel,
        [(region, size)] * 2 + [(side, size)] * 2 + [(n_slab * n_cross, size)],
        True,
        table, mirror, gain, selfs, edges, valid, total.reshape(region, size), src, s, jac,
    )
    total, _, _ = merge_sides(v, east, west)
    from_north = shift(total[rows], "slab", 1)
    total = total.at[0].add(jnp.where(has_north, from_north, 0.0))
    gathered = lax.all_to_all(sums, ("slab", "cross"), 0, 0, tiled=True)

    pressure, residual = call(
        last_kernel,
        [(rows, cols, size)] * 2,
        False,
        gathered, total.reshape(region, size), s, jac, w,
    )
    return (pressure, residual)


def solution(mesh):
    in_specs = (
        P(None, "slab", "cross", None),
        P(None, "slab", "cross", None),
        P(None, "slab", "cross", None),
        P("slab", "cross", None),
        P("slab", "cross", None),
        P("slab", "cross", None, None),
        P("slab", "cross", None, None, None),
        P("slab", "cross"),
        P("slab", "cross", None),
        P("cross"),
        P("cross", None),
        P("cross", None),
    )
    out_specs = (P("slab", "cross", None), P("slab", "cross", None))
    return jax.shard_map(
        per_device, mesh=mesh, in_specs=in_specs, out_specs=out_specs, check_vma=False
    )
```

time: 447 us -> 84.5 us (0.19)
  blocking collectives: 232 us -> 0 us
  other arithmetic: 71 us -> 9.17 us
  matrix products: 38.4 us -> 0 us
  local copies, waits for them, and re-layouts: 35.6 us -> 6.78 us
  Pallas kernels: 0 us -> 16.5 us
  starting transfers between devices: 53.6 us -> 39 us
  between operations: 5.8 us -> 0.84 us
    psum x3 -> x0, blocking collectives: 232 us -> none  [inner(): return lax.psum(jnp.sum(left * right), ('slab', 'cross'))]
    scatter-add x8 -> x3, other arithmetic: 68 us -> 0.01 us  [the longest x1 0.01 us: per_device(): total = total.at[0].add(jnp.where(has_north, from_north, 0.0))]
    dot_general x18 -> x0, matrix products: 38.4 us -> none  [the longest x3 15.8 us: coupling(): jnp.einsum('abkij,abkj->abi', edge_tiles, picked, precision=highest)]
    ppermute x18 -> x11, starting transfers between devices: 53.6 us -> 29.1 us  [shift(): lax.ppermute(value, axis, [(i, (i + step) % count) for i in range(count)])]
    pallas_call x0 -> x4, Pallas kernels: none -> 16.5 us  [call(): pl.pallas_call(functools.partial(kernel, rows, cols), out_shape=[jax.Shap...]
    unnamed x28 -> x10, local copies, waits for them, and re-layouts: 17.9 us -> 1.85 us
    gather x5 -> x0, local copies, waits for them, and re-layouts: 16 us -> none  [the longest x3 14 us: coupling(): mirrored = wall_row[ghost_owner[:, None], ghost_mirror]]
    all_to_all x0 -> x1, starting transfers between devices: none -> 9.86 us  [per_device(): gathered = lax.all_to_all(sums, ('slab', 'cross'), 0, 0, tiled=True)]
  transfers between devices with their start and end apart: 18 -> 12, of which waited for: 5 -> 7; matrix products, arithmetic and copies ran while one was open for 22% -> 8% of each run, Pallas kernels for 0% -> 0%
where the time goes in v1:
time: 84.5 us; the launch traced here: 84 us
  starting transfers between devices  39 us (46%)
  Pallas kernels  16.5 us (20%)
  waiting for transfers between devices  11.7 us (14%)
  other arithmetic  9.17 us (11%)
  local copies, waits for them, and re-layouts  6.78 us (8%)
    ppermute x11, starting transfers between devices, shift(): lax.ppermute(value, axis, [(i, (i + step) % count) for i in range(count)])  29.1 us
    pallas_call x4, Pallas kernels, call(): pl.pallas_call(functools.partial(kernel, rows, cols), out_shape=[jax.Shap...  16.5 us
    all_to_all x1, starting transfers between devices, per_device(): gathered = lax.all_to_all(sums, ('slab', 'cross'), 0, 0, tiled=True)  9.86 us
    ppermute x11, waiting for transfers between devices, shift(): lax.ppermute(value, axis, [(i, (i + step) % count) for i in range(count)])  8.12 us
    all_to_all x1, waiting for transfers between devices, per_device(): gathered = lax.all_to_all(sums, ('slab', 'cross'), 0, 0, tiled=True)  3.62 us
    another operation x3, other arithmetic  2.73 us
    add x3, other arithmetic, merge_sides(): v.reshape(rows + 1, STRIDE, size) + jnp.concatenate(parts, axis=1)  2.24 us
    unnamed x10, local copies, waits for them, and re-layouts  1.85 us
  transfers between devices with their start and end apart: 12, of which 7 were waited for; matrix products, arithmetic and copies ran while one was open for 8% of the time, Pallas kernels for 0%

profile of v1, /device:TPU:1, one launch (start us, length us, event | category | flops | bytes accessed | tf_op | source)
XLA Modules:
  0.0 84.0 jit_solution(17737779030730505552)
XLA Ops:
  2.1 0.8 add_select_fusion
  4.3 1.2 %pad_add_fusion.table = s32[68]{0:T(128)} fusion(s32[4]{0:T(128)} %param.41, s32[64]{0:T(128)S(1)} %reshape.383), kind=kLoop, calls=%fused_computation.56 | loop fusion | flops 68 | bytes 544 | tf_op jit(solution)/shard_map/concatenate | solution.py:202
  5.5 0.7 fusion.9.valid
  6.2 4.8 %shard_map.131 = (f32[40,128]{1,0:T(8,128)}, f32[40,128]{1,0:T(8,128)}, f32[16,128]{1,0:T(8,128)}, f32[16,128]{1,0:T(8,128)}) custom-call(s32[68]{0:T(128)} %pad_add_fusion.table, f32[3,4,4,128]{3,2,1,0:T(4,128)} %vel.1, f32[3,4,4,128]{3,2,1,0:T(4,128)} %acc.1, f32[3,4,4,128]{3,2,1,0:T(4,128)} %grad.1, f32[4,4,128]{2,1,0:T(4,128)} %dens.1, ...), custom_call_target="tpu_custom_call" | custom-call | tf_op jit(solution)/shard_map/pallas_call | solution.py:219
  11.0 2.5 %collective-permute-start = (f32[16,128]{1,0:T(8,128)}, f32[16,128]{1,0:T(8,128)S(1)}, u32[]{:S(2)}, u32[]{:S(2)}) collective-permute-start(f32[16,128]{1,0:T(8,128)} %get-tuple-element.137), channel_id=1, source_target_pairs={{0,1},{1,2},{2,3},{3,4},{4,5},{5,6},{6,7},{7,0},{8,9},{9,10},{10,1... | collective-permute-start | bytes 24584 | tf_op jit(solution)/shard_map/ppermute | solution.py:166
  13.5 4.0 %collective-permute-start.1 = (f32[16,128]{1,0:T(8,128)}, f32[16,128]{1,0:T(8,128)S(1)}, u32[]{:S(2)}, u32[]{:S(2)}) collective-permute-start(f32[16,128]{1,0:T(8,128)} %get-tuple-element.138), channel_id=1, source_target_pairs={{0,7},{1,0},{2,1},{3,2},{4,3},{5,4},{6,5},{7,6},{8,15},{9,8},{10,9... | collective-permute-start | bytes 24584 | tf_op jit(solution)/shard_map/ppermute | solution.py:166
  17.5 0.7 and_reduce_fusion
  18.9 0.7 copy.19
  19.7 0.7 fusion.3
  20.5 2.2 %collective-permute-start.2 = (f32[8,128]{1,0:T(8,128)S(1)}, f32[8,128]{1,0:T(8,128)S(1)}, u32[]{:S(2)}, u32[]{:S(2)}) collective-permute-start(f32[8,128]{1,0:T(8,128)S(1)} %slice_bitcast_fusion.3), channel_id=1, source_target_pairs={{0,8},{8,16},{16,24},{24,32},{32,40},{40,48},{48,56},{56,64},{64,7... | collective-permute-start | bytes 12296 | tf_op jit(solution)/shard_map/ppermute | solution.py:166
  22.7 2.0 %fusion.18 = f32[4,1,128]{2,0,1:T(4,128)S(1)} fusion(f32[16,128]{1,0:T(8,128)S(1)} %broadcast_select_fusion, f32[5,8,128]{2,0,1:T(8,128)S(1)} %fusion.19, s32[]{:T(128)} %bitcast.9, s32[]{:T(128)} %bitcast.10, pred[]{:T(512)} %and_reduce_fusion), kind=kLoop, calls=%fused_computation.48 | loop fusion | flops 512 | bytes 6153 | tf_op jit(solution)/shard_map/select.14
  24.7 1.5 %scatter.21 = f32[5,8,128]{2,0,1:T(8,128)S(1)} dynamic-update-slice(f32[5,8,128]{2,0,1:T(8,128)S(1)} %fusion.19, f32[4,1,128]{2,0,1:T(4,128)S(1)} %fusion.18, s32[]{:T(128)} %bitcast.9, s32[]{:T(128)} %bitcast.10, s32[]{:T(128)} %constant.272.clone.1) | dynamic-update-slice | bytes 4100 | tf_op jit(solution)/shard_map/scatter | solution.py:249
  26.2 1.6 %collective-permute-start.3 = (f32[16,128]{1,0:T(8,128)S(1)}, f32[16,128]{1,0:T(8,128)S(1)}, u32[]{:S(2)}, u32[]{:S(2)}) collective-permute-start(f32[16,128]{1,0:T(8,128)S(1)} %pad_maximum_fusion.6), channel_id=1, source_target_pairs={{0,248},{8,0},{16,8},{24,16},{32,24},{40,32},{48,40},{56,48},{64,5... | collective-permute-start | bytes 24584 | tf_op jit(solution)/shard_map/ppermute | solution.py:166
  27.9 1.5 %collective-permute-done.3 = f32[16,128]{1,0:T(8,128)S(1)} collective-permute-done((f32[16,128]{1,0:T(8,128)S(1)}, f32[16,128]{1,0:T(8,128)S(1)}, u32[]{:S(2)}, u32[]{:S(2)}) %collective-permute-start.3) | collective-permute-done | bytes 8224 | tf_op jit(solution)/shard_map/ppermute | solution.py:166
  30.6 4.8 %shard_map.132 = (f32[40,128]{1,0:T(8,128)}, f32[40,128]{1,0:T(8,128)}, f32[40,128]{1,0:T(8,128)}, f32[16,128]{1,0:T(8,128)}, f32[16,128]{1,0:T(8,128)}) custom-call(s32[68]{0:T(128)} %pad_add_fusion.table, f32[128,128]{1,0:T(8,128)} %scatter.16.mirror, f32[128,128]{1,0:T(8,128)} %scatter.19.gain, f32[16,128,128]{2,1,0:T(8,128)} %bitcast.67, ...), custom_call_target="tpu_custom_call" | custom-call | tf_op jit(solution)/shard_map/pallas_call | solution.py:219
  35.4 2.7 %collective-permute-start.5 = (f32[16,128]{1,0:T(8,128)}, f32[16,128]{1,0:T(8,128)S(1)}, u32[]{:S(2)}, u32[]{:S(2)}) collective-permute-start(f32[16,128]{1,0:T(8,128)} %get-tuple-element.142), channel_id=1, source_target_pairs={{0,7},{1,0},{2,1},{3,2},{4,3},{5,4},{6,5},{7,6},{8,15},{9,8},{10,9... | collective-permute-start | bytes 24584 | tf_op jit(solution)/shard_map/ppermute | solution.py:166
  38.1 1.2 %collective-permute-done.4 = f32[16,128]{1,0:T(8,128)S(1)} collective-permute-done((f32[16,128]{1,0:T(8,128)}, f32[16,128]{1,0:T(8,128)S(1)}, u32[]{:S(2)}, u32[]{:S(2)}) %collective-permute-start.4) | collective-permute-done | bytes 8224 | tf_op jit(solution)/shard_map/ppermute | solution.py:166
  39.4 0.7 fusion.4
  40.1 1.3 %collective-permute-start.6 = (f32[8,128]{1,0:T(8,128)S(1)}, f32[8,128]{1,0:T(8,128)S(1)}, u32[]{:S(2)}, u32[]{:S(2)}) collective-permute-start(f32[8,128]{1,0:T(8,128)S(1)} %slice_bitcast_fusion.1), channel_id=1, source_target_pairs={{0,8},{8,16},{16,24},{24,32},{32,40},{40,48},{48,56},{56,64},{64,7... | collective-permute-start | bytes 12296 | tf_op jit(solution)/shard_map/ppermute | solution.py:166
  41.4 2.8 %collective-permute-done.6 = f32[8,128]{1,0:T(8,128)S(1)} collective-permute-done((f32[8,128]{1,0:T(8,128)S(1)}, f32[8,128]{1,0:T(8,128)S(1)}, u32[]{:S(2)}, u32[]{:S(2)}) %collective-permute-start.6) | collective-permute-done | bytes 4128 | tf_op jit(solution)/shard_map/ppermute | solution.py:166
  44.2 5.7 %collective-permute-start.7 = (f32[8,128]{1,0:T(8,128)S(1)}, f32[8,128]{1,0:T(8,128)S(1)}, u32[]{:S(2)}, u32[]{:S(2)}) collective-permute-start(f32[8,128]{1,0:T(8,128)S(1)} %get-tuple-element.150), channel_id=1, source_target_pairs={{0,248},{8,0},{16,8},{24,16},{32,24},{40,32},{48,40},{56,48},{64,5... | collective-permute-start | bytes 12296 | tf_op jit(solution)/shard_map/ppermute | solution.py:166
  49.9 0.8 collective-permute-done.7
  51.3 4.9 %shard_map.133 = (f32[40,128]{1,0:T(8,128)}, f32[40,128]{1,0:T(8,128)}, f32[16,128]{1,0:T(8,128)}, f32[16,128]{1,0:T(8,128)}, f32[256,128]{1,0:T(8,128)}) custom-call(s32[68]{0:T(128)} %pad_add_fusion.table, f32[128,128]{1,0:T(8,128)} %scatter.16.mirror, f32[128,128]{1,0:T(8,128)} %scatter.19.gain, f32[16,128,128]{2,1,0:T(8,128)} %bitcast.68, ...), custom_call_target="tpu_custom_call" | custom-call | tf_op jit(solution)/shard_map/pallas_call | solution.py:219
  56.2 2.3 %collective-permute-start.8 = (f32[16,128]{1,0:T(8,128)}, f32[16,128]{1,0:T(8,128)S(1)}, u32[]{:S(2)}, u32[]{:S(2)}) collective-permute-start(f32[16,128]{1,0:T(8,128)} %get-tuple-element.147), channel_id=1, source_target_pairs={{0,1},{1,2},{2,3},{3,4},{4,5},{5,6},{6,7},{7,0},{8,9},{9,10},{10,1... | collective-permute-start | bytes 24584 | tf_op jit(solution)/shard_map/ppermute | solution.py:166
  58.5 9.9 %all-to-all-start = ((f32[256,1,128]{2,1,0:T(1,128)}), f32[256,1,128]{2,1,0:T(1,128)S(1)}, u32[]{:S(2)}, u32[]{:S(2)}) async-start(f32[256,1,128]{2,1,0:T(1,128)} %bitcast.74), calls=%async_computation | async-start | bytes 262144 | tf_op jit(solution)/shard_map/all_to_all | solution.py:278
  68.4 4.4 %collective-permute-start.9 = (f32[16,128]{1,0:T(8,128)}, f32[16,128]{1,0:T(8,128)S(1)}, u32[]{:S(2)}, u32[]{:S(2)}) collective-permute-start(f32[16,128]{1,0:T(8,128)} %get-tuple-element.148), channel_id=1, source_target_pairs={{0,7},{1,0},{2,1},{3,2},{4,3},{5,4},{6,5},{7,6},{8,15},{9,8},{10,9... | collective-permute-start | bytes 24584 | tf_op jit(solution)/shard_map/ppermute | solution.py:166
  72.8 1.0 %collective-permute-done.9 = f32[16,128]{1,0:T(8,128)S(1)} collective-permute-done((f32[16,128]{1,0:T(8,128)}, f32[16,128]{1,0:T(8,128)S(1)}, u32[]{:S(2)}, u32[]{:S(2)}) %collective-permute-start.9) | collective-permute-done | bytes 8224 | tf_op jit(solution)/shard_map/ppermute | solution.py:166
  73.8 0.7 fusion.5
  74.5 2.5 %collective-permute-start.10 = (f32[8,128]{1,0:T(8,128)S(1)}, f32[8,128]{1,0:T(8,128)S(1)}, u32[]{:S(2)}, u32[]{:S(2)}) collective-permute-start(f32[8,128]{1,0:T(8,128)S(1)} %slice_bitcast_fusion), channel_id=1, source_target_pairs={{0,8},{8,16},{16,24},{24,32},{32,40},{40,48},{48,56},{56,64},{64,7... | collective-permute-start | bytes 12296 | tf_op jit(solution)/shard_map/ppermute | solution.py:166
  77.0 0.8 collective-permute-done.10
  77.8 3.6 %all-to-all-done = f32[256,1,128]{2,1,0:T(1,128)S(1)} async-done(((f32[256,1,128]{2,1,0:T(1,128)}), f32[256,1,128]{2,1,0:T(1,128)S(1)}, u32[]{:S(2)}, u32[]{:S(2)}) %all-to-all-start) | async-done | bytes 131104 | tf_op jit(solution)/shard_map/all_to_all | solution.py:278
  82.0 1.9 %shard_map.134 = (f32[4,4,128]{2,1,0:T(4,128)}, f32[4,4,128]{2,1,0:T(4,128)}) custom-call(f32[256,128]{1,0:T(8,128)} %bitcast.69, f32[40,128]{1,0:T(8,128)} %bitcast.75, f32[40,128]{1,0:T(8,128)} %get-tuple-element.143.s_ref, f32[40,128]{1,0:T(8,128)} %get-tuple-element.144.jac.jac_ref, f32[40,128]{1,0:T(8,128)} %get-tuple-element.149.w_ref), custom_call_target="tpu_custom_call" | custom-call | tf_op jit(solution)/shard_map/pallas_call | solution.py:219
  (54 shorter events, 6.1 us)
Async XLA Ops:
  0.6 16.9 %copy-start.4 = (s32[3]{0:T(128)S(1)}, s32[3]{0:T(128)}, u32[]{:S(2)}) copy-start(s32[3]{0:T(128)} %constant.282.clone.1) | copy-start | bytes 40
  11.0 8.6 %collective-permute-start = (f32[16,128]{1,0:T(8,128)}, f32[16,128]{1,0:T(8,128)S(1)}, u32[]{:S(2)}, u32[]{:S(2)}) collective-permute-start(f32[16,128]{1,0:T(8,128)} %get-tuple-element.137), channel_id=1, source_target_pairs={{0,1},{1,2},{2,3},{3,4},{4,5},{5,6},{6,7},{7,0},{8,9},{9,10},{10,1... | collective-permute-start | bytes 24584 | tf_op jit(solution)/shard_map/ppermute | solution.py:166
  13.5 6.2 %collective-permute-start.1 = (f32[16,128]{1,0:T(8,128)}, f32[16,128]{1,0:T(8,128)S(1)}, u32[]{:S(2)}, u32[]{:S(2)}) collective-permute-start(f32[16,128]{1,0:T(8,128)} %get-tuple-element.138), channel_id=1, source_target_pairs={{0,7},{1,0},{2,1},{3,2},{4,3},{5,4},{6,5},{7,6},{8,15},{9,8},{10,9... | collective-permute-start | bytes 24584 | tf_op jit(solution)/shard_map/ppermute | solution.py:166
  20.5 5.7 %collective-permute-start.2 = (f32[8,128]{1,0:T(8,128)S(1)}, f32[8,128]{1,0:T(8,128)S(1)}, u32[]{:S(2)}, u32[]{:S(2)}) collective-permute-start(f32[8,128]{1,0:T(8,128)S(1)} %slice_bitcast_fusion.3), channel_id=1, source_target_pairs={{0,8},{8,16},{16,24},{24,32},{32,40},{40,48},{48,56},{56,64},{64,7... | collective-permute-start | bytes 12296 | tf_op jit(solution)/shard_map/ppermute | solution.py:166
  26.2 3.2 %collective-permute-start.3 = (f32[16,128]{1,0:T(8,128)S(1)}, f32[16,128]{1,0:T(8,128)S(1)}, u32[]{:S(2)}, u32[]{:S(2)}) collective-permute-start(f32[16,128]{1,0:T(8,128)S(1)} %pad_maximum_fusion.6), channel_id=1, source_target_pairs={{0,248},{8,0},{16,8},{24,16},{32,24},{40,32},{48,40},{56,48},{64,5... | collective-permute-start | bytes 24584 | tf_op jit(solution)/shard_map/ppermute | solution.py:166
  30.0 0.6 copy-start.1
  35.4 3.9 %collective-permute-start.4 = (f32[16,128]{1,0:T(8,128)}, f32[16,128]{1,0:T(8,128)S(1)}, u32[]{:S(2)}, u32[]{:S(2)}) collective-permute-start(f32[16,128]{1,0:T(8,128)} %get-tuple-element.141), channel_id=1, source_target_pairs={{0,1},{1,2},{2,3},{3,4},{4,5},{5,6},{6,7},{7,0},{8,9},{9,10},{10,1... | collective-permute-start | bytes 24584 | tf_op jit(solution)/shard_map/ppermute | solution.py:166
  35.4 3.9 %collective-permute-start.5 = (f32[16,128]{1,0:T(8,128)}, f32[16,128]{1,0:T(8,128)S(1)}, u32[]{:S(2)}, u32[]{:S(2)}) collective-permute-start(f32[16,128]{1,0:T(8,128)} %get-tuple-element.142), channel_id=1, source_target_pairs={{0,7},{1,0},{2,1},{3,2},{4,3},{5,4},{6,5},{7,6},{8,15},{9,8},{10,9... | collective-permute-start | bytes 24584 | tf_op jit(solution)/shard_map/ppermute | solution.py:166
  40.1 4.1 %collective-permute-start.6 = (f32[8,128]{1,0:T(8,128)S(1)}, f32[8,128]{1,0:T(8,128)S(1)}, u32[]{:S(2)}, u32[]{:S(2)}) collective-permute-start(f32[8,128]{1,0:T(8,128)S(1)} %slice_bitcast_fusion.1), channel_id=1, source_target_pairs={{0,8},{8,16},{16,24},{24,32},{32,40},{40,48},{48,56},{56,64},{64,7... | collective-permute-start | bytes 12296 | tf_op jit(solution)/shard_map/ppermute | solution.py:166
  44.2 6.5 %collective-permute-start.7 = (f32[8,128]{1,0:T(8,128)S(1)}, f32[8,128]{1,0:T(8,128)S(1)}, u32[]{:S(2)}, u32[]{:S(2)}) collective-permute-start(f32[8,128]{1,0:T(8,128)S(1)} %get-tuple-element.150), channel_id=1, source_target_pairs={{0,248},{8,0},{16,8},{24,16},{32,24},{40,32},{48,40},{56,48},{64,5... | collective-permute-start | bytes 12296 | tf_op jit(solution)/shard_map/ppermute | solution.py:166
  50.7 0.6 copy-start.2
  56.2 16.6 %collective-permute-start.8 = (f32[16,128]{1,0:T(8,128)}, f32[16,128]{1,0:T(8,128)S(1)}, u32[]{:S(2)}, u32[]{:S(2)}) collective-permute-start(f32[16,128]{1,0:T(8,128)} %get-tuple-element.147), channel_id=1, source_target_pairs={{0,1},{1,2},{2,3},{3,4},{4,5},{5,6},{6,7},{7,0},{8,9},{9,10},{10,1... | collective-permute-start | bytes 24584 | tf_op jit(solution)/shard_map/ppermute | solution.py:166
  58.5 22.9 %all-to-all-start = ((f32[256,1,128]{2,1,0:T(1,128)}), f32[256,1,128]{2,1,0:T(1,128)S(1)}, u32[]{:S(2)}, u32[]{:S(2)}) async-start(f32[256,1,128]{2,1,0:T(1,128)} %bitcast.74), calls=%async_computation | async-start | bytes 262144 | tf_op jit(solution)/shard_map/all_to_all | solution.py:278
  68.4 5.4 %collective-permute-start.9 = (f32[16,128]{1,0:T(8,128)}, f32[16,128]{1,0:T(8,128)S(1)}, u32[]{:S(2)}, u32[]{:S(2)}) collective-permute-start(f32[16,128]{1,0:T(8,128)} %get-tuple-element.148), channel_id=1, source_target_pairs={{0,7},{1,0},{2,1},{3,2},{4,3},{5,4},{6,5},{7,6},{8,15},{9,8},{10,9... | collective-permute-start | bytes 24584 | tf_op jit(solution)/shard_map/ppermute | solution.py:166
  74.5 3.2 %collective-permute-start.10 = (f32[8,128]{1,0:T(8,128)S(1)}, f32[8,128]{1,0:T(8,128)S(1)}, u32[]{:S(2)}, u32[]{:S(2)}) collective-permute-start(f32[8,128]{1,0:T(8,128)S(1)} %slice_bitcast_fusion), channel_id=1, source_target_pairs={{0,8},{8,16},{16,24},{24,32},{32,40},{40,48},{48,56},{56,64},{64,7... | collective-permute-start | bytes 12296 | tf_op jit(solution)/shard_map/ppermute | solution.py:166
  77.8 3.6 %copy-start.3 = (f32[5,8,128]{2,1,0:T(8,128)}, f32[5,8,128]{2,1,0:T(8,128)S(1)}, u32[]{:S(2)}) copy-start(f32[5,8,128]{2,1,0:T(8,128)S(1)} %fusion.12) | copy-start | bytes 61444
  81.4 0.7 copy-start

commit v2 on v1

v2 whole, which is shorter than its diff:
```python
import functools

import jax
import jax.numpy as jnp
from jax import lax
from jax.experimental import pallas as pl
from jax.experimental.pallas import tpu as pltpu
from jax.sharding import PartitionSpec as P

STRIDE = 8
CODE_STEP = (1, STRIDE - 1, STRIDE, STRIDE + 1)

VMEM = pl.BlockSpec(memory_space=pltpu.VMEM)
SMEM = pl.BlockSpec(memory_space=pltpu.SMEM)
ANY = pl.BlockSpec(memory_space=pl.ANY)
f32 = jnp.float32


def inside_grid(rows, cols, shape):
    slab, cross = lax.axis_index("slab"), lax.axis_index("cross")
    has_south = slab < lax.axis_size("slab") - 1
    at = lax.broadcasted_iota(jnp.int32, shape, 0)
    column = at % STRIDE
    first = jnp.where(cross > 0, 0, 1)
    last = jnp.where(cross < lax.axis_size("cross") - 1, cols + 1, cols)
    end = jnp.where(has_south, rows + 1, rows) * STRIDE
    own = (at < rows * STRIDE) & (column >= 1) & (column <= cols)
    return (column >= first) & (column <= last) & (at < end), own


class Tiles:
    def __init__(self, rows, cols, p_ref, mask, selfs, edges, ghosts):
        self.rows, self.cols, self.p_ref, self.mask = rows, cols, p_ref, mask
        self.selfs, self.edges, self.ghosts = selfs, edges, ghosts
        self.size = p_ref.shape[1]
        full = (self.size, self.size)
        self.lane = lax.broadcasted_iota(jnp.int32, full, 1)
        self.eye = self.lane == lax.broadcasted_iota(jnp.int32, full, 0)
        self.columns = jnp.transpose(p_ref[...])
        self.sums = jnp.zeros(full, f32)
        self.parts = {}

    def fold(self, product, at, factor=None):
        part = jnp.sum(product.reshape(self.size // 8, 8, self.size), axis=0)
        if factor is not None:
            part = part * factor
        self.parts[at] = self.parts[at] + part if at in self.parts else part

    def block(self, r, c):
        size, cols = self.size, self.cols
        at = r * STRIDE + c + 1
        down = jnp.broadcast_to(self.columns[:, at : at + 1], (size, size))
        tile = jnp.where(self.eye, 0.0, self.selfs[r * cols + c])
        acc = tile * self.p_ref[at : at + 1, :]
        self.fold(tile * down, at)
        for code, distance in enumerate(CODE_STEP):
            slot = (r * cols + c) * len(CODE_STEP) + code
            live = self.mask[slot : slot + 1, :]
            j = at + distance
            tile = self.edges[slot]
            acc += tile * (self.p_ref[j : j + 1, :] * live)
            self.fold(tile * down, j, live)
        if r == self.rows - 1:
            tile = self.ghosts[c]
            base = self.rows * cols * len(CODE_STEP) + c * cols
            field = jnp.zeros((1, size), f32)
            for o in range(cols):
                j = r * STRIDE + 1 + o
                field += self.p_ref[j : j + 1, :] * self.mask[base + o : base + o + 1, :]
            acc += tile * field
            part = jnp.sum((tile * down).reshape(size // 8, 8, size), axis=0)
            for o in range(cols):
                j = r * STRIDE + 1 + o
                self.parts[j] += part * self.mask[base + o : base + o + 1, :]
        self.sums = jnp.where(self.lane == at, jnp.sum(acc, axis=1, keepdims=True), self.sums)

    def store(self, v_ref):
        v_ref[...] += jnp.transpose(self.sums)[: v_ref.shape[0], :]
        for at, part in self.parts.items():
            v_ref[at : at + 1, :] += jnp.sum(part, axis=0, keepdims=True)


def pack_sides(v_ref, east_ref, west_ref, rows, cols):
    for r in range(rows + 1):
        east_ref[2 * r : 2 * r + 2, :] = v_ref[r * STRIDE + cols : r * STRIDE + cols + 2, :]
        west_ref[2 * r : 2 * r + 2, :] = v_ref[r * STRIDE : r * STRIDE + 2, :]


def first_kernel(
    rows, cols, count, offset, owner, mirror, gain, vel, acc, grad, dens, weight,
    self_hbm, edge_hbm,
    v_out, src_out, east, west, mask, selfs, edges, ghosts, p_ref, self_sem, edge_sem,
):
    size = p_ref.shape[1]
    slots = len(CODE_STEP)
    for r in range(rows):
        part = pl.ds(r * cols, cols)
        pltpu.make_async_copy(self_hbm.at[part], selfs.at[part], self_sem.at[r]).start()
        for c in range(cols):
            for k in range(slots):
                slot = (r * cols + c) * slots + k
                place = (r * cols + c) * slots + offset[r, c, k]
                pltpu.make_async_copy(
                    edge_hbm.at[slot], edges.at[place], edge_sem.at[r]
                ).start()
                live = jnp.where(k < count[r, c], 1.0, 0.0)
                mask[pl.ds(place, 1), :] = jnp.full((1, size), live, f32)
    base = rows * cols * slots
    for c in range(cols):
        for o in range(cols):
            same = jnp.where(owner[c] == o, 1.0, 0.0)
            mask[base + c * cols + o : base + c * cols + o + 1, :] = jnp.full((1, size), same, f32)

    inside, _ = inside_grid(rows, cols, v_out.shape)
    p_ref[...] = jnp.zeros_like(p_ref)
    p_ref[: v_out.shape[0], :] = jnp.where(inside, 1.0, 0.0)
    v_out[...] = jnp.zeros_like(v_out)
    src_out[...] = jnp.zeros_like(src_out)
    for r in range(rows):
        lo = r * STRIDE + 1
        total = jnp.zeros((cols, size), f32)
        for d in range(3):
            total += grad[d, r] * (vel[d, r] + 0.5 * acc[d, r])
        src = dens[r] / 0.25 - total / 0.5
        src_out[lo : lo + cols, :] = src
        v_out[lo : lo + cols, :] = -weight[r]
        head = 2 * (rows + 1) + r
        east[head : head + 1, :] = src[cols - 1 : cols, :]
        west[head : head + 1, :] = src[0:1, :]
    for side in (east, west):
        for row in range(2 * (rows + 1) + rows, side.shape[0]):
            side[row : row + 1, :] = jnp.zeros((1, size), f32)

    on_wall = lax.axis_index("slab") == lax.axis_size("slab") - 1
    pad = jnp.zeros((size - cols, size), f32)
    mirrors = jnp.transpose(jnp.concatenate([mirror[...].astype(f32), pad], axis=0))
    gains = jnp.transpose(
        jnp.concatenate([gain[...] * jnp.where(on_wall, -1.0, 0.0), pad], axis=0)
    )
    lane = lax.broadcasted_iota(jnp.int32, (size, size), 1)
    sub = lax.broadcasted_iota(jnp.int32, (size, size), 0)
    lanef = lane.astype(f32)
    for c in range(cols):
        hit = lanef == mirrors[:, c : c + 1]
        tile = jnp.where(hit, gains[:, c : c + 1], 0.0)
        other = jnp.where(owner[c] == c, 0.0, 1.0)
        ghosts[c] = jnp.where(lane == sub, tile * other, tile)

    tiles = Tiles(rows, cols, p_ref, mask, selfs, edges, ghosts)
    for r in range(rows):
        part = pl.ds(r * cols, cols)
        pltpu.make_async_copy(self_hbm.at[part], selfs.at[part], self_sem.at[r]).wait()
        part = pl.ds(r * cols * slots, cols * slots)
        pltpu.make_async_copy(edge_hbm.at[part], edges.at[part], edge_sem.at[r]).wait()
        for c in range(cols):
            tiles.block(r, c)
    tiles.store(v_out)
    pack_sides(v_out, east, west, rows, cols)


def add_rims(rows, total, from_north, from_south, out):
    has_north = lax.axis_index("slab") > 0
    out[...] = total[...]
    out[:STRIDE, :] += jnp.where(has_north, from_north[...], 0.0)
    if from_south is not None:
        out[rows * STRIDE :, :] += from_south[:STRIDE, :]


def second_kernel(
    rows, cols, mask, selfs, edges, ghosts, total, src, from_north, from_south,
    v_out, s_out, jac_out, east, west, p_ref,
):
    inside, _ = inside_grid(rows, cols, v_out.shape)
    add_rims(rows, total, from_north, from_south, jac_out)
    s_out[...] = src[...]
    s_out[rows * STRIDE :, :] = from_south[STRIDE:, :]
    jac = jnp.where(inside, -jac_out[...], 1.0)
    s = jnp.where(inside, s_out[...] / jac, 0.0)
    p_ref[...] = jnp.zeros_like(p_ref)
    p_ref[: s.shape[0], :] = s
    s_out[...] = s
    jac_out[...] = jac
    v_out[...] = jnp.zeros_like(v_out)
    tiles = Tiles(rows, cols, p_ref, mask, selfs, edges, ghosts)
    for r in range(rows):
        for c in range(cols):
            tiles.block(r, c)
    tiles.store(v_out)
    for side in (east, west):
        side[...] = jnp.zeros_like(side)
    pack_sides(v_out, east, west, rows, cols)


def third_kernel(
    rows, cols, mask, selfs, edges, ghosts, total, src, s_ref, jac, from_north, from_south,
    v_out, w_out, east, west, sums_out, p_ref,
):
    size = p_ref.shape[1]
    inside, own = inside_grid(rows, cols, v_out.shape)
    add_rims(rows, total, from_north, from_south, w_out)
    u = w_out[...]
    w = jnp.where(inside, u / jac[...], 0.0)
    p_ref[...] = jnp.zeros_like(p_ref)
    p_ref[: w.shape[0], :] = w
    w_out[...] = w
    v_out[...] = jnp.zeros_like(v_out)
    tiles = Tiles(rows, cols, p_ref, mask, selfs, edges, ghosts)
    for r in range(rows):
        for c in range(cols):
            tiles.block(r, c)
    tiles.store(v_out)
    for side in (east, west):
        side[...] = jnp.zeros_like(side)
    pack_sides(v_out, east, west, rows, cols)
    s = s_ref[...]

    def whole(x):
        return jnp.sum(jnp.sum(x, axis=0, keepdims=True), axis=1, keepdims=True)

    sums = (
        whole(jnp.where(own, src[...] * s, 0.0)),
        whole(jnp.where(own, s * u, 0.0)),
        whole(jnp.where(own, w * u, 0.0)),
        whole(w * v_out[...]),
    )
    lane = lax.broadcasted_iota(jnp.int32, (1, size), 1)
    line = jnp.zeros((1, size), f32)
    for k, value in enumerate(sums):
        line = jnp.where(lane == k, value, line)
    sums_out[...] = jnp.broadcast_to(line, sums_out.shape)


def merge_kernel(rows, cols, with_src, with_north, *refs):
    refs = list(refs)
    v, from_west, from_east = refs[:3]
    total, south = refs[3 + with_src : 5 + with_src]
    has_west = lax.axis_index("cross") > 0
    has_east = lax.axis_index("cross") < lax.axis_size("cross") - 1
    total[...] = v[...]
    for r in range(rows + 1):
        lo = r * STRIDE
        total[lo : lo + 2, :] += jnp.where(has_west, from_west[2 * r : 2 * r + 2, :], 0.0)
        lo += cols
        total[lo : lo + 2, :] += jnp.where(has_east, from_east[2 * r : 2 * r + 2, :], 0.0)
    south[...] = total[rows * STRIDE :, :]
    if with_north:
        north = refs[5 + with_src]
        north[:STRIDE, :] = total[:STRIDE, :]
    if with_src:
        src, src_out = refs[3], refs[7]
        src_out[...] = src[...]
        for r in range(rows):
            lo, head = r * STRIDE, 2 * (rows + 1) + r
            src_out[lo : lo + 1, :] = from_west[head : head + 1, :]
            src_out[lo + cols + 1 : lo + cols + 2, :] = from_east[head : head + 1, :]
        north[STRIDE:, :] = src_out[:STRIDE, :]


def last_kernel(rows, cols, gathered, total, from_north, s_ref, jac_ref, w_ref, pressure, residual, v):
    add_rims(rows, total, from_north, None, v)
    nu = jnp.sum(gathered[...], axis=0, keepdims=True)
    nu0, nu1, nu2, nu3 = (nu[:, k : k + 1] for k in range(4))
    rho = nu1 / nu0
    a0 = 1.0 / (1.0 + rho)
    norm1 = a0 * a0 * (nu2 - rho * nu1)
    beta = norm1 / nu0
    g = a0 * rho + beta
    cross = g * g * nu1 - 2.0 * g * a0 * nu2 + a0 * a0 * nu3
    sigma = jnp.where(norm1 > 0.0, beta + cross / norm1, 0.0)
    step = 1.0 / (1.0 + sigma)
    rest = sigma * step
    ps, pw = a0 + step * g, -step * a0
    rs, rw, rv = a0 * rho * rest - step * beta, -a0 * rest - step * g, step * a0
    for r in range(rows):
        lo = r * STRIDE + 1
        s, w, jac = s_ref[lo : lo + cols, :], w_ref[lo : lo + cols, :], jac_ref[lo : lo + cols, :]
        pressure[r] = ps * s + pw * w
        residual[r] = jac * (rs * s + rw * w) + rv * v[lo : lo + cols, :]


def shift(value, axis, step):
    count = lax.axis_size(axis)
    return lax.ppermute(value, axis, [(i, (i + step) % count) for i in range(count)])


def per_device(
    velocity,
    acceleration,
    grad_coef,
    density_dev,
    self_weight,
    self_tiles,
    edge_tiles,
    tile_count,
    tile_offset,
    ghost_owner,
    ghost_mirror,
    ghost_gain,
):
    rows, cols, size = self_weight.shape
    slots = tile_offset.shape[-1]
    region = ((rows + 1) * STRIDE, size)
    side = (STRIDE * pl.cdiv(2 * (rows + 1) + rows, STRIDE), size)
    line = (STRIDE, size)
    peers = lax.axis_size("slab") * lax.axis_size("cross")

    def call(kernel, shapes, specs, operands, scratch=(), extra=(), limit=2):
        return pl.pallas_call(
            functools.partial(kernel, rows, cols, *extra),
            out_shape=[pltpu.VMEM(shape, f32) for shape in shapes],
            in_specs=specs,
            out_specs=[VMEM] * len(shapes),
            scratch_shapes=list(scratch),
            compiler_params=pltpu.CompilerParams(vmem_limit_bytes=limit << 20),
        )(*operands)

    def merge(v, east, west, src=None, north=True):
        operands = [v, shift(east, "cross", 1), shift(west, "cross", -1)]
        shapes = [region, line]
        if src is not None:
            operands.append(src)
            shapes += [(2 * STRIDE, size), region]
        elif north:
            shapes.append(line)
        return call(
            merge_kernel, shapes, [VMEM] * len(operands), operands,
            extra=(src is not None, north),
        )

    field = pltpu.VMEM((size, size), f32)
    v, src, east, west, mask, selfs, edges, ghosts = call(
        first_kernel,
        [
            region, region, side, side, (rows * cols * slots + cols * cols, size),
            (rows * cols, size, size), (rows * cols * slots, size, size), (cols, size, size),
        ],
        [SMEM] * 3 + [VMEM] * 7 + [ANY] * 2,
        [
            tile_count, tile_offset, ghost_owner, ghost_mirror, ghost_gain,
            velocity, acceleration, grad_coef, density_dev, self_weight,
            self_tiles.reshape(rows * cols, size, size),
            edge_tiles.reshape(rows * cols * slots, size, size),
        ],
        [field, pltpu.SemaphoreType.DMA((rows,)), pltpu.SemaphoreType.DMA((rows,))],
        limit=10,
    )
    matrix = [mask, selfs, edges, ghosts]
    total, south, north, src = merge(v, east, west, src)
    from_north, from_south = shift(south, "slab", 1), shift(north, "slab", -1)

    operands = matrix + [total, src, from_north, from_south]
    v, s, jac, east, west = call(
        second_kernel, [region] * 3 + [side] * 2, [VMEM] * len(operands), operands, [field]
    )
    total, south, north = merge(v, east, west)
    from_north, from_south = shift(south, "slab", 1), shift(north, "slab", -1)

    operands = matrix + [total, src, s, jac, from_north, from_south]
    v, w, east, west, sums = call(
        third_kernel,
        [region] * 2 + [side] * 2 + [(peers, size)],
        [VMEM] * len(operands), operands, [field],
    )
    gathered = lax.all_to_all(sums, ("slab", "cross"), 0, 0, tiled=True)
    total, south = merge(v, east, west, north=False)
    from_north = shift(south, "slab", 1)

    return tuple(
        pl.pallas_call(
            functools.partial(last_kernel, rows, cols),
            out_shape=[jax.ShapeDtypeStruct((rows, cols, size), f32)] * 2,
            in_specs=[VMEM] * 6,
            out_specs=[VMEM] * 2,
            scratch_shapes=[pltpu.VMEM(region, f32)],
            compiler_params=pltpu.CompilerParams(vmem_limit_bytes=2 << 20),
        )(gathered, total, from_north, s, jac, w)
    )


def solution(mesh):
    in_specs = (
        P(None, "slab", "cross", None),
        P(None, "slab", "cross", None),
        P(None, "slab", "cross", None),
        P("slab", "cross", None),
        P("slab", "cross", None),
        P("slab", "cross", None, None),
        P("slab", "cross", None, None, None),
        P("slab", "cross"),
        P("slab", "cross", None),
        P("cross"),
        P("cross", None),
        P("cross", None),
    )
    out_specs = (P("slab", "cross", None), P("slab", "cross", None))
    return jax.shard_map(
        per_device, mesh=mesh, in_specs=in_specs, out_specs=out_specs, check_vma=False
    )
```

time: 84.5 us -> 79.3 us (0.938)
  other arithmetic: 9.17 us -> 0 us
  Pallas kernels: 16.5 us -> 12.7 us
  local copies, waits for them, and re-layouts: 6.78 us -> 10.4 us
  starting transfers between devices: 39 us -> 42.3 us
  waiting for transfers between devices: 11.7 us -> 12.7 us
    unnamed x10 -> x24, local copies, waits for them, and re-layouts: 1.85 us -> 10.4 us
    all_to_all x1, starting transfers between devices: 9.86 us -> 16.7 us  [per_device(): gathered = lax.all_to_all(sums, ('slab', 'cross'), 0, 0, tiled=True)]
    pallas_call x4 -> x7, Pallas kernels: 16.5 us -> 12.7 us  [the longest x6 11.7 us: call(): pl.pallas_call(functools.partial(kernel, rows, cols, *extra), out_shape=[...]
    ppermute x11, starting transfers between devices: 29.1 us -> 25.6 us  [shift(): lax.ppermute(value, axis, [(i, (i + step) % count) for i in range(count)])]
    scatter x6 -> x0, local copies, waits for them, and re-layouts: 3.37 us -> none  [the longest x2 1.48 us: per_device(): src3 = src3.at[:rows, 0].set(src_west).at[:rows, cols + 1].set(src_east)]
    another operation x3 -> x0, other arithmetic: 2.73 us -> none
    add x4 -> x0, other arithmetic: 2.31 us -> none  [the longest x3 2.24 us: merge_sides(): v.reshape(rows + 1, STRIDE, size) + jnp.concatenate(parts, axis=1)]
    select_n x8 -> x0, other arithmetic: 1.49 us -> none  [the longest x1 0.77 us: per_device(): target = jnp.where(live, here[..., None] + step, DUMMY)]
  transfers between devices with their start and end apart: 12 -> 12, of which waited for: 7 -> 8; matrix products, arithmetic and copies ran while one was open for 8% -> 0% of each run, Pallas kernels for 0% -> 0%
where the time goes in v2:
time: 79.3 us; the launch traced here: 78.7 us
  starting transfers between devices  42.3 us (53%)
  Pallas kernels  12.7 us (16%)
  waiting for transfers between devices  12.7 us (16%)
  local copies, waits for them, and re-layouts  10.4 us (13%)
    ppermute x11, starting transfers between devices, shift(): lax.ppermute(value, axis, [(i, (i + step) % count) for i in range(count)])  25.6 us
    all_to_all x1, starting transfers between devices, per_device(): gathered = lax.all_to_all(sums, ('slab', 'cross'), 0, 0, tiled=True)  16.7 us
    pallas_call x6, Pallas kernels, call(): pl.pallas_call(functools.partial(kernel, rows, cols, *extra), out_shape=[...  11.7 us
    unnamed x24, local copies, waits for them, and re-layouts  10.4 us
    ppermute x11, waiting for transfers between devices, shift(): lax.ppermute(value, axis, [(i, (i + step) % count) for i in range(count)])  8.85 us
    all_to_all x1, waiting for transfers between devices, per_device(): gathered = lax.all_to_all(sums, ('slab', 'cross'), 0, 0, tiled=True)  3.81 us
  transfers between devices with their start and end apart: 12, of which 8 were waited for; matrix products, arithmetic and copies ran while one was open for 0% of the time, Pallas kernels for 0%

profile of v2, /device:TPU:1, one launch (start us, length us, event | category | flops | bytes accessed | tf_op | source)
XLA Modules:
  0.0 78.7 jit_solution(16402862414658365648)
XLA Ops:
  0.6 2.2 %copy-done = f32[4,4,4,128,128]{4,3,2,1,0:T(8,128)S(1)} copy-done((f32[4,4,4,128,128]{4,3,2,1,0:T(8,128)S(1)}, f32[4,4,4,128,128]{4,3,2,1,0:T(8,128)}, u32[]{:S(2)}) %copy-start) | copy-done | bytes 4194328
  2.8 1.2 %copy-done.1 = f32[4,4,128,128]{3,2,1,0:T(8,128)S(1)} copy-done((f32[4,4,128,128]{3,2,1,0:T(8,128)S(1)}, f32[4,4,128,128]{3,2,1,0:T(8,128)}, u32[]{:S(2)}) %copy-start.1) | copy-done | bytes 1048600
  4.1 0.7 copy-done.2
  4.8 0.7 copy-done.3
  5.5 0.7 copy-done.4
  6.3 0.7 copy-done.5
  7.0 0.7 copy-done.6
  7.7 0.7 copy-done.7
  8.4 0.7 copy-done.8
  9.0 0.7 copy-done.9
  9.7 0.7 copy-done.10
  11.1 8.3 %shard_map.131 = (f32[40,128]{1,0:T(8,128)S(1)}, f32[40,128]{1,0:T(8,128)S(1)}, f32[16,128]{1,0:T(8,128)S(1)}, f32[16,128]{1,0:T(8,128)S(1)}, f32[80,128]{1,0:T(...) custom-call(s32[4,4]{1,0:T(4,128)S(1)} %copy-done.8, ...), custom_call_target="tpu_custom_call" | custom-call | tf_op jit(solution)/shard_map/pallas_call | solution.py:308
  19.4 2.5 %collective-permute-start = (f32[16,128]{1,0:T(8,128)S(1)}, f32[16,128]{1,0:T(8,128)S(1)}, u32[]{:S(2)}, u32[]{:S(2)}) collective-permute-start(f32[16,128]{1,0:T(8,128)S(1)} %get-tuple-element.34), channel_id=1, source_target_pairs={{0,1},{1,2},{2,3},{3,4},{4,5},{5,6},{6,7},{7,0},{8,9},{9,10},{10,1... | collective-permute-start | bytes 24584 | tf_op jit(solution)/shard_map/ppermute | solution.py:283
  21.9 4.0 %collective-permute-start.1 = (f32[16,128]{1,0:T(8,128)S(1)}, f32[16,128]{1,0:T(8,128)S(1)}, u32[]{:S(2)}, u32[]{:S(2)}) collective-permute-start(f32[16,128]{1,0:T(8,128)S(1)} %get-tuple-element.35), channel_id=1, source_target_pairs={{0,7},{1,0},{2,1},{3,2},{4,3},{5,4},{6,5},{7,6},{8,15},{9,8},{10,9... | collective-permute-start | bytes 24584 | tf_op jit(solution)/shard_map/ppermute | solution.py:283
  25.9 1.0 %collective-permute-done.refs_1_ = f32[16,128]{1,0:T(8,128)S(1)} collective-permute-done((f32[16,128]{1,0:T(8,128)S(1)}, f32[16,128]{1,0:T(8,128)S(1)}, u32[]{:S(2)}, u32[]{:S(2)}) %collective-permute-start) | collective-permute-done | bytes 8224 | tf_op jit(solution)/shard_map/ppermute | solution.py:283
  26.9 1.6 %collective-permute-start.3 = (f32[16,128]{1,0:T(8,128)S(1)}, f32[16,128]{1,0:T(8,128)S(1)}, u32[]{:S(2)}, u32[]{:S(2)}) collective-permute-start(f32[16,128]{1,0:T(8,128)S(1)} %get-tuple-element.40), channel_id=1, source_target_pairs={{0,248},{8,0},{16,8},{24,16},{32,24},{40,32},{48,40},{56,48},{64,5... | collective-permute-start | bytes 24584 | tf_op jit(solution)/shard_map/ppermute | solution.py:283
  28.5 1.3 %collective-permute-start.2 = (f32[8,128]{1,0:T(8,128)S(1)}, f32[8,128]{1,0:T(8,128)S(1)}, u32[]{:S(2)}, u32[]{:S(2)}) collective-permute-start(f32[8,128]{1,0:T(8,128)S(1)} %get-tuple-element.39), channel_id=1, source_target_pairs={{0,8},{8,16},{16,24},{24,32},{32,40},{40,48},{48,56},{56,64},{64,7... | collective-permute-start | bytes 12296 | tf_op jit(solution)/shard_map/ppermute | solution.py:283
  29.8 3.2 %collective-permute-done.2.from_north = f32[8,128]{1,0:T(8,128)S(1)} collective-permute-done((f32[8,128]{1,0:T(8,128)S(1)}, f32[8,128]{1,0:T(8,128)S(1)}, u32[]{:S(2)}, u32[]{:S(2)}) %collective-permute-start.2) | collective-permute-done | bytes 4128 | tf_op jit(solution)/shard_map/ppermute | solution.py:283
  33.0 1.3 %shard_map.133 = (f32[40,128]{1,0:T(8,128)S(1)}, f32[40,128]{1,0:T(8,128)S(1)}, f32[40,128]{1,0:T(8,128)S(1)}, f32[16,128]{1,0:T(8,128)S(1)}, f32[16,128]{1,0:T(8,128)S(1)}) custom-call(f32[80,128]{1,0:T(8,128)S(1)} %get-tuple-element.29.mask, f32[16,128,128]{2,1,0:T(8,128)S(1)} %get-tuple-element.30.selfs, f32[64,128,128]{2,1,0:T(8,128)S(1)} %get-tuple-element.31.edges, ...), custom_call_target="tpu_custom_call" | custom-call | tf_op jit(solution)/shard_map/pallas_call | solution.py:308
  34.4 2.8 %collective-permute-start.5 = (f32[16,128]{1,0:T(8,128)S(1)}, f32[16,128]{1,0:T(8,128)S(1)}, u32[]{:S(2)}, u32[]{:S(2)}) collective-permute-start(f32[16,128]{1,0:T(8,128)S(1)} %get-tuple-element.43), channel_id=1, source_target_pairs={{0,7},{1,0},{2,1},{3,2},{4,3},{5,4},{6,5},{7,6},{8,15},{9,8},{10,9... | collective-permute-start | bytes 24584 | tf_op jit(solution)/shard_map/ppermute | solution.py:283
  37.2 1.1 %collective-permute-done.4.refs_1_ = f32[16,128]{1,0:T(8,128)S(1)} collective-permute-done((f32[16,128]{1,0:T(8,128)S(1)}, f32[16,128]{1,0:T(8,128)S(1)}, u32[]{:S(2)}, u32[]{:S(2)}) %collective-permute-start.4) | collective-permute-done | bytes 8224 | tf_op jit(solution)/shard_map/ppermute | solution.py:283
  38.3 1.0 %collective-permute-start.6 = (f32[8,128]{1,0:T(8,128)S(1)}, f32[8,128]{1,0:T(8,128)S(1)}, u32[]{:S(2)}, u32[]{:S(2)}) collective-permute-start(f32[8,128]{1,0:T(8,128)S(1)} %get-tuple-element.47), channel_id=1, source_target_pairs={{0,8},{8,16},{16,24},{24,32},{32,40},{40,48},{48,56},{56,64},{64,7... | collective-permute-start | bytes 12296 | tf_op jit(solution)/shard_map/ppermute | solution.py:283
  39.3 5.8 %collective-permute-start.7 = (f32[8,128]{1,0:T(8,128)S(1)}, f32[8,128]{1,0:T(8,128)S(1)}, u32[]{:S(2)}, u32[]{:S(2)}) collective-permute-start(f32[8,128]{1,0:T(8,128)S(1)} %get-tuple-element.48), channel_id=1, source_target_pairs={{0,248},{8,0},{16,8},{24,16},{32,24},{40,32},{48,40},{56,48},{64,5... | collective-permute-start | bytes 12296 | tf_op jit(solution)/shard_map/ppermute | solution.py:283
  45.9 2.1 %shard_map.135 = (f32[40,128]{1,0:T(8,128)S(1)}, f32[40,128]{1,0:T(8,128)S(1)}, f32[16,128]{1,0:T(8,128)S(1)}, f32[16,128]{1,0:T(8,128)S(1)}, f32[256,128]{1,0:T(8,128)}) custom-call(f32[80,128]{1,0:T(8,128)S(1)} %get-tuple-element.29.mask, f32[16,128,128]{2,1,0:T(8,128)S(1)} %get-tuple-element.30.selfs, f32[64,128,128]{2,1,0:T(8,128)S(1)} %get-tuple-element.31.edges, ...), custom_call_target="tpu_custom_call" | custom-call | tf_op jit(solution)/shard_map/pallas_call | solution.py:308
  48.0 16.7 %all-to-all-start = ((f32[256,1,128]{2,1,0:T(1,128)}), f32[256,1,128]{2,1,0:T(1,128)S(1)}, u32[]{:S(2)}, u32[]{:S(2)}) async-start(f32[256,1,128]{2,1,0:T(1,128)} %bitcast.3), calls=%async_computation | async-start | bytes 262144 | tf_op jit(solution)/shard_map/all_to_all | solution.py:364
  64.7 1.6 %collective-permute-start.8 = (f32[16,128]{1,0:T(8,128)S(1)}, f32[16,128]{1,0:T(8,128)S(1)}, u32[]{:S(2)}, u32[]{:S(2)}) collective-permute-start(f32[16,128]{1,0:T(8,128)S(1)} %get-tuple-element.51), channel_id=1, source_target_pairs={{0,1},{1,2},{2,3},{3,4},{4,5},{5,6},{6,7},{7,0},{8,9},{9,10},{10,1... | collective-permute-start | bytes 24584 | tf_op jit(solution)/shard_map/ppermute | solution.py:283
  66.2 2.9 %collective-permute-start.9 = (f32[16,128]{1,0:T(8,128)S(1)}, f32[16,128]{1,0:T(8,128)S(1)}, u32[]{:S(2)}, u32[]{:S(2)}) collective-permute-start(f32[16,128]{1,0:T(8,128)S(1)} %get-tuple-element.52), channel_id=1, source_target_pairs={{0,7},{1,0},{2,1},{3,2},{4,3},{5,4},{6,5},{7,6},{8,15},{9,8},{10,9... | collective-permute-start | bytes 24584 | tf_op jit(solution)/shard_map/ppermute | solution.py:283
  69.1 2.1 %collective-permute-done.8.refs_1_ = f32[16,128]{1,0:T(8,128)S(1)} collective-permute-done((f32[16,128]{1,0:T(8,128)S(1)}, f32[16,128]{1,0:T(8,128)S(1)}, u32[]{:S(2)}, u32[]{:S(2)}) %collective-permute-start.8) | collective-permute-done | bytes 8224 | tf_op jit(solution)/shard_map/ppermute | solution.py:283
  71.2 2.0 %collective-permute-start.10 = (f32[8,128]{1,0:T(8,128)S(1)}, f32[8,128]{1,0:T(8,128)S(1)}, u32[]{:S(2)}, u32[]{:S(2)}) collective-permute-start(f32[8,128]{1,0:T(8,128)S(1)} %get-tuple-element.54), channel_id=1, source_target_pairs={{0,8},{8,16},{16,24},{24,32},{32,40},{40,48},{48,56},{56,64},{64,7... | collective-permute-start | bytes 12296 | tf_op jit(solution)/shard_map/ppermute | solution.py:283
  73.2 0.8 collective-permute-done.10.from_north
  74.0 3.8 %all-to-all-done = f32[256,1,128]{2,1,0:T(1,128)S(1)} async-done(((f32[256,1,128]{2,1,0:T(1,128)}), f32[256,1,128]{2,1,0:T(1,128)S(1)}, u32[]{:S(2)}, u32[]{:S(2)}) %all-to-all-start) | async-done | bytes 131104 | tf_op jit(solution)/shard_map/all_to_all | solution.py:364
  77.8 1.0 %shard_map.137 = (f32[4,4,128]{2,1,0:T(4,128)}, f32[4,4,128]{2,1,0:T(4,128)}) custom-call(f32[256,128]{1,0:T(8,128)S(1)} %bitcast.8, f32[40,128]{1,0:T(8,128)S(1)} %get-tuple-element.53.total, f32[8,128]{1,0:T(8,128)S(1)} %collective-permute-done.10.from_north, f32[40,128]{1,0:T(8,128)S(1)} %get-tuple-element.45.s_ref, ...), custom_call_target="tpu_custom_call" | custom-call | tf_op jit(solution)/shard_map/pallas_call | solution.py:369
  (23 shorter events, 1.7 us)
Async XLA Ops:
  0.6 2.2 %copy-start = (f32[4,4,4,128,128]{4,3,2,1,0:T(8,128)S(1)}, f32[4,4,4,128,128]{4,3,2,1,0:T(8,128)}, u32[]{:S(2)}) copy-start(f32[4,4,4,128,128]{4,3,2,1,0:T(8,128)} %param.18) | copy-start | bytes 12582916
  2.8 1.2 %copy-start.1 = (f32[4,4,128,128]{3,2,1,0:T(8,128)S(1)}, f32[4,4,128,128]{3,2,1,0:T(8,128)}, u32[]{:S(2)}) copy-start(f32[4,4,128,128]{3,2,1,0:T(8,128)} %param.17) | copy-start | bytes 3145732
  4.0 0.7 copy-start.2
  4.8 0.7 copy-start.3
  5.5 0.7 copy-start.4
  6.3 0.7 copy-start.5
  7.0 0.7 copy-start.6
  7.7 0.7 copy-start.7
  8.4 0.7 copy-start.8
  9.0 0.7 copy-start.9
  9.7 0.7 copy-start.10
  10.4 0.7 copy-start.11
  19.4 7.5 %collective-permute-start = (f32[16,128]{1,0:T(8,128)S(1)}, f32[16,128]{1,0:T(8,128)S(1)}, u32[]{:S(2)}, u32[]{:S(2)}) collective-permute-start(f32[16,128]{1,0:T(8,128)S(1)} %get-tuple-element.34), channel_id=1, source_target_pairs={{0,1},{1,2},{2,3},{3,4},{4,5},{5,6},{6,7},{7,0},{8,9},{9,10},{10,1... | collective-permute-start | bytes 24584 | tf_op jit(solution)/shard_map/ppermute | solution.py:283
  21.9 5.0 %collective-permute-start.1 = (f32[16,128]{1,0:T(8,128)S(1)}, f32[16,128]{1,0:T(8,128)S(1)}, u32[]{:S(2)}, u32[]{:S(2)}) collective-permute-start(f32[16,128]{1,0:T(8,128)S(1)} %get-tuple-element.35), channel_id=1, source_target_pairs={{0,7},{1,0},{2,1},{3,2},{4,3},{5,4},{6,5},{7,6},{8,15},{9,8},{10,9... | collective-permute-start | bytes 24584 | tf_op jit(solution)/shard_map/ppermute | solution.py:283
  26.9 6.1 %collective-permute-start.3 = (f32[16,128]{1,0:T(8,128)S(1)}, f32[16,128]{1,0:T(8,128)S(1)}, u32[]{:S(2)}, u32[]{:S(2)}) collective-permute-start(f32[16,128]{1,0:T(8,128)S(1)} %get-tuple-element.40), channel_id=1, source_target_pairs={{0,248},{8,0},{16,8},{24,16},{32,24},{40,32},{48,40},{56,48},{64,5... | collective-permute-start | bytes 24584 | tf_op jit(solution)/shard_map/ppermute | solution.py:283
  28.5 4.4 %collective-permute-start.2 = (f32[8,128]{1,0:T(8,128)S(1)}, f32[8,128]{1,0:T(8,128)S(1)}, u32[]{:S(2)}, u32[]{:S(2)}) collective-permute-start(f32[8,128]{1,0:T(8,128)S(1)} %get-tuple-element.39), channel_id=1, source_target_pairs={{0,8},{8,16},{16,24},{24,32},{32,40},{40,48},{48,56},{56,64},{64,7... | collective-permute-start | bytes 12296 | tf_op jit(solution)/shard_map/ppermute | solution.py:283
  34.3 4.0 %collective-permute-start.4 = (f32[16,128]{1,0:T(8,128)S(1)}, f32[16,128]{1,0:T(8,128)S(1)}, u32[]{:S(2)}, u32[]{:S(2)}) collective-permute-start(f32[16,128]{1,0:T(8,128)S(1)} %get-tuple-element.42), channel_id=1, source_target_pairs={{0,1},{1,2},{2,3},{3,4},{4,5},{5,6},{6,7},{7,0},{8,9},{9,10},{10,1... | collective-permute-start | bytes 24584 | tf_op jit(solution)/shard_map/ppermute | solution.py:283
  34.4 3.9 %collective-permute-start.5 = (f32[16,128]{1,0:T(8,128)S(1)}, f32[16,128]{1,0:T(8,128)S(1)}, u32[]{:S(2)}, u32[]{:S(2)}) collective-permute-start(f32[16,128]{1,0:T(8,128)S(1)} %get-tuple-element.43), channel_id=1, source_target_pairs={{0,7},{1,0},{2,1},{3,2},{4,3},{5,4},{6,5},{7,6},{8,15},{9,8},{10,9... | collective-permute-start | bytes 24584 | tf_op jit(solution)/shard_map/ppermute | solution.py:283
  38.3 7.4 %collective-permute-start.6 = (f32[8,128]{1,0:T(8,128)S(1)}, f32[8,128]{1,0:T(8,128)S(1)}, u32[]{:S(2)}, u32[]{:S(2)}) collective-permute-start(f32[8,128]{1,0:T(8,128)S(1)} %get-tuple-element.47), channel_id=1, source_target_pairs={{0,8},{8,16},{16,24},{24,32},{32,40},{40,48},{48,56},{56,64},{64,7... | collective-permute-start | bytes 12296 | tf_op jit(solution)/shard_map/ppermute | solution.py:283
  39.3 6.7 %collective-permute-start.7 = (f32[8,128]{1,0:T(8,128)S(1)}, f32[8,128]{1,0:T(8,128)S(1)}, u32[]{:S(2)}, u32[]{:S(2)}) collective-permute-start(f32[8,128]{1,0:T(8,128)S(1)} %get-tuple-element.48), channel_id=1, source_target_pairs={{0,248},{8,0},{16,8},{24,16},{32,24},{40,32},{48,40},{56,48},{64,5... | collective-permute-start | bytes 12296 | tf_op jit(solution)/shard_map/ppermute | solution.py:283
  48.0 29.8 %all-to-all-start = ((f32[256,1,128]{2,1,0:T(1,128)}), f32[256,1,128]{2,1,0:T(1,128)S(1)}, u32[]{:S(2)}, u32[]{:S(2)}) async-start(f32[256,1,128]{2,1,0:T(1,128)} %bitcast.3), calls=%async_computation | async-start | bytes 262144 | tf_op jit(solution)/shard_map/all_to_all | solution.py:364
  64.7 6.6 %collective-permute-start.8 = (f32[16,128]{1,0:T(8,128)S(1)}, f32[16,128]{1,0:T(8,128)S(1)}, u32[]{:S(2)}, u32[]{:S(2)}) collective-permute-start(f32[16,128]{1,0:T(8,128)S(1)} %get-tuple-element.51), channel_id=1, source_target_pairs={{0,1},{1,2},{2,3},{3,4},{4,5},{5,6},{6,7},{7,0},{8,9},{9,10},{10,1... | collective-permute-start | bytes 24584 | tf_op jit(solution)/shard_map/ppermute | solution.py:283
  66.2 5.0 %collective-permute-start.9 = (f32[16,128]{1,0:T(8,128)S(1)}, f32[16,128]{1,0:T(8,128)S(1)}, u32[]{:S(2)}, u32[]{:S(2)}) collective-permute-start(f32[16,128]{1,0:T(8,128)S(1)} %get-tuple-element.52), channel_id=1, source_target_pairs={{0,7},{1,0},{2,1},{3,2},{4,3},{5,4},{6,5},{7,6},{8,15},{9,8},{10,9... | collective-permute-start | bytes 24584 | tf_op jit(solution)/shard_map/ppermute | solution.py:283
  71.2 2.7 %collective-permute-start.10 = (f32[8,128]{1,0:T(8,128)S(1)}, f32[8,128]{1,0:T(8,128)S(1)}, u32[]{:S(2)}, u32[]{:S(2)}) collective-permute-start(f32[8,128]{1,0:T(8,128)S(1)} %get-tuple-element.54), channel_id=1, source_target_pairs={{0,8},{8,16},{16,24},{24,32},{32,40},{40,48},{48,56},{56,64},{64,7... | collective-permute-start | bytes 12296 | tf_op jit(solution)/shard_map/ppermute | solution.py:283

commit v3 on v2

--- a/solution.py
+++ b/solution.py
@@ -11,8 +11,7 @@
 CODE_STEP = (1, STRIDE - 1, STRIDE, STRIDE + 1)
 
 VMEM = pl.BlockSpec(memory_space=pltpu.VMEM)
-SMEM = pl.BlockSpec(memory_space=pltpu.SMEM)
-ANY = pl.BlockSpec(memory_space=pl.ANY)
+HBM = pl.BlockSpec(memory_space=pltpu.HBM)
 f32 = jnp.float32
 
 
@@ -80,22 +79,39 @@
             v_ref[at : at + 1, :] += jnp.sum(part, axis=0, keepdims=True)
 
 
-def pack_sides(v_ref, east_ref, west_ref, rows, cols):
+def on_even(axis):
+    return lax.axis_index(axis) % 2 == 0
+
+
+def pack_sides(v_ref, first, second, rows, cols):
+    even = on_even("cross")
     for r in range(rows + 1):
-        east_ref[2 * r : 2 * r + 2, :] = v_ref[r * STRIDE + cols : r * STRIDE + cols + 2, :]
-        west_ref[2 * r : 2 * r + 2, :] = v_ref[r * STRIDE : r * STRIDE + 2, :]
-
-
-def first_kernel(
-    rows, cols, count, offset, owner, mirror, gain, vel, acc, grad, dens, weight,
-    self_hbm, edge_hbm,
-    v_out, src_out, east, west, mask, selfs, edges, ghosts, p_ref, self_sem, edge_sem,
-):
+        east = v_ref[r * STRIDE + cols : r * STRIDE + cols + 2, :]
+        west = v_ref[r * STRIDE : r * STRIDE + 2, :]
+        first[2 * r : 2 * r + 2, :] = jnp.where(even, east, west)
+        second[2 * r : 2 * r + 2, :] = jnp.where(even, west, east)
+
+
+def first_kernel(rows, cols, *refs):
+    inputs, refs = refs[:12], refs[12:]
+    (v_out, src_out, first, second, mask, selfs, edges, ghosts), refs = refs[:8], refs[8:]
+    staged, (p_ref, small_sem, self_sem, edge_sem) = refs[:10], refs[10:]
+    self_hbm, edge_hbm = inputs[10:]
     size = p_ref.shape[1]
     slots = len(CODE_STEP)
+    small = [
+        pltpu.make_async_copy(hbm, here, small_sem.at[k])
+        for k, (hbm, here) in enumerate(zip(inputs[:10], staged))
+    ]
+    for copy in small:
+        copy.start()
     for r in range(rows):
         part = pl.ds(r * cols, cols)
         pltpu.make_async_copy(self_hbm.at[part], selfs.at[part], self_sem.at[r]).start()
+    count, offset, owner, mirror, gain, vel, acc, grad, dens, weight = staged
+    for copy in small[:3]:
+        copy.wait()
+    for r in range(rows):
         for c in range(cols):
             for k in range(slots):
                 slot = (r * cols + c) * slots + k
@@ -103,6 +119,10 @@
                 pltpu.make_async_copy(
                     edge_hbm.at[slot], edges.at[place], edge_sem.at[r]
                 ).start()
+    for r in range(rows):
+        for c in range(cols):
+            for k in range(slots):
+                place = (r * cols + c) * slots + offset[r, c, k]
                 live = jnp.where(k < count[r, c], 1.0, 0.0)
                 mask[pl.ds(place, 1), :] = jnp.full((1, size), live, f32)
     base = rows * cols * slots
@@ -110,12 +130,15 @@
         for o in range(cols):
             same = jnp.where(owner[c] == o, 1.0, 0.0)
             mask[base + c * cols + o : base + c * cols + o + 1, :] = jnp.full((1, size), same, f32)
+    for copy in small[3:]:
+        copy.wait()
 
     inside, _ = inside_grid(rows, cols, v_out.shape)
     p_ref[...] = jnp.zeros_like(p_ref)
     p_ref[: v_out.shape[0], :] = jnp.where(inside, 1.0, 0.0)
     v_out[...] = jnp.zeros_like(v_out)
     src_out[...] = jnp.zeros_like(src_out)
+    even = on_even("cross")
     for r in range(rows):
         lo = r * STRIDE + 1
         total = jnp.zeros((cols, size), f32)
@@ -125,9 +148,10 @@
         src_out[lo : lo + cols, :] = src
         v_out[lo : lo + cols, :] = -weight[r]
         head = 2 * (rows + 1) + r
-        east[head : head + 1, :] = src[cols - 1 : cols, :]
-        west[head : head + 1, :] = src[0:1, :]
-    for side in (east, west):
+        east, west = src[cols - 1 : cols, :], src[0:1, :]
+        first[head : head + 1, :] = jnp.where(even, east, west)
+        second[head : head + 1, :] = jnp.where(even, west, east)
+    for side in (first, second):
         for row in range(2 * (rows + 1) + rows, side.shape[0]):
             side[row : row + 1, :] = jnp.zeros((1, size), f32)
 
@@ -155,25 +179,28 @@
         for c in range(cols):
             tiles.block(r, c)
     tiles.store(v_out)
-    pack_sides(v_out, east, west, rows, cols)
-
-
-def add_rims(rows, total, from_north, from_south, out):
+    pack_sides(v_out, first, second, rows, cols)
+
+
+def add_rims(rows, total, first, second, out):
+    even = on_even("slab")
     has_north = lax.axis_index("slab") > 0
     out[...] = total[...]
-    out[:STRIDE, :] += jnp.where(has_north, from_north[...], 0.0)
-    if from_south is not None:
-        out[rows * STRIDE :, :] += from_south[:STRIDE, :]
+    north = jnp.where(even, second[:STRIDE, :], first[:STRIDE, :])
+    out[:STRIDE, :] += jnp.where(has_north, north, 0.0)
+    out[rows * STRIDE :, :] += jnp.where(even, first[:STRIDE, :], second[:STRIDE, :])
 
 
 def second_kernel(
-    rows, cols, mask, selfs, edges, ghosts, total, src, from_north, from_south,
-    v_out, s_out, jac_out, east, west, p_ref,
+    rows, cols, mask, selfs, edges, ghosts, total, src, rim1, rim2,
+    v_out, s_out, jac_out, side1, side2, p_ref,
 ):
     inside, _ = inside_grid(rows, cols, v_out.shape)
-    add_rims(rows, total, from_north, from_south, jac_out)
+    add_rims(rows, total, rim1, rim2, jac_out)
     s_out[...] = src[...]
-    s_out[rows * STRIDE :, :] = from_south[STRIDE:, :]
+    s_out[rows * STRIDE :, :] = jnp.where(
+        on_even("slab"), rim1[STRIDE:, :], rim2[STRIDE:, :]
+    )
     jac = jnp.where(inside, -jac_out[...], 1.0)
     s = jnp.where(inside, s_out[...] / jac, 0.0)
     p_ref[...] = jnp.zeros_like(p_ref)
@@ -186,18 +213,18 @@
         for c in range(cols):
             tiles.block(r, c)
     tiles.store(v_out)
-    for side in (east, west):
+    for side in (side1, side2):
         side[...] = jnp.zeros_like(side)
-    pack_sides(v_out, east, west, rows, cols)
+    pack_sides(v_out, side1, side2, rows, cols)
 
 
 def third_kernel(
-    rows, cols, mask, selfs, edges, ghosts, total, src, s_ref, jac, from_north, from_south,
-    v_out, w_out, east, west, sums_out, p_ref,
+    rows, cols, mask, selfs, edges, ghosts, total, src, s_ref, jac, rim1, rim2,
+    v_out, w_out, side1, side2, sums_out, p_ref,
 ):
     size = p_ref.shape[1]
     inside, own = inside_grid(rows, cols, v_out.shape)
-    add_rims(rows, total, from_north, from_south, w_out)
+    add_rims(rows, total, rim1, rim2, w_out)
     u = w_out[...]
     w = jnp.where(inside, u / jac[...], 0.0)
     p_ref[...] = jnp.zeros_like(p_ref)
@@ -209,9 +236,9 @@
         for c in range(cols):
             tiles.block(r, c)
     tiles.store(v_out)
-    for side in (east, west):
+    for side in (side1, side2):
         side[...] = jnp.zeros_like(side)
-    pack_sides(v_out, east, west, rows, cols)
+    pack_sides(v_out, side1, side2, rows, cols)
     s = s_ref[...]
 
     def whole(x):
@@ -230,34 +257,40 @@
     sums_out[...] = jnp.broadcast_to(line, sums_out.shape)
 
 
-def merge_kernel(rows, cols, with_src, with_north, *refs):
-    refs = list(refs)
-    v, from_west, from_east = refs[:3]
-    total, south = refs[3 + with_src : 5 + with_src]
+def merge_kernel(rows, cols, with_src, *refs):
+    v, side1, side2 = refs[:3]
+    total, first, second = refs[3 + with_src : 6 + with_src]
+    even = on_even("cross")
     has_west = lax.axis_index("cross") > 0
     has_east = lax.axis_index("cross") < lax.axis_size("cross") - 1
+    west = jnp.where(even, side2[...], side1[...])
+    east = jnp.where(even, side1[...], side2[...])
+    west = jnp.where(has_west, west, 0.0)
+    east = jnp.where(has_east, east, 0.0)
     total[...] = v[...]
     for r in range(rows + 1):
         lo = r * STRIDE
-        total[lo : lo + 2, :] += jnp.where(has_west, from_west[2 * r : 2 * r + 2, :], 0.0)
-        lo += cols
-        total[lo : lo + 2, :] += jnp.where(has_east, from_east[2 * r : 2 * r + 2, :], 0.0)
-    south[...] = total[rows * STRIDE :, :]
-    if with_north:
-        north = refs[5 + with_src]
-        north[:STRIDE, :] = total[:STRIDE, :]
+        total[lo : lo + 2, :] += west[2 * r : 2 * r + 2, :]
+        total[lo + cols : lo + cols + 2, :] += east[2 * r : 2 * r + 2, :]
+    top, bottom = total[:STRIDE, :], total[rows * STRIDE :, :]
+    even = on_even("slab")
+    first[:STRIDE, :] = jnp.where(even, bottom, top)
+    second[:STRIDE, :] = jnp.where(even, top, bottom)
     if with_src:
         src, src_out = refs[3], refs[7]
         src_out[...] = src[...]
         for r in range(rows):
             lo, head = r * STRIDE, 2 * (rows + 1) + r
-            src_out[lo : lo + 1, :] = from_west[head : head + 1, :]
-            src_out[lo + cols + 1 : lo + cols + 2, :] = from_east[head : head + 1, :]
-        north[STRIDE:, :] = src_out[:STRIDE, :]
-
-
-def last_kernel(rows, cols, gathered, total, from_north, s_ref, jac_ref, w_ref, pressure, residual, v):
-    add_rims(rows, total, from_north, None, v)
+            src_out[lo : lo + 1, :] = west[head : head + 1, :]
+            src_out[lo + cols + 1 : lo + cols + 2, :] = east[head : head + 1, :]
+        for out in (first, second):
+            out[STRIDE:, :] = src_out[:STRIDE, :]
+
+
+def last_kernel(
+    rows, cols, gathered, total, rim1, rim2, s_ref, jac_ref, w_ref, pressure, residual, v
+):
+    add_rims(rows, total, rim1, rim2, v)
     nu = jnp.sum(gathered[...], axis=0, keepdims=True)
     nu0, nu1, nu2, nu3 = (nu[:, k : k + 1] for k in range(4))
     rho = nu1 / nu0
@@ -278,9 +311,21 @@
         residual[r] = jac * (rs * s + rw * w) + rv * v[lo : lo + cols, :]
 
 
-def shift(value, axis, step):
-    count = lax.axis_size(axis)
-    return lax.ppermute(value, axis, [(i, (i + step) % count) for i in range(count)])
+def swap(value, second, axis):
+    slabs, crosses = lax.axis_size("slab"), lax.axis_size("cross")
+    pairs = []
+    for a in range(slabs):
+        for c in range(crosses):
+            if axis == "cross":
+                to = (a, (((c + 1) ^ 1) - 1) % crosses if second else c ^ 1)
+            elif not second:
+                to = (a ^ 1, c)
+            elif 0 < a < slabs - 1:
+                to = (((a + 1) ^ 1) - 1, c)
+            else:
+                to = (a, c ^ 1)
+            pairs.append((a * crosses + c, to[0] * crosses + to[1]))
+    return lax.ppermute(value, ("slab", "cross"), pairs)
 
 
 def per_device(
@@ -314,66 +359,71 @@
             compiler_params=pltpu.CompilerParams(vmem_limit_bytes=limit << 20),
         )(*operands)
 
-    def merge(v, east, west, src=None, north=True):
-        operands = [v, shift(east, "cross", 1), shift(west, "cross", -1)]
-        shapes = [region, line]
+    def exchange(v, first, second, src=None):
+        operands = [v, swap(first, False, "cross"), swap(second, True, "cross")]
+        shapes = [region, line, line]
         if src is not None:
             operands.append(src)
-            shapes += [(2 * STRIDE, size), region]
-        elif north:
-            shapes.append(line)
-        return call(
-            merge_kernel, shapes, [VMEM] * len(operands), operands,
-            extra=(src is not None, north),
+            shapes = [region, (2 * STRIDE, size), (2 * STRIDE, size), region]
+        total, first, second, *rest = call(
+            merge_kernel, shapes, [VMEM] * len(operands), operands, extra=(src is not None,)
         )
+        return [total, *rest, swap(first, False, "slab"), swap(second, True, "slab")]
 
     field = pltpu.VMEM((size, size), f32)
-    v, src, east, west, mask, selfs, edges, ghosts = call(
+    small = [
+        tile_count, tile_offset, ghost_owner, ghost_mirror, ghost_gain,
+        velocity, acceleration, grad_coef, density_dev, self_weight,
+    ]
+    staged = [
+        (pltpu.SMEM if k < 3 else pltpu.VMEM)(x.shape, x.dtype) for k, x in enumerate(small)
+    ]
+    v, src, first, second, *matrix = call(
         first_kernel,
         [
             region, region, side, side, (rows * cols * slots + cols * cols, size),
             (rows * cols, size, size), (rows * cols * slots, size, size), (cols, size, size),
         ],
-        [SMEM] * 3 + [VMEM] * 7 + [ANY] * 2,
+        [HBM] * 12,
         [
-            tile_count, tile_offset, ghost_owner, ghost_mirror, ghost_gain,
-            velocity, acceleration, grad_coef, density_dev, self_weight,
-            self_tiles.reshape(rows * cols, size, size),
-            edge_tiles.reshape(rows * cols * slots, size, size),
+            pltpu.with_memory_space_constraint(x, pltpu.HBM)
+            for x in small
+            + [
+                self_tiles.reshape(rows * cols, size, size),
+                edge_tiles.reshape(rows * cols * slots, size, size),
+            ]
         ],
-        [field, pltpu.SemaphoreType.DMA((rows,)), pltpu.SemaphoreType.DMA((rows,))],
+        staged
+        + [field]
+        + [pltpu.SemaphoreType.DMA((n,)) for n in (len(small), rows, rows)],
         limit=10,
     )
-    matrix = [mask, selfs, edges, ghosts]
-    total, south, north, src = merge(v, east, west, src)
-    from_north, from_south = shift(south, "slab", 1), shift(north, "slab", -1)
-
-    operands = matrix + [total, src, from_north, from_south]
-    v, s, jac, east, west = call(
+    total, src, rim1, rim2 = exchange(v, first, second, src)
+
+    operands = matrix + [total, src, rim1, rim2]
+    v, s, jac, first, second = call(
         second_kernel, [region] * 3 + [side] * 2, [VMEM] * len(operands), operands, [field]
     )
-    total, south, north = merge(v, east, west)
-    from_north, from_south = shift(south, "slab", 1), shift(north, "slab", -1)
-
-    operands = matrix + [total, src, s, jac, from_north, from_south]
-    v, w, east, west, sums = call(
+    total, rim1, rim2 = exchange(v, first, second)
+
+    operands = matrix + [total, src, s, jac, rim1, rim2]
+    v, w, first, second, sums = call(
         third_kernel,
         [region] * 2 + [side] * 2 + [(peers, size)],
         [VMEM] * len(operands), operands, [field],
     )
     gathered = lax.all_to_all(sums, ("slab", "cross"), 0, 0, tiled=True)
-    total, south = merge(v, east, west, north=False)
-    from_north = shift(south, "slab", 1)
+    total, rim1, rim2 = exchange(v, first, second)
 
     return tuple(
         pl.pallas_call(
             functools.partial(last_kernel, rows, cols),
             out_shape=[jax.ShapeDtypeStruct((rows, cols, size), f32)] * 2,
-            in_specs=[VMEM] * 6,
+            in_specs=[VMEM] * 7,
             out_specs=[VMEM] * 2,
             scratch_shapes=[pltpu.VMEM(region, f32)],
             compiler_params=pltpu.CompilerParams(vmem_limit_bytes=2 << 20),
-        )(gathered, total, from_north, s, jac, w)
+        )(gathered, total, rim1, rim2, s, jac, w)
     )
 
 

time: 79.3 us -> 58.1 us (0.73)
  local copies, waits for them, and re-layouts: 10.4 us -> 0 us
  starting transfers between devices: 42.3 us -> 37 us
  Pallas kernels: 12.7 us -> 8.13 us
    unnamed x24 -> x0, local copies, waits for them, and re-layouts: 10.4 us -> none
    pallas_call x6, Pallas kernels: 11.7 us -> 7.15 us  [call(): pl.pallas_call(functools.partial(kernel, rows, cols, *extra), out_shape=[...]
    all_to_all x1, starting transfers between devices: 16.7 us -> 13.7 us  [per_device(): gathered = lax.all_to_all(sums, ('slab', 'cross'), 0, 0, tiled=True)]
    ppermute x11 -> x12, starting transfers between devices: 25.6 us -> 23.4 us  [swap(): return lax.ppermute(value, ('slab', 'cross'), pairs)]
    all_to_all x1, waiting for transfers between devices: 3.81 us -> 1.77 us  [per_device(): gathered = lax.all_to_all(sums, ('slab', 'cross'), 0, 0, tiled=True)]
    ppermute x11 -> x12, waiting for transfers between devices: 8.85 us -> 10.3 us  [swap(): return lax.ppermute(value, ('slab', 'cross'), pairs)]
  transfers between devices with their start and end apart: 12 -> 13, of which waited for: 8 -> 8; matrix products, arithmetic and copies ran while one was open for 0% -> 0% of each run, Pallas kernels for 0% -> 0%
where the time goes in v3:
time: 58.1 us; the launch traced here: 57.9 us
  starting transfers between devices  37 us (64%)
  waiting for transfers between devices  12.1 us (21%)
  Pallas kernels  8.13 us (14%)
  between operations  0.68 us (1%)
    ppermute x12, starting transfers between devices, swap(): return lax.ppermute(value, ('slab', 'cross'), pairs)  23.4 us
    all_to_all x1, starting transfers between devices, per_device(): gathered = lax.all_to_all(sums, ('slab', 'cross'), 0, 0, tiled=True)  13.7 us
    ppermute x12, waiting for transfers between devices, swap(): return lax.ppermute(value, ('slab', 'cross'), pairs)  10.3 us
    pallas_call x6, Pallas kernels, call(): pl.pallas_call(functools.partial(kernel, rows, cols, *extra), out_shape=[...  7.15 us
    all_to_all x1, waiting for transfers between devices, per_device(): gathered = lax.all_to_all(sums, ('slab', 'cross'), 0, 0, tiled=True)  1.77 us
  transfers between devices with their start and end apart: 13, of which 8 were waited for; matrix products, arithmetic and copies ran while one was open for 0% of the time, Pallas kernels for 0%

profile of v3, /device:TPU:1, one launch (start us, length us, event | category | flops | bytes accessed | tf_op | source)
XLA Modules:
  0.0 57.9 jit_solution(8989544575761443766)
XLA Ops:
  0.6 3.7 %shard_map.131 = (f32[40,128]{1,0:T(8,128)S(1)}, f32[40,128]{1,0:T(8,128)S(1)}, f32[16,128]{1,0:T(8,128)S(1)}, f32[16,128]{1,0:T(8,128)S(1)}, f32[80,128]{1,0:T(...) custom-call(s32[4,4]{1,0:T(4,128)} %refs_0_.1, ...), custom_call_target="tpu_custom_call" | custom-call | tf_op jit(solution)/shard_map/pallas_call | solution.py:353
  4.3 2.5 %collective-permute-start = (f32[16,128]{1,0:T(8,128)S(1)}, f32[16,128]{1,0:T(8,128)S(1)}, u32[]{:S(2)}, u32[]{:S(2)}) collective-permute-start(f32[16,128]{1,0:T(8,128)S(1)} %get-tuple-element.35), channel_id=1, source_target_pairs={{0,1},{1,0},{2,3},{3,2},{4,5},{5,4},{6,7},{7,6},{8,9},{9,8},{10,11... | collective-permute-start | bytes 24584 | tf_op jit(solution)/shard_map/ppermute | solution.py:328
  6.8 4.7 %collective-permute-start.1 = (f32[16,128]{1,0:T(8,128)S(1)}, f32[16,128]{1,0:T(8,128)S(1)}, u32[]{:S(2)}, u32[]{:S(2)}) collective-permute-start(f32[16,128]{1,0:T(8,128)S(1)} %get-tuple-element.36), channel_id=1, source_target_pairs={{0,7},{1,2},{2,1},{3,4},{4,3},{5,6},{6,5},{7,0},{8,15},{9,10},{10,... | collective-permute-start | bytes 24584 | tf_op jit(solution)/shard_map/ppermute | solution.py:328
  11.5 0.0 collective-permute-done.refs_1_
  11.5 1.0 %collective-permute-done.1.refs_2_ = f32[16,128]{1,0:T(8,128)S(1)} collective-permute-done((f32[16,128]{1,0:T(8,128)S(1)}, f32[16,128]{1,0:T(8,128)S(1)}, u32[]{:S(2)}, u32[]{:S(2)}) %collective-permute-start.1) | collective-permute-done | bytes 8224 | tf_op jit(solution)/shard_map/ppermute | solution.py:328
  12.6 1.9 %collective-permute-start.2 = (f32[16,128]{1,0:T(8,128)S(1)}, f32[16,128]{1,0:T(8,128)S(1)}, u32[]{:S(2)}, u32[]{:S(2)}) collective-permute-start(f32[16,128]{1,0:T(8,128)S(1)} %get-tuple-element.40), channel_id=1, source_target_pairs={{0,8},{1,9},{2,10},{3,11},{4,12},{5,13},{6,14},{7,15},{8,0},{9,1},... | collective-permute-start | bytes 24584 | tf_op jit(solution)/shard_map/ppermute | solution.py:328
  14.5 1.3 %collective-permute-start.3 = (f32[16,128]{1,0:T(8,128)S(1)}, f32[16,128]{1,0:T(8,128)S(1)}, u32[]{:S(2)}, u32[]{:S(2)}) collective-permute-start(f32[16,128]{1,0:T(8,128)S(1)} %get-tuple-element.41), channel_id=1, source_target_pairs={{0,1},{1,0},{2,3},{3,2},{4,5},{5,4},{6,7},{7,6},{8,16},{9,17},{10,... | collective-permute-start | bytes 24584 | tf_op jit(solution)/shard_map/ppermute | solution.py:328
  15.8 0.0 collective-permute-done.2.rim1
  15.8 2.1 %collective-permute-done.3.rim2 = f32[16,128]{1,0:T(8,128)S(1)} collective-permute-done((f32[16,128]{1,0:T(8,128)S(1)}, f32[16,128]{1,0:T(8,128)S(1)}, u32[]{:S(2)}, u32[]{:S(2)}) %collective-permute-start.3) | collective-permute-done | bytes 8224 | tf_op jit(solution)/shard_map/ppermute | solution.py:328
  17.8 1.3 %shard_map.133 = (f32[40,128]{1,0:T(8,128)S(1)}, f32[40,128]{1,0:T(8,128)S(1)}, f32[40,128]{1,0:T(8,128)S(1)}, f32[16,128]{1,0:T(8,128)S(1)}, f32[16,128]{1,0:T(8,128)S(1)}) custom-call(f32[80,128]{1,0:T(8,128)S(1)} %get-tuple-element.30.mask, f32[16,128,128]{2,1,0:T(8,128)S(1)} %get-tuple-element.31.selfs, f32[64,128,128]{2,1,0:T(8,128)S(1)} %get-tuple-element.32.edges, ...), custom_call_target="tpu_custom_call" | custom-call | tf_op jit(solution)/shard_map/pallas_call | solution.py:353
  19.2 0.1 collective-permute-start.4
  19.3 3.0 %collective-permute-start.5 = (f32[16,128]{1,0:T(8,128)S(1)}, f32[16,128]{1,0:T(8,128)S(1)}, u32[]{:S(2)}, u32[]{:S(2)}) collective-permute-start(f32[16,128]{1,0:T(8,128)S(1)} %get-tuple-element.44), channel_id=1, source_target_pairs={{0,7},{1,2},{2,1},{3,4},{4,3},{5,6},{6,5},{7,0},{8,15},{9,10},{10,... | collective-permute-start | bytes 24584 | tf_op jit(solution)/shard_map/ppermute | solution.py:328
  22.3 0.0 collective-permute-done.4.refs_1_
  22.3 1.0 %collective-permute-done.5.refs_2_ = f32[16,128]{1,0:T(8,128)S(1)} collective-permute-done((f32[16,128]{1,0:T(8,128)S(1)}, f32[16,128]{1,0:T(8,128)S(1)}, u32[]{:S(2)}, u32[]{:S(2)}) %collective-permute-start.5) | collective-permute-done | bytes 8224 | tf_op jit(solution)/shard_map/ppermute | solution.py:328
  23.4 1.4 %collective-permute-start.6 = (f32[8,128]{1,0:T(8,128)S(1)}, f32[8,128]{1,0:T(8,128)S(1)}, u32[]{:S(2)}, u32[]{:S(2)}) collective-permute-start(f32[8,128]{1,0:T(8,128)S(1)} %get-tuple-element.48), channel_id=1, source_target_pairs={{0,8},{1,9},{2,10},{3,11},{4,12},{5,13},{6,14},{7,15},{8,0},{9,1},... | collective-permute-start | bytes 12296 | tf_op jit(solution)/shard_map/ppermute | solution.py:328
  24.7 0.7 %collective-permute-start.7 = (f32[8,128]{1,0:T(8,128)S(1)}, f32[8,128]{1,0:T(8,128)S(1)}, u32[]{:S(2)}, u32[]{:S(2)}) collective-permute-start(f32[8,128]{1,0:T(8,128)S(1)} %get-tuple-element.49), channel_id=1, source_target_pairs={{0,1},{1,0},{2,3},{3,2},{4,5},{5,4},{6,7},{7,6},{8,16},{9,17},{10,... | collective-permute-start | bytes 12296 | tf_op jit(solution)/shard_map/ppermute | solution.py:328
  25.5 0.1 collective-permute-done.6.rim1
  25.6 2.5 %collective-permute-done.7.rim2 = f32[8,128]{1,0:T(8,128)S(1)} collective-permute-done((f32[8,128]{1,0:T(8,128)S(1)}, f32[8,128]{1,0:T(8,128)S(1)}, u32[]{:S(2)}, u32[]{:S(2)}) %collective-permute-start.7) | collective-permute-done | bytes 4128 | tf_op jit(solution)/shard_map/ppermute | solution.py:328
  28.1 2.1 %shard_map.135 = (f32[40,128]{1,0:T(8,128)S(1)}, f32[40,128]{1,0:T(8,128)S(1)}, f32[16,128]{1,0:T(8,128)S(1)}, f32[16,128]{1,0:T(8,128)S(1)}, f32[256,128]{1,0:T(8,128)}) custom-call(f32[80,128]{1,0:T(8,128)S(1)} %get-tuple-element.30.mask, f32[16,128,128]{2,1,0:T(8,128)S(1)} %get-tuple-element.31.selfs, f32[64,128,128]{2,1,0:T(8,128)S(1)} %get-tuple-element.32.edges, ...), custom_call_target="tpu_custom_call" | custom-call | tf_op jit(solution)/shard_map/pallas_call | solution.py:353
  30.1 13.7 %all-to-all-start = ((f32[256,1,128]{2,1,0:T(1,128)}), f32[256,1,128]{2,1,0:T(1,128)S(1)}, u32[]{:S(2)}, u32[]{:S(2)}) async-start(f32[256,1,128]{2,1,0:T(1,128)} %bitcast.3), calls=%async_computation | async-start | bytes 262144 | tf_op jit(solution)/shard_map/all_to_all | solution.py:415
  43.8 1.6 %collective-permute-start.8 = (f32[16,128]{1,0:T(8,128)S(1)}, f32[16,128]{1,0:T(8,128)S(1)}, u32[]{:S(2)}, u32[]{:S(2)}) collective-permute-start(f32[16,128]{1,0:T(8,128)S(1)} %get-tuple-element.52), channel_id=1, source_target_pairs={{0,1},{1,0},{2,3},{3,2},{4,5},{5,4},{6,7},{7,6},{8,9},{9,8},{10,11... | collective-permute-start | bytes 24584 | tf_op jit(solution)/shard_map/ppermute | solution.py:328
  45.4 3.7 %collective-permute-start.9 = (f32[16,128]{1,0:T(8,128)S(1)}, f32[16,128]{1,0:T(8,128)S(1)}, u32[]{:S(2)}, u32[]{:S(2)}) collective-permute-start(f32[16,128]{1,0:T(8,128)S(1)} %get-tuple-element.53), channel_id=1, source_target_pairs={{0,7},{1,2},{2,1},{3,4},{4,3},{5,6},{6,5},{7,0},{8,15},{9,10},{10,... | collective-permute-start | bytes 24584 | tf_op jit(solution)/shard_map/ppermute | solution.py:328
  49.1 0.0 collective-permute-done.8.refs_1_
  49.2 1.5 %collective-permute-done.9.refs_2_ = f32[16,128]{1,0:T(8,128)S(1)} collective-permute-done((f32[16,128]{1,0:T(8,128)S(1)}, f32[16,128]{1,0:T(8,128)S(1)}, u32[]{:S(2)}, u32[]{:S(2)}) %collective-permute-start.9) | collective-permute-done | bytes 8224 | tf_op jit(solution)/shard_map/ppermute | solution.py:328
  50.6 1.2 %collective-permute-start.10 = (f32[8,128]{1,0:T(8,128)S(1)}, f32[8,128]{1,0:T(8,128)S(1)}, u32[]{:S(2)}, u32[]{:S(2)}) collective-permute-start(f32[8,128]{1,0:T(8,128)S(1)} %get-tuple-element.55), channel_id=1, source_target_pairs={{0,8},{1,9},{2,10},{3,11},{4,12},{5,13},{6,14},{7,15},{8,0},{9,1},... | collective-permute-start | bytes 12296 | tf_op jit(solution)/shard_map/ppermute | solution.py:328
  51.8 1.2 %collective-permute-start.11 = (f32[8,128]{1,0:T(8,128)S(1)}, f32[8,128]{1,0:T(8,128)S(1)}, u32[]{:S(2)}, u32[]{:S(2)}) collective-permute-start(f32[8,128]{1,0:T(8,128)S(1)} %get-tuple-element.56), channel_id=1, source_target_pairs={{0,1},{1,0},{2,3},{3,2},{4,5},{5,4},{6,7},{7,6},{8,16},{9,17},{10,... | collective-permute-start | bytes 12296 | tf_op jit(solution)/shard_map/ppermute | solution.py:328
  53.1 0.0 collective-permute-done.10.rim1
  53.1 2.1 %collective-permute-done.11.rim2 = f32[8,128]{1,0:T(8,128)S(1)} collective-permute-done((f32[8,128]{1,0:T(8,128)S(1)}, f32[8,128]{1,0:T(8,128)S(1)}, u32[]{:S(2)}, u32[]{:S(2)}) %collective-permute-start.11) | collective-permute-done | bytes 4128 | tf_op jit(solution)/shard_map/ppermute | solution.py:328
  55.2 1.8 %all-to-all-done = f32[256,1,128]{2,1,0:T(1,128)S(1)} async-done(((f32[256,1,128]{2,1,0:T(1,128)}), f32[256,1,128]{2,1,0:T(1,128)S(1)}, u32[]{:S(2)}, u32[]{:S(2)}) %all-to-all-start) | async-done | bytes 131104 | tf_op jit(solution)/shard_map/all_to_all | solution.py:415
  56.9 1.0 %shard_map.137 = (f32[4,4,128]{2,1,0:T(4,128)}, f32[4,4,128]{2,1,0:T(4,128)}) custom-call(f32[256,128]{1,0:T(8,128)S(1)} %bitcast.6, f32[40,128]{1,0:T(8,128)S(1)} %get-tuple-element.54.total, f32[8,128]{1,0:T(8,128)S(1)} %collective-permute-done.10.rim1, f32[8,128]{1,0:T(8,128)S(1)} %collective-permute-done.11.rim2, f32[40,128]{1,0:T(8,128)S(1)} %get-tuple-element.46.s_ref, ...), custom_call_target="tpu_custom_call" | custom-call | tf_op jit(solution)/shard_map/pallas_call | solution.py:419
  (3 shorter events, 0.1 us)
Async XLA Ops:
  4.3 7.2 %collective-permute-start = (f32[16,128]{1,0:T(8,128)S(1)}, f32[16,128]{1,0:T(8,128)S(1)}, u32[]{:S(2)}, u32[]{:S(2)}) collective-permute-start(f32[16,128]{1,0:T(8,128)S(1)} %get-tuple-element.35), channel_id=1, source_target_pairs={{0,1},{1,0},{2,3},{3,2},{4,5},{5,4},{6,7},{7,6},{8,9},{9,8},{10,11... | collective-permute-start | bytes 24584 | tf_op jit(solution)/shard_map/ppermute | solution.py:328
  6.8 5.7 %collective-permute-start.1 = (f32[16,128]{1,0:T(8,128)S(1)}, f32[16,128]{1,0:T(8,128)S(1)}, u32[]{:S(2)}, u32[]{:S(2)}) collective-permute-start(f32[16,128]{1,0:T(8,128)S(1)} %get-tuple-element.36), channel_id=1, source_target_pairs={{0,7},{1,2},{2,1},{3,4},{4,3},{5,6},{6,5},{7,0},{8,15},{9,10},{10,... | collective-permute-start | bytes 24584 | tf_op jit(solution)/shard_map/ppermute | solution.py:328
  12.6 3.2 %collective-permute-start.2 = (f32[16,128]{1,0:T(8,128)S(1)}, f32[16,128]{1,0:T(8,128)S(1)}, u32[]{:S(2)}, u32[]{:S(2)}) collective-permute-start(f32[16,128]{1,0:T(8,128)S(1)} %get-tuple-element.40), channel_id=1, source_target_pairs={{0,8},{1,9},{2,10},{3,11},{4,12},{5,13},{6,14},{7,15},{8,0},{9,1},... | collective-permute-start | bytes 24584 | tf_op jit(solution)/shard_map/ppermute | solution.py:328
  14.5 3.4 %collective-permute-start.3 = (f32[16,128]{1,0:T(8,128)S(1)}, f32[16,128]{1,0:T(8,128)S(1)}, u32[]{:S(2)}, u32[]{:S(2)}) collective-permute-start(f32[16,128]{1,0:T(8,128)S(1)} %get-tuple-element.41), channel_id=1, source_target_pairs={{0,1},{1,0},{2,3},{3,2},{4,5},{5,4},{6,7},{7,6},{8,16},{9,17},{10,... | collective-permute-start | bytes 24584 | tf_op jit(solution)/shard_map/ppermute | solution.py:328
  19.2 3.1 %collective-permute-start.4 = (f32[16,128]{1,0:T(8,128)S(1)}, f32[16,128]{1,0:T(8,128)S(1)}, u32[]{:S(2)}, u32[]{:S(2)}) collective-permute-start(f32[16,128]{1,0:T(8,128)S(1)} %get-tuple-element.43), channel_id=1, source_target_pairs={{0,1},{1,0},{2,3},{3,2},{4,5},{5,4},{6,7},{7,6},{8,9},{9,8},{10,11... | collective-permute-start | bytes 24584 | tf_op jit(solution)/shard_map/ppermute | solution.py:328
  19.3 4.1 %collective-permute-start.5 = (f32[16,128]{1,0:T(8,128)S(1)}, f32[16,128]{1,0:T(8,128)S(1)}, u32[]{:S(2)}, u32[]{:S(2)}) collective-permute-start(f32[16,128]{1,0:T(8,128)S(1)} %get-tuple-element.44), channel_id=1, source_target_pairs={{0,7},{1,2},{2,1},{3,4},{4,3},{5,6},{6,5},{7,0},{8,15},{9,10},{10,... | collective-permute-start | bytes 24584 | tf_op jit(solution)/shard_map/ppermute | solution.py:328
  23.4 2.2 %collective-permute-start.6 = (f32[8,128]{1,0:T(8,128)S(1)}, f32[8,128]{1,0:T(8,128)S(1)}, u32[]{:S(2)}, u32[]{:S(2)}) collective-permute-start(f32[8,128]{1,0:T(8,128)S(1)} %get-tuple-element.48), channel_id=1, source_target_pairs={{0,8},{1,9},{2,10},{3,11},{4,12},{5,13},{6,14},{7,15},{8,0},{9,1},... | collective-permute-start | bytes 12296 | tf_op jit(solution)/shard_map/ppermute | solution.py:328
  24.7 3.3 %collective-permute-start.7 = (f32[8,128]{1,0:T(8,128)S(1)}, f32[8,128]{1,0:T(8,128)S(1)}, u32[]{:S(2)}, u32[]{:S(2)}) collective-permute-start(f32[8,128]{1,0:T(8,128)S(1)} %get-tuple-element.49), channel_id=1, source_target_pairs={{0,1},{1,0},{2,3},{3,2},{4,5},{5,4},{6,7},{7,6},{8,16},{9,17},{10,... | collective-permute-start | bytes 12296 | tf_op jit(solution)/shard_map/ppermute | solution.py:328
  30.1 26.8 %all-to-all-start = ((f32[256,1,128]{2,1,0:T(1,128)}), f32[256,1,128]{2,1,0:T(1,128)S(1)}, u32[]{:S(2)}, u32[]{:S(2)}) async-start(f32[256,1,128]{2,1,0:T(1,128)} %bitcast.3), calls=%async_computation | async-start | bytes 262144 | tf_op jit(solution)/shard_map/all_to_all | solution.py:415
  43.8 5.3 %collective-permute-start.8 = (f32[16,128]{1,0:T(8,128)S(1)}, f32[16,128]{1,0:T(8,128)S(1)}, u32[]{:S(2)}, u32[]{:S(2)}) collective-permute-start(f32[16,128]{1,0:T(8,128)S(1)} %get-tuple-element.52), channel_id=1, source_target_pairs={{0,1},{1,0},{2,3},{3,2},{4,5},{5,4},{6,7},{7,6},{8,9},{9,8},{10,11... | collective-permute-start | bytes 24584 | tf_op jit(solution)/shard_map/ppermute | solution.py:328
  45.4 5.2 %collective-permute-start.9 = (f32[16,128]{1,0:T(8,128)S(1)}, f32[16,128]{1,0:T(8,128)S(1)}, u32[]{:S(2)}, u32[]{:S(2)}) collective-permute-start(f32[16,128]{1,0:T(8,128)S(1)} %get-tuple-element.53), channel_id=1, source_target_pairs={{0,7},{1,2},{2,1},{3,4},{4,3},{5,6},{6,5},{7,0},{8,15},{9,10},{10,... | collective-permute-start | bytes 24584 | tf_op jit(solution)/shard_map/ppermute | solution.py:328
  50.6 2.5 %collective-permute-start.10 = (f32[8,128]{1,0:T(8,128)S(1)}, f32[8,128]{1,0:T(8,128)S(1)}, u32[]{:S(2)}, u32[]{:S(2)}) collective-permute-start(f32[8,128]{1,0:T(8,128)S(1)} %get-tuple-element.55), channel_id=1, source_target_pairs={{0,8},{1,9},{2,10},{3,11},{4,12},{5,13},{6,14},{7,15},{8,0},{9,1},... | collective-permute-start | bytes 12296 | tf_op jit(solution)/shard_map/ppermute | solution.py:328
  51.8 3.3 %collective-permute-start.11 = (f32[8,128]{1,0:T(8,128)S(1)}, f32[8,128]{1,0:T(8,128)S(1)}, u32[]{:S(2)}, u32[]{:S(2)}) collective-permute-start(f32[8,128]{1,0:T(8,128)S(1)} %get-tuple-element.56), channel_id=1, source_target_pairs={{0,1},{1,0},{2,3},{3,2},{4,5},{5,4},{6,7},{7,6},{8,16},{9,17},{10,... | collective-permute-start | bytes 12296 | tf_op jit(solution)/shard_map/ppermute | solution.py:328

commit v4 on v3

--- a/solution.py
+++ b/solution.py
@@ -6,6 +6,7 @@
 from jax.experimental import pallas as pl
 from jax.experimental.pallas import tpu as pltpu
 from jax.sharding import PartitionSpec as P
+
 
 STRIDE = 8
 CODE_STEP = (1, STRIDE - 1, STRIDE, STRIDE + 1)
@@ -34,7 +35,6 @@
         self.size = p_ref.shape[1]
         full = (self.size, self.size)
         self.lane = lax.broadcasted_iota(jnp.int32, full, 1)
-        self.eye = self.lane == lax.broadcasted_iota(jnp.int32, full, 0)
         self.columns = jnp.transpose(p_ref[...])
         self.sums = jnp.zeros(full, f32)
         self.parts = {}
@@ -49,7 +49,7 @@
         size, cols = self.size, self.cols
         at = r * STRIDE + c + 1
         down = jnp.broadcast_to(self.columns[:, at : at + 1], (size, size))
-        tile = jnp.where(self.eye, 0.0, self.selfs[r * cols + c])
+        tile = self.selfs[r * cols + c]
         acc = tile * self.p_ref[at : at + 1, :]
         self.fold(tile * down, at)
         for code, distance in enumerate(CODE_STEP):
@@ -95,9 +95,9 @@
 def first_kernel(rows, cols, *refs):
     inputs, refs = refs[:12], refs[12:]
     (v_out, src_out, first, second, mask, selfs, edges, ghosts), refs = refs[:8], refs[8:]
-    staged, (p_ref, small_sem, self_sem, edge_sem) = refs[:10], refs[10:]
+    staged, (self_in, edge_in, small_sem, self_sem, edge_sem) = refs[:10], refs[10:]
     self_hbm, edge_hbm = inputs[10:]
-    size = p_ref.shape[1]
+    size = v_out.shape[1]
     slots = len(CODE_STEP)
     small = [
         pltpu.make_async_copy(hbm, here, small_sem.at[k])
@@ -107,35 +107,19 @@
         copy.start()
     for r in range(rows):
         part = pl.ds(r * cols, cols)
-        pltpu.make_async_copy(self_hbm.at[part], selfs.at[part], self_sem.at[r]).start()
+        pltpu.make_async_copy(self_hbm.at[part], self_in.at[part], self_sem.at[r]).start()
+    for r in range(rows):
+        part = pl.ds(r * cols * slots, cols * slots)
+        pltpu.make_async_copy(edge_hbm.at[part], edge_in.at[part], edge_sem.at[r]).start()
     count, offset, owner, mirror, gain, vel, acc, grad, dens, weight = staged
-    for copy in small[:3]:
+    for copy in small:
         copy.wait()
-    for r in range(rows):
-        for c in range(cols):
-            for k in range(slots):
-                slot = (r * cols + c) * slots + k
-                place = (r * cols + c) * slots + offset[r, c, k]
-                pltpu.make_async_copy(
-                    edge_hbm.at[slot], edges.at[place], edge_sem.at[r]
-                ).start()
-    for r in range(rows):
-        for c in range(cols):
-            for k in range(slots):
-                place = (r * cols + c) * slots + offset[r, c, k]
-                live = jnp.where(k < count[r, c], 1.0, 0.0)
-                mask[pl.ds(place, 1), :] = jnp.full((1, size), live, f32)
     base = rows * cols * slots
     for c in range(cols):
         for o in range(cols):
             same = jnp.where(owner[c] == o, 1.0, 0.0)
             mask[base + c * cols + o : base + c * cols + o + 1, :] = jnp.full((1, size), same, f32)
-    for copy in small[3:]:
-        copy.wait()
-
-    inside, _ = inside_grid(rows, cols, v_out.shape)
-    p_ref[...] = jnp.zeros_like(p_ref)
-    p_ref[: v_out.shape[0], :] = jnp.where(inside, 1.0, 0.0)
+
     v_out[...] = jnp.zeros_like(v_out)
     src_out[...] = jnp.zeros_like(src_out)
     even = on_even("cross")
@@ -162,23 +146,54 @@
         jnp.concatenate([gain[...] * jnp.where(on_wall, -1.0, 0.0), pad], axis=0)
     )
     lane = lax.broadcasted_iota(jnp.int32, (size, size), 1)
-    sub = lax.broadcasted_iota(jnp.int32, (size, size), 0)
+    eye = lane == lax.broadcasted_iota(jnp.int32, (size, size), 0)
     lanef = lane.astype(f32)
     for c in range(cols):
         hit = lanef == mirrors[:, c : c + 1]
         tile = jnp.where(hit, gains[:, c : c + 1], 0.0)
         other = jnp.where(owner[c] == c, 0.0, 1.0)
-        ghosts[c] = jnp.where(lane == sub, tile * other, tile)
-
-    tiles = Tiles(rows, cols, p_ref, mask, selfs, edges, ghosts)
+        ghosts[c] = jnp.where(eye, tile * other, tile)
+
+    has_south = lax.axis_index("slab") < lax.axis_size("slab") - 1
+    has_west = lax.axis_index("cross") > 0
+    has_east = lax.axis_index("cross") < lax.axis_size("cross") - 1
+    sums = jnp.zeros((size, size), f32)
     for r in range(rows):
         part = pl.ds(r * cols, cols)
-        pltpu.make_async_copy(self_hbm.at[part], selfs.at[part], self_sem.at[r]).wait()
+        pltpu.make_async_copy(self_hbm.at[part], self_in.at[part], self_sem.at[r]).wait()
         part = pl.ds(r * cols * slots, cols * slots)
-        pltpu.make_async_copy(edge_hbm.at[part], edges.at[part], edge_sem.at[r]).wait()
+        pltpu.make_async_copy(edge_hbm.at[part], edge_in.at[part], edge_sem.at[r]).wait()
         for c in range(cols):
-            tiles.block(r, c)
-    tiles.store(v_out)
+            block = r * cols + c
+            at = r * STRIDE + c + 1
+            tile = jnp.where(eye, 0.0, self_in[block])
+            selfs[block] = tile
+            rowwise = tile
+            v_out[at : at + 1, :] += jnp.sum(tile, axis=0, keepdims=True)
+            for k in range(slots):
+                code = offset[r, c, k]
+                place = block * slots + code
+                live = jnp.where(k < count[r, c], 1.0, 0.0)
+                mask[pl.ds(place, 1), :] = jnp.full((1, size), live, f32)
+                there = jnp.asarray(True)
+                if c == 0:
+                    there = there & (has_west | (code != 1))
+                if c == cols - 1:
+                    there = there & (has_east | ((code != 0) & (code != 3)))
+                if r == rows - 1:
+                    there = there & (has_south | (code == 0))
+                tile = edge_in[block * slots + k]
+                edges[place] = tile
+                rowwise += tile * jnp.where(there, live, 0.0)
+                step = jnp.where(code == 0, CODE_STEP[0], CODE_STEP[1] - 1 + code)
+                v_out[pl.ds(at + step, 1), :] += jnp.sum(tile, axis=0, keepdims=True) * live
+            if r == rows - 1:
+                tile = ghosts[c]
+                rowwise += tile
+                j = r * STRIDE + 1 + owner[c]
+                v_out[pl.ds(j, 1), :] += jnp.sum(tile, axis=0, keepdims=True)
+            sums = jnp.where(lane == at, jnp.sum(rowwise, axis=1, keepdims=True), sums)
+    v_out[...] += jnp.transpose(sums)[: v_out.shape[0], :]
     pack_sides(v_out, first, second, rows, cols)
 
 
@@ -360,7 +375,9 @@
         )(*operands)
 
     def exchange(v, first, second, src=None):
-        operands = [v, swap(first, False, "cross"), swap(second, True, "cross")]
+        first = swap(first, False, "cross")
+        second = swap(second, True, "cross")
+        operands = [v, first, second]
         shapes = [region, line, line]
         if src is not None:
             operands.append(src)
@@ -394,9 +411,9 @@
             ]
         ],
         staged
-        + [field]
+        + [pltpu.VMEM((n, size, size), f32) for n in (rows * cols, rows * cols * slots)]
         + [pltpu.SemaphoreType.DMA((n,)) for n in (len(small), rows, rows)],
-        limit=10,
+        limit=16,
     )
     total, src, rim1, rim2 = exchange(v, first, second, src)
 

time: 58.1 us -> 58.2 us (level)
  no operation moved by 1% of the time
where the time goes in v4:
time: 58.2 us; the launch traced here: 58 us
  starting transfers between devices  37 us (64%)
  waiting for transfers between devices  12.1 us (21%)
  Pallas kernels  8.24 us (14%)
  between operations  0.68 us (1%)
    ppermute x12, starting transfers between devices, swap(): return lax.ppermute(value, ('slab', 'cross'), pairs)  23.4 us
    all_to_all x1, starting transfers between devices, per_device(): gathered = lax.all_to_all(sums, ('slab', 'cross'), 0, 0, tiled=True)  13.7 us
    ppermute x12, waiting for transfers between devices, swap(): return lax.ppermute(value, ('slab', 'cross'), pairs)  10.3 us
    pallas_call x6, Pallas kernels, call(): pl.pallas_call(functools.partial(kernel, rows, cols, *extra), out_shape=[...  7.26 us
    all_to_all x1, waiting for transfers between devices, per_device(): gathered = lax.all_to_all(sums, ('slab', 'cross'), 0, 0, tiled=True)  1.77 us
  transfers between devices with their start and end apart: 13, of which 8 were waited for; matrix products, arithmetic and copies ran while one was open for 0% of the time, Pallas kernels for 0%

profile of v4, /device:TPU:1, one launch (start us, length us, event | category | flops | bytes accessed | tf_op | source)
XLA Modules:
  0.0 58.0 jit_solution(9451762698624981585)
XLA Ops:
  0.6 3.8 %shard_map.131 = (f32[40,128]{1,0:T(8,128)S(1)}, f32[40,128]{1,0:T(8,128)S(1)}, f32[16,128]{1,0:T(8,128)S(1)}, f32[16,128]{1,0:T(8,128)S(1)}, f32[80,128]{1,0:T(...) custom-call(s32[4,4]{1,0:T(4,128)} %refs_0_.1, ...), custom_call_target="tpu_custom_call" | custom-call | tf_op jit(solution)/shard_map/pallas_call | solution.py:368
  4.4 2.5 %collective-permute-start = (f32[16,128]{1,0:T(8,128)S(1)}, f32[16,128]{1,0:T(8,128)S(1)}, u32[]{:S(2)}, u32[]{:S(2)}) collective-permute-start(f32[16,128]{1,0:T(8,128)S(1)} %get-tuple-element.35), channel_id=1, source_target_pairs={{0,1},{1,0},{2,3},{3,2},{4,5},{5,4},{6,7},{7,6},{8,9},{9,8},{10,11... | collective-permute-start | bytes 24584 | tf_op jit(solution)/shard_map/ppermute | solution.py:343
  7.0 4.7 %collective-permute-start.1 = (f32[16,128]{1,0:T(8,128)S(1)}, f32[16,128]{1,0:T(8,128)S(1)}, u32[]{:S(2)}, u32[]{:S(2)}) collective-permute-start(f32[16,128]{1,0:T(8,128)S(1)} %get-tuple-element.36), channel_id=1, source_target_pairs={{0,7},{1,2},{2,1},{3,4},{4,3},{5,6},{6,5},{7,0},{8,15},{9,10},{10,... | collective-permute-start | bytes 24584 | tf_op jit(solution)/shard_map/ppermute | solution.py:343
  11.6 0.0 collective-permute-done.refs_1_
  11.6 1.0 %collective-permute-done.1.refs_2_ = f32[16,128]{1,0:T(8,128)S(1)} collective-permute-done((f32[16,128]{1,0:T(8,128)S(1)}, f32[16,128]{1,0:T(8,128)S(1)}, u32[]{:S(2)}, u32[]{:S(2)}) %collective-permute-start.1) | collective-permute-done | bytes 8224 | tf_op jit(solution)/shard_map/ppermute | solution.py:343
  12.7 1.9 %collective-permute-start.2 = (f32[16,128]{1,0:T(8,128)S(1)}, f32[16,128]{1,0:T(8,128)S(1)}, u32[]{:S(2)}, u32[]{:S(2)}) collective-permute-start(f32[16,128]{1,0:T(8,128)S(1)} %get-tuple-element.40), channel_id=1, source_target_pairs={{0,8},{1,9},{2,10},{3,11},{4,12},{5,13},{6,14},{7,15},{8,0},{9,1},... | collective-permute-start | bytes 24584 | tf_op jit(solution)/shard_map/ppermute | solution.py:343
  14.6 1.3 %collective-permute-start.3 = (f32[16,128]{1,0:T(8,128)S(1)}, f32[16,128]{1,0:T(8,128)S(1)}, u32[]{:S(2)}, u32[]{:S(2)}) collective-permute-start(f32[16,128]{1,0:T(8,128)S(1)} %get-tuple-element.41), channel_id=1, source_target_pairs={{0,1},{1,0},{2,3},{3,2},{4,5},{5,4},{6,7},{7,6},{8,16},{9,17},{10,... | collective-permute-start | bytes 24584 | tf_op jit(solution)/shard_map/ppermute | solution.py:343
  15.9 0.0 collective-permute-done.2.rim1
  15.9 2.1 %collective-permute-done.3.rim2 = f32[16,128]{1,0:T(8,128)S(1)} collective-permute-done((f32[16,128]{1,0:T(8,128)S(1)}, f32[16,128]{1,0:T(8,128)S(1)}, u32[]{:S(2)}, u32[]{:S(2)}) %collective-permute-start.3) | collective-permute-done | bytes 8224 | tf_op jit(solution)/shard_map/ppermute | solution.py:343
  18.0 1.3 %shard_map.133 = (f32[40,128]{1,0:T(8,128)S(1)}, f32[40,128]{1,0:T(8,128)S(1)}, f32[40,128]{1,0:T(8,128)S(1)}, f32[16,128]{1,0:T(8,128)S(1)}, f32[16,128]{1,0:T(8,128)S(1)}) custom-call(f32[80,128]{1,0:T(8,128)S(1)} %get-tuple-element.30.mask, f32[16,128,128]{2,1,0:T(8,128)S(1)} %get-tuple-element.31.selfs, f32[64,128,128]{2,1,0:T(8,128)S(1)} %get-tuple-element.32.edges, ...), custom_call_target="tpu_custom_call" | custom-call | tf_op jit(solution)/shard_map/pallas_call | solution.py:368
  19.3 0.1 collective-permute-start.4
  19.4 3.0 %collective-permute-start.5 = (f32[16,128]{1,0:T(8,128)S(1)}, f32[16,128]{1,0:T(8,128)S(1)}, u32[]{:S(2)}, u32[]{:S(2)}) collective-permute-start(f32[16,128]{1,0:T(8,128)S(1)} %get-tuple-element.44), channel_id=1, source_target_pairs={{0,7},{1,2},{2,1},{3,4},{4,3},{5,6},{6,5},{7,0},{8,15},{9,10},{10,... | collective-permute-start | bytes 24584 | tf_op jit(solution)/shard_map/ppermute | solution.py:343
  22.4 0.0 collective-permute-done.4.refs_1_
  22.4 1.0 %collective-permute-done.5.refs_2_ = f32[16,128]{1,0:T(8,128)S(1)} collective-permute-done((f32[16,128]{1,0:T(8,128)S(1)}, f32[16,128]{1,0:T(8,128)S(1)}, u32[]{:S(2)}, u32[]{:S(2)}) %collective-permute-start.5) | collective-permute-done | bytes 8224 | tf_op jit(solution)/shard_map/ppermute | solution.py:343
  23.5 1.4 %collective-permute-start.6 = (f32[8,128]{1,0:T(8,128)S(1)}, f32[8,128]{1,0:T(8,128)S(1)}, u32[]{:S(2)}, u32[]{:S(2)}) collective-permute-start(f32[8,128]{1,0:T(8,128)S(1)} %get-tuple-element.48), channel_id=1, source_target_pairs={{0,8},{1,9},{2,10},{3,11},{4,12},{5,13},{6,14},{7,15},{8,0},{9,1},... | collective-permute-start | bytes 12296 | tf_op jit(solution)/shard_map/ppermute | solution.py:343
  24.9 0.7 %collective-permute-start.7 = (f32[8,128]{1,0:T(8,128)S(1)}, f32[8,128]{1,0:T(8,128)S(1)}, u32[]{:S(2)}, u32[]{:S(2)}) collective-permute-start(f32[8,128]{1,0:T(8,128)S(1)} %get-tuple-element.49), channel_id=1, source_target_pairs={{0,1},{1,0},{2,3},{3,2},{4,5},{5,4},{6,7},{7,6},{8,16},{9,17},{10,... | collective-permute-start | bytes 12296 | tf_op jit(solution)/shard_map/ppermute | solution.py:343
  25.6 0.1 collective-permute-done.6.rim1
  25.7 2.5 %collective-permute-done.7.rim2 = f32[8,128]{1,0:T(8,128)S(1)} collective-permute-done((f32[8,128]{1,0:T(8,128)S(1)}, f32[8,128]{1,0:T(8,128)S(1)}, u32[]{:S(2)}, u32[]{:S(2)}) %collective-permute-start.7) | collective-permute-done | bytes 4128 | tf_op jit(solution)/shard_map/ppermute | solution.py:343
  28.2 2.1 %shard_map.135 = (f32[40,128]{1,0:T(8,128)S(1)}, f32[40,128]{1,0:T(8,128)S(1)}, f32[16,128]{1,0:T(8,128)S(1)}, f32[16,128]{1,0:T(8,128)S(1)}, f32[256,128]{1,0:T(8,128)}) custom-call(f32[80,128]{1,0:T(8,128)S(1)} %get-tuple-element.30.mask, f32[16,128,128]{2,1,0:T(8,128)S(1)} %get-tuple-element.31.selfs, f32[64,128,128]{2,1,0:T(8,128)S(1)} %get-tuple-element.32.edges, ...), custom_call_target="tpu_custom_call" | custom-call | tf_op jit(solution)/shard_map/pallas_call | solution.py:368
  30.2 13.7 %all-to-all-start = ((f32[256,1,128]{2,1,0:T(1,128)}), f32[256,1,128]{2,1,0:T(1,128)S(1)}, u32[]{:S(2)}, u32[]{:S(2)}) async-start(f32[256,1,128]{2,1,0:T(1,128)} %bitcast.3), calls=%async_computation | async-start | bytes 262144 | tf_op jit(solution)/shard_map/all_to_all | solution.py:432
  44.0 1.6 %collective-permute-start.8 = (f32[16,128]{1,0:T(8,128)S(1)}, f32[16,128]{1,0:T(8,128)S(1)}, u32[]{:S(2)}, u32[]{:S(2)}) collective-permute-start(f32[16,128]{1,0:T(8,128)S(1)} %get-tuple-element.52), channel_id=1, source_target_pairs={{0,1},{1,0},{2,3},{3,2},{4,5},{5,4},{6,7},{7,6},{8,9},{9,8},{10,11... | collective-permute-start | bytes 24584 | tf_op jit(solution)/shard_map/ppermute | solution.py:343
  45.5 3.7 %collective-permute-start.9 = (f32[16,128]{1,0:T(8,128)S(1)}, f32[16,128]{1,0:T(8,128)S(1)}, u32[]{:S(2)}, u32[]{:S(2)}) collective-permute-start(f32[16,128]{1,0:T(8,128)S(1)} %get-tuple-element.53), channel_id=1, source_target_pairs={{0,7},{1,2},{2,1},{3,4},{4,3},{5,6},{6,5},{7,0},{8,15},{9,10},{10,... | collective-permute-start | bytes 24584 | tf_op jit(solution)/shard_map/ppermute | solution.py:343
  49.3 0.0 collective-permute-done.8.refs_1_
  49.3 1.5 %collective-permute-done.9.refs_2_ = f32[16,128]{1,0:T(8,128)S(1)} collective-permute-done((f32[16,128]{1,0:T(8,128)S(1)}, f32[16,128]{1,0:T(8,128)S(1)}, u32[]{:S(2)}, u32[]{:S(2)}) %collective-permute-start.9) | collective-permute-done | bytes 8224 | tf_op jit(solution)/shard_map/ppermute | solution.py:343
  50.7 1.2 %collective-permute-start.10 = (f32[8,128]{1,0:T(8,128)S(1)}, f32[8,128]{1,0:T(8,128)S(1)}, u32[]{:S(2)}, u32[]{:S(2)}) collective-permute-start(f32[8,128]{1,0:T(8,128)S(1)} %get-tuple-element.55), channel_id=1, source_target_pairs={{0,8},{1,9},{2,10},{3,11},{4,12},{5,13},{6,14},{7,15},{8,0},{9,1},... | collective-permute-start | bytes 12296 | tf_op jit(solution)/shard_map/ppermute | solution.py:343
  52.0 1.2 %collective-permute-start.11 = (f32[8,128]{1,0:T(8,128)S(1)}, f32[8,128]{1,0:T(8,128)S(1)}, u32[]{:S(2)}, u32[]{:S(2)}) collective-permute-start(f32[8,128]{1,0:T(8,128)S(1)} %get-tuple-element.56), channel_id=1, source_target_pairs={{0,1},{1,0},{2,3},{3,2},{4,5},{5,4},{6,7},{7,6},{8,16},{9,17},{10,... | collective-permute-start | bytes 12296 | tf_op jit(solution)/shard_map/ppermute | solution.py:343
  53.2 0.0 collective-permute-done.10.rim1
  53.2 2.1 %collective-permute-done.11.rim2 = f32[8,128]{1,0:T(8,128)S(1)} collective-permute-done((f32[8,128]{1,0:T(8,128)S(1)}, f32[8,128]{1,0:T(8,128)S(1)}, u32[]{:S(2)}, u32[]{:S(2)}) %collective-permute-start.11) | collective-permute-done | bytes 4128 | tf_op jit(solution)/shard_map/ppermute | solution.py:343
  55.3 1.8 %all-to-all-done = f32[256,1,128]{2,1,0:T(1,128)S(1)} async-done(((f32[256,1,128]{2,1,0:T(1,128)}), f32[256,1,128]{2,1,0:T(1,128)S(1)}, u32[]{:S(2)}, u32[]{:S(2)}) %all-to-all-start) | async-done | bytes 131104 | tf_op jit(solution)/shard_map/all_to_all | solution.py:432
  57.1 1.0 %shard_map.137 = (f32[4,4,128]{2,1,0:T(4,128)}, f32[4,4,128]{2,1,0:T(4,128)}) custom-call(f32[256,128]{1,0:T(8,128)S(1)} %bitcast.6, f32[40,128]{1,0:T(8,128)S(1)} %get-tuple-element.54.total, f32[8,128]{1,0:T(8,128)S(1)} %collective-permute-done.10.rim1, f32[8,128]{1,0:T(8,128)S(1)} %collective-permute-done.11.rim2, f32[40,128]{1,0:T(8,128)S(1)} %get-tuple-element.46.s_ref, ...), custom_call_target="tpu_custom_call" | custom-call | tf_op jit(solution)/shard_map/pallas_call | solution.py:436
  (3 shorter events, 0.1 us)
Async XLA Ops:
  4.4 7.2 %collective-permute-start = (f32[16,128]{1,0:T(8,128)S(1)}, f32[16,128]{1,0:T(8,128)S(1)}, u32[]{:S(2)}, u32[]{:S(2)}) collective-permute-start(f32[16,128]{1,0:T(8,128)S(1)} %get-tuple-element.35), channel_id=1, source_target_pairs={{0,1},{1,0},{2,3},{3,2},{4,5},{5,4},{6,7},{7,6},{8,9},{9,8},{10,11... | collective-permute-start | bytes 24584 | tf_op jit(solution)/shard_map/ppermute | solution.py:343
  7.0 5.7 %collective-permute-start.1 = (f32[16,128]{1,0:T(8,128)S(1)}, f32[16,128]{1,0:T(8,128)S(1)}, u32[]{:S(2)}, u32[]{:S(2)}) collective-permute-start(f32[16,128]{1,0:T(8,128)S(1)} %get-tuple-element.36), channel_id=1, source_target_pairs={{0,7},{1,2},{2,1},{3,4},{4,3},{5,6},{6,5},{7,0},{8,15},{9,10},{10,... | collective-permute-start | bytes 24584 | tf_op jit(solution)/shard_map/ppermute | solution.py:343
  12.7 3.2 %collective-permute-start.2 = (f32[16,128]{1,0:T(8,128)S(1)}, f32[16,128]{1,0:T(8,128)S(1)}, u32[]{:S(2)}, u32[]{:S(2)}) collective-permute-start(f32[16,128]{1,0:T(8,128)S(1)} %get-tuple-element.40), channel_id=1, source_target_pairs={{0,8},{1,9},{2,10},{3,11},{4,12},{5,13},{6,14},{7,15},{8,0},{9,1},... | collective-permute-start | bytes 24584 | tf_op jit(solution)/shard_map/ppermute | solution.py:343
  14.6 3.4 %collective-permute-start.3 = (f32[16,128]{1,0:T(8,128)S(1)}, f32[16,128]{1,0:T(8,128)S(1)}, u32[]{:S(2)}, u32[]{:S(2)}) collective-permute-start(f32[16,128]{1,0:T(8,128)S(1)} %get-tuple-element.41), channel_id=1, source_target_pairs={{0,1},{1,0},{2,3},{3,2},{4,5},{5,4},{6,7},{7,6},{8,16},{9,17},{10,... | collective-permute-start | bytes 24584 | tf_op jit(solution)/shard_map/ppermute | solution.py:343
  19.3 3.1 %collective-permute-start.4 = (f32[16,128]{1,0:T(8,128)S(1)}, f32[16,128]{1,0:T(8,128)S(1)}, u32[]{:S(2)}, u32[]{:S(2)}) collective-permute-start(f32[16,128]{1,0:T(8,128)S(1)} %get-tuple-element.43), channel_id=1, source_target_pairs={{0,1},{1,0},{2,3},{3,2},{4,5},{5,4},{6,7},{7,6},{8,9},{9,8},{10,11... | collective-permute-start | bytes 24584 | tf_op jit(solution)/shard_map/ppermute | solution.py:343
  19.4 4.1 %collective-permute-start.5 = (f32[16,128]{1,0:T(8,128)S(1)}, f32[16,128]{1,0:T(8,128)S(1)}, u32[]{:S(2)}, u32[]{:S(2)}) collective-permute-start(f32[16,128]{1,0:T(8,128)S(1)} %get-tuple-element.44), channel_id=1, source_target_pairs={{0,7},{1,2},{2,1},{3,4},{4,3},{5,6},{6,5},{7,0},{8,15},{9,10},{10,... | collective-permute-start | bytes 24584 | tf_op jit(solution)/shard_map/ppermute | solution.py:343
  23.5 2.2 %collective-permute-start.6 = (f32[8,128]{1,0:T(8,128)S(1)}, f32[8,128]{1,0:T(8,128)S(1)}, u32[]{:S(2)}, u32[]{:S(2)}) collective-permute-start(f32[8,128]{1,0:T(8,128)S(1)} %get-tuple-element.48), channel_id=1, source_target_pairs={{0,8},{1,9},{2,10},{3,11},{4,12},{5,13},{6,14},{7,15},{8,0},{9,1},... | collective-permute-start | bytes 12296 | tf_op jit(solution)/shard_map/ppermute | solution.py:343
  24.9 3.3 %collective-permute-start.7 = (f32[8,128]{1,0:T(8,128)S(1)}, f32[8,128]{1,0:T(8,128)S(1)}, u32[]{:S(2)}, u32[]{:S(2)}) collective-permute-start(f32[8,128]{1,0:T(8,128)S(1)} %get-tuple-element.49), channel_id=1, source_target_pairs={{0,1},{1,0},{2,3},{3,2},{4,5},{5,4},{6,7},{7,6},{8,16},{9,17},{10,... | collective-permute-start | bytes 12296 | tf_op jit(solution)/shard_map/ppermute | solution.py:343
  30.2 26.8 %all-to-all-start = ((f32[256,1,128]{2,1,0:T(1,128)}), f32[256,1,128]{2,1,0:T(1,128)S(1)}, u32[]{:S(2)}, u32[]{:S(2)}) async-start(f32[256,1,128]{2,1,0:T(1,128)} %bitcast.3), calls=%async_computation | async-start | bytes 262144 | tf_op jit(solution)/shard_map/all_to_all | solution.py:432
  44.0 5.3 %collective-permute-start.8 = (f32[16,128]{1,0:T(8,128)S(1)}, f32[16,128]{1,0:T(8,128)S(1)}, u32[]{:S(2)}, u32[]{:S(2)}) collective-permute-start(f32[16,128]{1,0:T(8,128)S(1)} %get-tuple-element.52), channel_id=1, source_target_pairs={{0,1},{1,0},{2,3},{3,2},{4,5},{5,4},{6,7},{7,6},{8,9},{9,8},{10,11... | collective-permute-start | bytes 24584 | tf_op jit(solution)/shard_map/ppermute | solution.py:343
  45.5 5.2 %collective-permute-start.9 = (f32[16,128]{1,0:T(8,128)S(1)}, f32[16,128]{1,0:T(8,128)S(1)}, u32[]{:S(2)}, u32[]{:S(2)}) collective-permute-start(f32[16,128]{1,0:T(8,128)S(1)} %get-tuple-element.53), channel_id=1, source_target_pairs={{0,7},{1,2},{2,1},{3,4},{4,3},{5,6},{6,5},{7,0},{8,15},{9,10},{10,... | collective-permute-start | bytes 24584 | tf_op jit(solution)/shard_map/ppermute | solution.py:343
  50.7 2.5 %collective-permute-start.10 = (f32[8,128]{1,0:T(8,128)S(1)}, f32[8,128]{1,0:T(8,128)S(1)}, u32[]{:S(2)}, u32[]{:S(2)}) collective-permute-start(f32[8,128]{1,0:T(8,128)S(1)} %get-tuple-element.55), channel_id=1, source_target_pairs={{0,8},{1,9},{2,10},{3,11},{4,12},{5,13},{6,14},{7,15},{8,0},{9,1},... | collective-permute-start | bytes 12296 | tf_op jit(solution)/shard_map/ppermute | solution.py:343
  52.0 3.3 %collective-permute-start.11 = (f32[8,128]{1,0:T(8,128)S(1)}, f32[8,128]{1,0:T(8,128)S(1)}, u32[]{:S(2)}, u32[]{:S(2)}) collective-permute-start(f32[8,128]{1,0:T(8,128)S(1)} %get-tuple-element.56), channel_id=1, source_target_pairs={{0,1},{1,0},{2,3},{3,2},{4,5},{5,4},{6,7},{7,6},{8,16},{9,17},{10,... | collective-permute-start | bytes 12296 | tf_op jit(solution)/shard_map/ppermute | solution.py:343

commit v5 on v3

--- a/solution.py
+++ b/solution.py
@@ -6,6 +6,7 @@
 from jax.experimental import pallas as pl
 from jax.experimental.pallas import tpu as pltpu
 from jax.sharding import PartitionSpec as P
+
 
 STRIDE = 8
 CODE_STEP = (1, STRIDE - 1, STRIDE, STRIDE + 1)
@@ -45,21 +46,24 @@
             part = part * factor
         self.parts[at] = self.parts[at] + part if at in self.parts else part
 
-    def block(self, r, c):
+    def block(self, r, c, codes=(0, 1, 2, 3), local=True):
         size, cols = self.size, self.cols
         at = r * STRIDE + c + 1
         down = jnp.broadcast_to(self.columns[:, at : at + 1], (size, size))
-        tile = jnp.where(self.eye, 0.0, self.selfs[r * cols + c])
-        acc = tile * self.p_ref[at : at + 1, :]
-        self.fold(tile * down, at)
-        for code, distance in enumerate(CODE_STEP):
+        acc = None
+        if local:
+            tile = jnp.where(self.eye, 0.0, self.selfs[r * cols + c])
+            acc = tile * self.p_ref[at : at + 1, :]
+            self.fold(tile * down, at)
+        for code in codes:
             slot = (r * cols + c) * len(CODE_STEP) + code
             live = self.mask[slot : slot + 1, :]
-            j = at + distance
+            j = at + CODE_STEP[code]
             tile = self.edges[slot]
-            acc += tile * (self.p_ref[j : j + 1, :] * live)
+            product = tile * (self.p_ref[j : j + 1, :] * live)
+            acc = product if acc is None else acc + product
             self.fold(tile * down, j, live)
-        if r == self.rows - 1:
+        if local and r == self.rows - 1:
             tile = self.ghosts[c]
             base = self.rows * cols * len(CODE_STEP) + c * cols
             field = jnp.zeros((1, size), f32)
@@ -67,11 +71,21 @@
                 j = r * STRIDE + 1 + o
                 field += self.p_ref[j : j + 1, :] * self.mask[base + o : base + o + 1, :]
             acc += tile * field
-            part = jnp.sum((tile * down).reshape(size // 8, 8, size), axis=0)
+            product = tile * down
             for o in range(cols):
-                j = r * STRIDE + 1 + o
-                self.parts[j] += part * self.mask[base + o : base + o + 1, :]
+                self.fold(product, r * STRIDE + 1 + o, self.mask[base + o : base + o + 1, :])
         self.sums = jnp.where(self.lane == at, jnp.sum(acc, axis=1, keepdims=True), self.sums)
+
+    def early(self):
+        for r in range(1, self.rows):
+            for c in range(self.cols):
+                self.block(r, c, (0, 1, 2, 3) if r < self.rows - 1 else (0,))
+
+    def late(self):
+        for c in range(self.cols):
+            self.block(0, c)
+        for c in range(self.cols):
+            self.block(self.rows - 1, c, (1, 2, 3), False)
 
     def store(self, v_ref):
         v_ref[...] += jnp.transpose(self.sums)[: v_ref.shape[0], :]
@@ -191,8 +205,21 @@
     out[rows * STRIDE :, :] += jnp.where(even, first[:STRIDE, :], second[:STRIDE, :])
 
 
+def early_kernel(rows, cols, sign, mask, selfs, edges, ghosts, top, bottom, v_out, p_ref):
+    inside, _ = inside_grid(rows, cols, v_out.shape)
+    at = lax.broadcasted_iota(jnp.int32, v_out.shape, 0)
+    known = inside & (at >= STRIDE) & (at < rows * STRIDE)
+    field = jnp.where(known, top[...] / jnp.where(known, sign * bottom[...], 1.0), 0.0)
+    p_ref[...] = jnp.zeros_like(p_ref)
+    p_ref[: field.shape[0], :] = field
+    v_out[...] = jnp.zeros_like(v_out)
+    tiles = Tiles(rows, cols, p_ref, mask, selfs, edges, ghosts)
+    tiles.early()
+    tiles.store(v_out)
+
+
 def second_kernel(
-    rows, cols, mask, selfs, edges, ghosts, total, src, rim1, rim2,
+    rows, cols, mask, selfs, edges, ghosts, early, total, src, rim1, rim2,
     v_out, s_out, jac_out, side1, side2, p_ref,
 ):
     inside, _ = inside_grid(rows, cols, v_out.shape)
@@ -207,11 +234,9 @@
     p_ref[: s.shape[0], :] = s
     s_out[...] = s
     jac_out[...] = jac
-    v_out[...] = jnp.zeros_like(v_out)
+    v_out[...] = early[...]
     tiles = Tiles(rows, cols, p_ref, mask, selfs, edges, ghosts)
-    for r in range(rows):
-        for c in range(cols):
-            tiles.block(r, c)
+    tiles.late()
     tiles.store(v_out)
     for side in (side1, side2):
         side[...] = jnp.zeros_like(side)
@@ -219,7 +244,7 @@
 
 
 def third_kernel(
-    rows, cols, mask, selfs, edges, ghosts, total, src, s_ref, jac, rim1, rim2,
+    rows, cols, mask, selfs, edges, ghosts, early, total, src, s_ref, jac, rim1, rim2,
     v_out, w_out, side1, side2, sums_out, p_ref,
 ):
     size = p_ref.shape[1]
@@ -230,11 +255,9 @@
     p_ref[...] = jnp.zeros_like(p_ref)
     p_ref[: w.shape[0], :] = w
     w_out[...] = w
-    v_out[...] = jnp.zeros_like(v_out)
+    v_out[...] = early[...]
     tiles = Tiles(rows, cols, p_ref, mask, selfs, edges, ghosts)
-    for r in range(rows):
-        for c in range(cols):
-            tiles.block(r, c)
+    tiles.late()
     tiles.store(v_out)
     for side in (side1, side2):
         side[...] = jnp.zeros_like(side)
@@ -360,7 +383,9 @@
         )(*operands)
 
     def exchange(v, first, second, src=None):
-        operands = [v, swap(first, False, "cross"), swap(second, True, "cross")]
+        first = swap(first, False, "cross")
+        second = swap(second, True, "cross")
+        operands = [v, first, second]
         shapes = [region, line, line]
         if src is not None:
             operands.append(src)
@@ -368,7 +393,13 @@
         total, first, second, *rest = call(
             merge_kernel, shapes, [VMEM] * len(operands), operands, extra=(src is not None,)
         )
-        return [total, *rest, swap(first, False, "slab"), swap(second, True, "slab")]
+        first = swap(first, False, "slab")
+        second = swap(second, True, "slab")
+        return [total, *rest, first, second]
+
+    def early(top, bottom, sign):
+        operands = matrix + [top, bottom]
+        return call(early_kernel, [region], [VMEM] * len(operands), operands, [field], (sign,))[0]
 
     field = pltpu.VMEM((size, size), f32)
     small = [
@@ -399,14 +430,16 @@
         limit=10,
     )
     total, src, rim1, rim2 = exchange(v, first, second, src)
-
-    operands = matrix + [total, src, rim1, rim2]
+    part = early(src, total, -1.0)
+
+    operands = matrix + [part, total, src, rim1, rim2]
     v, s, jac, first, second = call(
         second_kernel, [region] * 3 + [side] * 2, [VMEM] * len(operands), operands, [field]
     )
     total, rim1, rim2 = exchange(v, first, second)
-
-    operands = matrix + [total, src, s, jac, rim1, rim2]
+    part = early(total, jac, 1.0)
+
+    operands = matrix + [part, total, src, s, jac, rim1, rim2]
     v, w, first, second, sums = call(
         third_kernel,
         [region] * 2 + [side] * 2 + [(peers, size)],

time: 58.1 us -> 57 us (0.981)
  waiting for transfers between devices: 12.1 us -> 9.99 us
  Pallas kernels: 8.13 us -> 9.05 us
    ppermute x12, waiting for transfers between devices: 10.3 us -> 8.23 us  [swap(): return lax.ppermute(value, ('slab', 'cross'), pairs)]
    pallas_call x6 -> x8, Pallas kernels: 7.15 us -> 8.07 us  [call(): pl.pallas_call(functools.partial(kernel, rows, cols, *extra), out_shape=[...]
  transfers between devices with their start and end apart: 13 -> 13, of which waited for: 8 -> 7; matrix products, arithmetic and copies ran while one was open for 0% -> 0% of each run, Pallas kernels for 0% -> 4%
where the time goes in v5:
time: 57 us; the launch traced here: 56.8 us
  starting transfers between devices  37 us (65%)
  waiting for transfers between devices  9.99 us (18%)
  Pallas kernels  9.05 us (16%)
  between operations  0.7 us (1%)
    ppermute x12, starting transfers between devices, swap(): return lax.ppermute(value, ('slab', 'cross'), pairs)  23.4 us
    all_to_all x1, starting transfers between devices, per_device(): gathered = lax.all_to_all(sums, ('slab', 'cross'), 0, 0, tiled=True)  13.7 us
    ppermute x12, waiting for transfers between devices, swap(): return lax.ppermute(value, ('slab', 'cross'), pairs)  8.23 us
    pallas_call x8, Pallas kernels, call(): pl.pallas_call(functools.partial(kernel, rows, cols, *extra), out_shape=[...  8.07 us
    all_to_all x1, waiting for transfers between devices, per_device(): gathered = lax.all_to_all(sums, ('slab', 'cross'), 0, 0, tiled=True)  1.77 us
  transfers between devices with their start and end apart: 13, of which 7 were waited for; matrix products, arithmetic and copies ran while one was open for 0% of the time, Pallas kernels for 4%

profile of v5, /device:TPU:1, one launch (start us, length us, event | category | flops | bytes accessed | tf_op | source)
XLA Modules:
  0.0 56.8 jit_solution(7471252929994689109)
XLA Ops:
  0.6 3.7 %shard_map.131 = (f32[40,128]{1,0:T(8,128)S(1)}, f32[40,128]{1,0:T(8,128)S(1)}, f32[16,128]{1,0:T(8,128)S(1)}, f32[16,128]{1,0:T(8,128)S(1)}, f32[80,128]{1,0:T(...) custom-call(s32[4,4]{1,0:T(4,128)} %refs_0_.1, ...), custom_call_target="tpu_custom_call" | custom-call | tf_op jit(solution)/shard_map/pallas_call | solution.py:376
  4.3 2.5 %collective-permute-start = (f32[16,128]{1,0:T(8,128)S(1)}, f32[16,128]{1,0:T(8,128)S(1)}, u32[]{:S(2)}, u32[]{:S(2)}) collective-permute-start(f32[16,128]{1,0:T(8,128)S(1)} %get-tuple-element.35), channel_id=1, source_target_pairs={{0,1},{1,0},{2,3},{3,2},{4,5},{5,4},{6,7},{7,6},{8,9},{9,8},{10,11... | collective-permute-start | bytes 24584 | tf_op jit(solution)/shard_map/ppermute | solution.py:351
  6.8 4.7 %collective-permute-start.1 = (f32[16,128]{1,0:T(8,128)S(1)}, f32[16,128]{1,0:T(8,128)S(1)}, u32[]{:S(2)}, u32[]{:S(2)}) collective-permute-start(f32[16,128]{1,0:T(8,128)S(1)} %get-tuple-element.36), channel_id=1, source_target_pairs={{0,7},{1,2},{2,1},{3,4},{4,3},{5,6},{6,5},{7,0},{8,15},{9,10},{10,... | collective-permute-start | bytes 24584 | tf_op jit(solution)/shard_map/ppermute | solution.py:351
  11.5 0.0 collective-permute-done.refs_1_
  11.5 1.0 %collective-permute-done.1.refs_2_ = f32[16,128]{1,0:T(8,128)S(1)} collective-permute-done((f32[16,128]{1,0:T(8,128)S(1)}, f32[16,128]{1,0:T(8,128)S(1)}, u32[]{:S(2)}, u32[]{:S(2)}) %collective-permute-start.1) | collective-permute-done | bytes 8224 | tf_op jit(solution)/shard_map/ppermute | solution.py:351
  12.6 1.9 %collective-permute-start.2 = (f32[16,128]{1,0:T(8,128)S(1)}, f32[16,128]{1,0:T(8,128)S(1)}, u32[]{:S(2)}, u32[]{:S(2)}) collective-permute-start(f32[16,128]{1,0:T(8,128)S(1)} %get-tuple-element.40), channel_id=1, source_target_pairs={{0,8},{1,9},{2,10},{3,11},{4,12},{5,13},{6,14},{7,15},{8,0},{9,1},... | collective-permute-start | bytes 24584 | tf_op jit(solution)/shard_map/ppermute | solution.py:351
  14.5 1.3 %collective-permute-start.3 = (f32[16,128]{1,0:T(8,128)S(1)}, f32[16,128]{1,0:T(8,128)S(1)}, u32[]{:S(2)}, u32[]{:S(2)}) collective-permute-start(f32[16,128]{1,0:T(8,128)S(1)} %get-tuple-element.41), channel_id=1, source_target_pairs={{0,1},{1,0},{2,3},{3,2},{4,5},{5,4},{6,7},{7,6},{8,16},{9,17},{10,... | collective-permute-start | bytes 24584 | tf_op jit(solution)/shard_map/ppermute | solution.py:351
  15.8 1.0 %shard_map.133.early = f32[40,128]{1,0:T(8,128)S(1)} custom-call(f32[80,128]{1,0:T(8,128)S(1)} %get-tuple-element.30.mask, f32[16,128,128]{2,1,0:T(8,128)S(1)} %get-tuple-element.31.selfs, f32[64,128,128]{2,1,0:T(8,128)S(1)} %get-tuple-element.32.edges, f32[4,128,128]{2,1,0:T(8,128)S(1)} %get-tuple-element.33.ghosts, ...), custom_call_target="tpu_custom_call" | custom-call | tf_op jit(solution)/shard_map/pallas_call | solution.py:376
  16.8 0.0 collective-permute-done.2.rim1
  16.8 1.0 %collective-permute-done.3.rim2 = f32[16,128]{1,0:T(8,128)S(1)} collective-permute-done((f32[16,128]{1,0:T(8,128)S(1)}, f32[16,128]{1,0:T(8,128)S(1)}, u32[]{:S(2)}, u32[]{:S(2)}) %collective-permute-start.3) | collective-permute-done | bytes 8224 | tf_op jit(solution)/shard_map/ppermute | solution.py:351
  17.8 0.8 %shard_map.134 = (f32[40,128]{1,0:T(8,128)S(1)}, f32[40,128]{1,0:T(8,128)S(1)}, f32[40,128]{1,0:T(8,128)S(1)}, f32[16,128]{1,0:T(8,128)S(1)}, f32[16,128]{1,0:T(8,128)S(1)}) custom-call(f32[80,128]{1,0:T(8,128)S(1)} %get-tuple-element.30.mask, f32[16,128,128]{2,1,0:T(8,128)S(1)} %get-tuple-element.31.selfs, f32[64,128,128]{2,1,0:T(8,128)S(1)} %get-tuple-element.32.edges, ...), custom_call_target="tpu_custom_call" | custom-call | tf_op jit(solution)/shard_map/pallas_call | solution.py:376
  18.6 0.1 collective-permute-start.4
  18.7 3.0 %collective-permute-start.5 = (f32[16,128]{1,0:T(8,128)S(1)}, f32[16,128]{1,0:T(8,128)S(1)}, u32[]{:S(2)}, u32[]{:S(2)}) collective-permute-start(f32[16,128]{1,0:T(8,128)S(1)} %get-tuple-element.44), channel_id=1, source_target_pairs={{0,7},{1,2},{2,1},{3,4},{4,3},{5,6},{6,5},{7,0},{8,15},{9,10},{10,... | collective-permute-start | bytes 24584 | tf_op jit(solution)/shard_map/ppermute | solution.py:351
  21.8 0.0 collective-permute-done.4.refs_1_
  21.8 1.0 %collective-permute-done.5.refs_2_ = f32[16,128]{1,0:T(8,128)S(1)} collective-permute-done((f32[16,128]{1,0:T(8,128)S(1)}, f32[16,128]{1,0:T(8,128)S(1)}, u32[]{:S(2)}, u32[]{:S(2)}) %collective-permute-start.5) | collective-permute-done | bytes 8224 | tf_op jit(solution)/shard_map/ppermute | solution.py:351
  22.8 1.4 %collective-permute-start.6 = (f32[8,128]{1,0:T(8,128)S(1)}, f32[8,128]{1,0:T(8,128)S(1)}, u32[]{:S(2)}, u32[]{:S(2)}) collective-permute-start(f32[8,128]{1,0:T(8,128)S(1)} %get-tuple-element.48), channel_id=1, source_target_pairs={{0,8},{1,9},{2,10},{3,11},{4,12},{5,13},{6,14},{7,15},{8,0},{9,1},... | collective-permute-start | bytes 12296 | tf_op jit(solution)/shard_map/ppermute | solution.py:351
  24.2 0.7 %collective-permute-start.7 = (f32[8,128]{1,0:T(8,128)S(1)}, f32[8,128]{1,0:T(8,128)S(1)}, u32[]{:S(2)}, u32[]{:S(2)}) collective-permute-start(f32[8,128]{1,0:T(8,128)S(1)} %get-tuple-element.49), channel_id=1, source_target_pairs={{0,1},{1,0},{2,3},{3,2},{4,5},{5,4},{6,7},{7,6},{8,16},{9,17},{10,... | collective-permute-start | bytes 12296 | tf_op jit(solution)/shard_map/ppermute | solution.py:351
  24.9 1.0 %shard_map.136.early = f32[40,128]{1,0:T(8,128)S(1)} custom-call(f32[80,128]{1,0:T(8,128)S(1)} %get-tuple-element.30.mask, f32[16,128,128]{2,1,0:T(8,128)S(1)} %get-tuple-element.31.selfs, f32[64,128,128]{2,1,0:T(8,128)S(1)} %get-tuple-element.32.edges, f32[4,128,128]{2,1,0:T(8,128)S(1)} %get-tuple-element.33.ghosts, ...), custom_call_target="tpu_custom_call" | custom-call | tf_op jit(solution)/shard_map/pallas_call | solution.py:376
  25.9 0.0 collective-permute-done.6.rim1
  25.9 1.6 %collective-permute-done.7.rim2 = f32[8,128]{1,0:T(8,128)S(1)} collective-permute-done((f32[8,128]{1,0:T(8,128)S(1)}, f32[8,128]{1,0:T(8,128)S(1)}, u32[]{:S(2)}, u32[]{:S(2)}) %collective-permute-start.7) | collective-permute-done | bytes 4128 | tf_op jit(solution)/shard_map/ppermute | solution.py:351
  27.5 1.5 %shard_map.137 = (f32[40,128]{1,0:T(8,128)S(1)}, f32[40,128]{1,0:T(8,128)S(1)}, f32[16,128]{1,0:T(8,128)S(1)}, f32[16,128]{1,0:T(8,128)S(1)}, f32[256,128]{1,0:T(8,128)}) custom-call(f32[80,128]{1,0:T(8,128)S(1)} %get-tuple-element.30.mask, f32[16,128,128]{2,1,0:T(8,128)S(1)} %get-tuple-element.31.selfs, f32[64,128,128]{2,1,0:T(8,128)S(1)} %get-tuple-element.32.edges, ...), custom_call_target="tpu_custom_call" | custom-call | tf_op jit(solution)/shard_map/pallas_call | solution.py:376
  29.0 13.7 %all-to-all-start = ((f32[256,1,128]{2,1,0:T(1,128)}), f32[256,1,128]{2,1,0:T(1,128)S(1)}, u32[]{:S(2)}, u32[]{:S(2)}) async-start(f32[256,1,128]{2,1,0:T(1,128)} %bitcast.3), calls=%async_computation | async-start | bytes 262144 | tf_op jit(solution)/shard_map/all_to_all | solution.py:448
  42.7 1.6 %collective-permute-start.8 = (f32[16,128]{1,0:T(8,128)S(1)}, f32[16,128]{1,0:T(8,128)S(1)}, u32[]{:S(2)}, u32[]{:S(2)}) collective-permute-start(f32[16,128]{1,0:T(8,128)S(1)} %get-tuple-element.52), channel_id=1, source_target_pairs={{0,1},{1,0},{2,3},{3,2},{4,5},{5,4},{6,7},{7,6},{8,9},{9,8},{10,11... | collective-permute-start | bytes 24584 | tf_op jit(solution)/shard_map/ppermute | solution.py:351
  44.3 3.7 %collective-permute-start.9 = (f32[16,128]{1,0:T(8,128)S(1)}, f32[16,128]{1,0:T(8,128)S(1)}, u32[]{:S(2)}, u32[]{:S(2)}) collective-permute-start(f32[16,128]{1,0:T(8,128)S(1)} %get-tuple-element.53), channel_id=1, source_target_pairs={{0,7},{1,2},{2,1},{3,4},{4,3},{5,6},{6,5},{7,0},{8,15},{9,10},{10,... | collective-permute-start | bytes 24584 | tf_op jit(solution)/shard_map/ppermute | solution.py:351
  48.0 0.0 collective-permute-done.8.refs_1_
  48.0 1.5 %collective-permute-done.9.refs_2_ = f32[16,128]{1,0:T(8,128)S(1)} collective-permute-done((f32[16,128]{1,0:T(8,128)S(1)}, f32[16,128]{1,0:T(8,128)S(1)}, u32[]{:S(2)}, u32[]{:S(2)}) %collective-permute-start.9) | collective-permute-done | bytes 8224 | tf_op jit(solution)/shard_map/ppermute | solution.py:351
  49.5 1.2 %collective-permute-start.10 = (f32[8,128]{1,0:T(8,128)S(1)}, f32[8,128]{1,0:T(8,128)S(1)}, u32[]{:S(2)}, u32[]{:S(2)}) collective-permute-start(f32[8,128]{1,0:T(8,128)S(1)} %get-tuple-element.55), channel_id=1, source_target_pairs={{0,8},{1,9},{2,10},{3,11},{4,12},{5,13},{6,14},{7,15},{8,0},{9,1},... | collective-permute-start | bytes 12296 | tf_op jit(solution)/shard_map/ppermute | solution.py:351
  50.7 1.2 %collective-permute-start.11 = (f32[8,128]{1,0:T(8,128)S(1)}, f32[8,128]{1,0:T(8,128)S(1)}, u32[]{:S(2)}, u32[]{:S(2)}) collective-permute-start(f32[8,128]{1,0:T(8,128)S(1)} %get-tuple-element.56), channel_id=1, source_target_pairs={{0,1},{1,0},{2,3},{3,2},{4,5},{5,4},{6,7},{7,6},{8,16},{9,17},{10,... | collective-permute-start | bytes 12296 | tf_op jit(solution)/shard_map/ppermute | solution.py:351
  52.0 0.0 collective-permute-done.10.rim1
  52.0 2.1 %collective-permute-done.11.rim2 = f32[8,128]{1,0:T(8,128)S(1)} collective-permute-done((f32[8,128]{1,0:T(8,128)S(1)}, f32[8,128]{1,0:T(8,128)S(1)}, u32[]{:S(2)}, u32[]{:S(2)}) %collective-permute-start.11) | collective-permute-done | bytes 4128 | tf_op jit(solution)/shard_map/ppermute | solution.py:351
  54.0 1.8 %all-to-all-done = f32[256,1,128]{2,1,0:T(1,128)S(1)} async-done(((f32[256,1,128]{2,1,0:T(1,128)}), f32[256,1,128]{2,1,0:T(1,128)S(1)}, u32[]{:S(2)}, u32[]{:S(2)}) %all-to-all-start) | async-done | bytes 131104 | tf_op jit(solution)/shard_map/all_to_all | solution.py:448
  55.8 1.0 %shard_map.139 = (f32[4,4,128]{2,1,0:T(4,128)}, f32[4,4,128]{2,1,0:T(4,128)}) custom-call(f32[256,128]{1,0:T(8,128)S(1)} %bitcast.6, f32[40,128]{1,0:T(8,128)S(1)} %get-tuple-element.54.total, f32[8,128]{1,0:T(8,128)S(1)} %collective-permute-done.10.rim1, f32[8,128]{1,0:T(8,128)S(1)} %collective-permute-done.11.rim2, f32[40,128]{1,0:T(8,128)S(1)} %get-tuple-element.47.s_ref, ...), custom_call_target="tpu_custom_call" | custom-call | tf_op jit(solution)/shard_map/pallas_call | solution.py:452
  (3 shorter events, 0.1 us)
Async XLA Ops:
  4.3 7.2 %collective-permute-start = (f32[16,128]{1,0:T(8,128)S(1)}, f32[16,128]{1,0:T(8,128)S(1)}, u32[]{:S(2)}, u32[]{:S(2)}) collective-permute-start(f32[16,128]{1,0:T(8,128)S(1)} %get-tuple-element.35), channel_id=1, source_target_pairs={{0,1},{1,0},{2,3},{3,2},{4,5},{5,4},{6,7},{7,6},{8,9},{9,8},{10,11... | collective-permute-start | bytes 24584 | tf_op jit(solution)/shard_map/ppermute | solution.py:351
  6.8 5.7 %collective-permute-start.1 = (f32[16,128]{1,0:T(8,128)S(1)}, f32[16,128]{1,0:T(8,128)S(1)}, u32[]{:S(2)}, u32[]{:S(2)}) collective-permute-start(f32[16,128]{1,0:T(8,128)S(1)} %get-tuple-element.36), channel_id=1, source_target_pairs={{0,7},{1,2},{2,1},{3,4},{4,3},{5,6},{6,5},{7,0},{8,15},{9,10},{10,... | collective-permute-start | bytes 24584 | tf_op jit(solution)/shard_map/ppermute | solution.py:351
  12.6 4.2 %collective-permute-start.2 = (f32[16,128]{1,0:T(8,128)S(1)}, f32[16,128]{1,0:T(8,128)S(1)}, u32[]{:S(2)}, u32[]{:S(2)}) collective-permute-start(f32[16,128]{1,0:T(8,128)S(1)} %get-tuple-element.40), channel_id=1, source_target_pairs={{0,8},{1,9},{2,10},{3,11},{4,12},{5,13},{6,14},{7,15},{8,0},{9,1},... | collective-permute-start | bytes 24584 | tf_op jit(solution)/shard_map/ppermute | solution.py:351
  14.5 3.4 %collective-permute-start.3 = (f32[16,128]{1,0:T(8,128)S(1)}, f32[16,128]{1,0:T(8,128)S(1)}, u32[]{:S(2)}, u32[]{:S(2)}) collective-permute-start(f32[16,128]{1,0:T(8,128)S(1)} %get-tuple-element.41), channel_id=1, source_target_pairs={{0,1},{1,0},{2,3},{3,2},{4,5},{5,4},{6,7},{7,6},{8,16},{9,17},{10,... | collective-permute-start | bytes 24584 | tf_op jit(solution)/shard_map/ppermute | solution.py:351
  18.6 3.1 %collective-permute-start.4 = (f32[16,128]{1,0:T(8,128)S(1)}, f32[16,128]{1,0:T(8,128)S(1)}, u32[]{:S(2)}, u32[]{:S(2)}) collective-permute-start(f32[16,128]{1,0:T(8,128)S(1)} %get-tuple-element.43), channel_id=1, source_target_pairs={{0,1},{1,0},{2,3},{3,2},{4,5},{5,4},{6,7},{7,6},{8,9},{9,8},{10,11... | collective-permute-start | bytes 24584 | tf_op jit(solution)/shard_map/ppermute | solution.py:351
  18.7 4.1 %collective-permute-start.5 = (f32[16,128]{1,0:T(8,128)S(1)}, f32[16,128]{1,0:T(8,128)S(1)}, u32[]{:S(2)}, u32[]{:S(2)}) collective-permute-start(f32[16,128]{1,0:T(8,128)S(1)} %get-tuple-element.44), channel_id=1, source_target_pairs={{0,7},{1,2},{2,1},{3,4},{4,3},{5,6},{6,5},{7,0},{8,15},{9,10},{10,... | collective-permute-start | bytes 24584 | tf_op jit(solution)/shard_map/ppermute | solution.py:351
  22.8 3.1 %collective-permute-start.6 = (f32[8,128]{1,0:T(8,128)S(1)}, f32[8,128]{1,0:T(8,128)S(1)}, u32[]{:S(2)}, u32[]{:S(2)}) collective-permute-start(f32[8,128]{1,0:T(8,128)S(1)} %get-tuple-element.48), channel_id=1, source_target_pairs={{0,8},{1,9},{2,10},{3,11},{4,12},{5,13},{6,14},{7,15},{8,0},{9,1},... | collective-permute-start | bytes 12296 | tf_op jit(solution)/shard_map/ppermute | solution.py:351
  24.2 3.3 %collective-permute-start.7 = (f32[8,128]{1,0:T(8,128)S(1)}, f32[8,128]{1,0:T(8,128)S(1)}, u32[]{:S(2)}, u32[]{:S(2)}) collective-permute-start(f32[8,128]{1,0:T(8,128)S(1)} %get-tuple-element.49), channel_id=1, source_target_pairs={{0,1},{1,0},{2,3},{3,2},{4,5},{5,4},{6,7},{7,6},{8,16},{9,17},{10,... | collective-permute-start | bytes 12296 | tf_op jit(solution)/shard_map/ppermute | solution.py:351
  29.0 26.8 %all-to-all-start = ((f32[256,1,128]{2,1,0:T(1,128)}), f32[256,1,128]{2,1,0:T(1,128)S(1)}, u32[]{:S(2)}, u32[]{:S(2)}) async-start(f32[256,1,128]{2,1,0:T(1,128)} %bitcast.3), calls=%async_computation | async-start | bytes 262144 | tf_op jit(solution)/shard_map/all_to_all | solution.py:448
  42.7 5.3 %collective-permute-start.8 = (f32[16,128]{1,0:T(8,128)S(1)}, f32[16,128]{1,0:T(8,128)S(1)}, u32[]{:S(2)}, u32[]{:S(2)}) collective-permute-start(f32[16,128]{1,0:T(8,128)S(1)} %get-tuple-element.52), channel_id=1, source_target_pairs={{0,1},{1,0},{2,3},{3,2},{4,5},{5,4},{6,7},{7,6},{8,9},{9,8},{10,11... | collective-permute-start | bytes 24584 | tf_op jit(solution)/shard_map/ppermute | solution.py:351
  44.3 5.2 %collective-permute-start.9 = (f32[16,128]{1,0:T(8,128)S(1)}, f32[16,128]{1,0:T(8,128)S(1)}, u32[]{:S(2)}, u32[]{:S(2)}) collective-permute-start(f32[16,128]{1,0:T(8,128)S(1)} %get-tuple-element.53), channel_id=1, source_target_pairs={{0,7},{1,2},{2,1},{3,4},{4,3},{5,6},{6,5},{7,0},{8,15},{9,10},{10,... | collective-permute-start | bytes 24584 | tf_op jit(solution)/shard_map/ppermute | solution.py:351
  49.5 2.5 %collective-permute-start.10 = (f32[8,128]{1,0:T(8,128)S(1)}, f32[8,128]{1,0:T(8,128)S(1)}, u32[]{:S(2)}, u32[]{:S(2)}) collective-permute-start(f32[8,128]{1,0:T(8,128)S(1)} %get-tuple-element.55), channel_id=1, source_target_pairs={{0,8},{1,9},{2,10},{3,11},{4,12},{5,13},{6,14},{7,15},{8,0},{9,1},... | collective-permute-start | bytes 12296 | tf_op jit(solution)/shard_map/ppermute | solution.py:351
  50.7 3.3 %collective-permute-start.11 = (f32[8,128]{1,0:T(8,128)S(1)}, f32[8,128]{1,0:T(8,128)S(1)}, u32[]{:S(2)}, u32[]{:S(2)}) collective-permute-start(f32[8,128]{1,0:T(8,128)S(1)} %get-tuple-element.56), channel_id=1, source_target_pairs={{0,1},{1,0},{2,3},{3,2},{4,5},{5,4},{6,7},{7,6},{8,16},{9,17},{10,... | collective-permute-start | bytes 12296 | tf_op jit(solution)/shard_map/ppermute | solution.py:351

commit v6 on v5

--- a/solution.py
+++ b/solution.py
@@ -12,6 +12,7 @@
 CODE_STEP = (1, STRIDE - 1, STRIDE, STRIDE + 1)
 
 VMEM = pl.BlockSpec(memory_space=pltpu.VMEM)
+SMEM = pl.BlockSpec(memory_space=pltpu.SMEM)
 HBM = pl.BlockSpec(memory_space=pltpu.HBM)
 f32 = jnp.float32
 
@@ -35,7 +36,6 @@
         self.size = p_ref.shape[1]
         full = (self.size, self.size)
         self.lane = lax.broadcasted_iota(jnp.int32, full, 1)
-        self.eye = self.lane == lax.broadcasted_iota(jnp.int32, full, 0)
         self.columns = jnp.transpose(p_ref[...])
         self.sums = jnp.zeros(full, f32)
         self.parts = {}
@@ -52,7 +52,7 @@
         down = jnp.broadcast_to(self.columns[:, at : at + 1], (size, size))
         acc = None
         if local:
-            tile = jnp.where(self.eye, 0.0, self.selfs[r * cols + c])
+            tile = self.selfs[r * cols + c]
             acc = tile * self.p_ref[at : at + 1, :]
             self.fold(tile * down, at)
         for code in codes:
@@ -108,10 +108,10 @@
 
 def first_kernel(rows, cols, *refs):
     inputs, refs = refs[:12], refs[12:]
-    (v_out, src_out, first, second, mask, selfs, edges, ghosts), refs = refs[:8], refs[8:]
-    staged, (p_ref, small_sem, self_sem, edge_sem) = refs[:10], refs[10:]
+    (v_out, src_out, first, second, self_in, edge_in, ghosts), refs = refs[:7], refs[7:]
+    staged, (small_sem, self_sem, edge_sem) = refs[:10], refs[10:]
     self_hbm, edge_hbm = inputs[10:]
-    size = p_ref.shape[1]
+    size = v_out.shape[1]
     slots = len(CODE_STEP)
     small = [
         pltpu.make_async_copy(hbm, here, small_sem.at[k])
@@ -121,35 +121,13 @@
         copy.start()
     for r in range(rows):
         part = pl.ds(r * cols, cols)
-        pltpu.make_async_copy(self_hbm.at[part], selfs.at[part], self_sem.at[r]).start()
+        pltpu.make_async_copy(self_hbm.at[part], self_in.at[part], self_sem.at[r]).start()
+    for r in range(rows):
+        part = pl.ds(r * cols * slots, cols * slots)
+        pltpu.make_async_copy(edge_hbm.at[part], edge_in.at[part], edge_sem.at[r]).start()
     count, offset, owner, mirror, gain, vel, acc, grad, dens, weight = staged
-    for copy in small[:3]:
+    for copy in small:
         copy.wait()
-    for r in range(rows):
-        for c in range(cols):
-            for k in range(slots):
-                slot = (r * cols + c) * slots + k
-                place = (r * cols + c) * slots + offset[r, c, k]
-                pltpu.make_async_copy(
-                    edge_hbm.at[slot], edges.at[place], edge_sem.at[r]
-                ).start()
-    for r in range(rows):
-        for c in range(cols):
-            for k in range(slots):
-                place = (r * cols + c) * slots + offset[r, c, k]
-                live = jnp.where(k < count[r, c], 1.0, 0.0)
-                mask[pl.ds(place, 1), :] = jnp.full((1, size), live, f32)
-    base = rows * cols * slots
-    for c in range(cols):
-        for o in range(cols):
-            same = jnp.where(owner[c] == o, 1.0, 0.0)
-            mask[base + c * cols + o : base + c * cols + o + 1, :] = jnp.full((1, size), same, f32)
-    for copy in small[3:]:
-        copy.wait()
-
-    inside, _ = inside_grid(rows, cols, v_out.shape)
-    p_ref[...] = jnp.zeros_like(p_ref)
-    p_ref[: v_out.shape[0], :] = jnp.where(inside, 1.0, 0.0)
     v_out[...] = jnp.zeros_like(v_out)
     src_out[...] = jnp.zeros_like(src_out)
     even = on_even("cross")
@@ -176,24 +154,74 @@
         jnp.concatenate([gain[...] * jnp.where(on_wall, -1.0, 0.0), pad], axis=0)
     )
     lane = lax.broadcasted_iota(jnp.int32, (size, size), 1)
-    sub = lax.broadcasted_iota(jnp.int32, (size, size), 0)
+    eye = lane == lax.broadcasted_iota(jnp.int32, (size, size), 0)
     lanef = lane.astype(f32)
     for c in range(cols):
         hit = lanef == mirrors[:, c : c + 1]
         tile = jnp.where(hit, gains[:, c : c + 1], 0.0)
         other = jnp.where(owner[c] == c, 0.0, 1.0)
-        ghosts[c] = jnp.where(lane == sub, tile * other, tile)
-
-    tiles = Tiles(rows, cols, p_ref, mask, selfs, edges, ghosts)
+        ghosts[c] = jnp.where(eye, tile * other, tile)
+
+    has_south = lax.axis_index("slab") < lax.axis_size("slab") - 1
+    has_west = lax.axis_index("cross") > 0
+    has_east = lax.axis_index("cross") < lax.axis_size("cross") - 1
+    sums = jnp.zeros((size, size), f32)
     for r in range(rows):
         part = pl.ds(r * cols, cols)
-        pltpu.make_async_copy(self_hbm.at[part], selfs.at[part], self_sem.at[r]).wait()
+        pltpu.make_async_copy(self_hbm.at[part], self_in.at[part], self_sem.at[r]).wait()
         part = pl.ds(r * cols * slots, cols * slots)
-        pltpu.make_async_copy(edge_hbm.at[part], edges.at[part], edge_sem.at[r]).wait()
+        pltpu.make_async_copy(edge_hbm.at[part], edge_in.at[part], edge_sem.at[r]).wait()
         for c in range(cols):
-            tiles.block(r, c)
-    tiles.store(v_out)
+            block = r * cols + c
+            at = r * STRIDE + c + 1
+            tile = jnp.where(eye, 0.0, self_in[block])
+            rowwise = tile
+            v_out[at : at + 1, :] += jnp.sum(tile, axis=0, keepdims=True)
+            for k in range(slots):
+                code = offset[r, c, k]
+                live = jnp.where(k < count[r, c], 1.0, 0.0)
+                there = jnp.asarray(True)
+                if c == 0:
+                    there = there & (has_west | (code != 1))
+                if c == cols - 1:
+                    there = there & (has_east | ((code != 0) & (code != 3)))
+                if r == rows - 1:
+                    there = there & (has_south | (code == 0))
+                tile = edge_in[block * slots + k]
+                rowwise += tile * jnp.where(there, live, 0.0)
+                step = jnp.where(code == 0, CODE_STEP[0], CODE_STEP[1] - 1 + code)
+                v_out[pl.ds(at + step, 1), :] += jnp.sum(tile, axis=0, keepdims=True) * live
+            if r == rows - 1:
+                tile = ghosts[c]
+                rowwise += tile
+                j = r * STRIDE + 1 + owner[c]
+                v_out[pl.ds(j, 1), :] += jnp.sum(tile, axis=0, keepdims=True)
+            sums = jnp.where(lane == at, jnp.sum(rowwise, axis=1, keepdims=True), sums)
+    v_out[...] += jnp.transpose(sums)[: v_out.shape[0], :]
     pack_sides(v_out, first, second, rows, cols)
+
+
+def place_kernel(
+    rows, cols, count, offset, owner, self_in, edge_in, mask, selfs, edges
+):
+    size = mask.shape[1]
+    slots = len(CODE_STEP)
+    lane = lax.broadcasted_iota(jnp.int32, (size, size), 1)
+    eye = lane == lax.broadcasted_iota(jnp.int32, (size, size), 0)
+    for r in range(rows):
+        for c in range(cols):
+            block = r * cols + c
+            selfs[block] = jnp.where(eye, 0.0, self_in[block])
+            for k in range(slots):
+                place = block * slots + offset[r, c, k]
+                live = jnp.where(k < count[r, c], 1.0, 0.0)
+                mask[pl.ds(place, 1), :] = jnp.full((1, size), live, f32)
+                edges[place] = edge_in[block * slots + k]
+    base = rows * cols * slots
+    for c in range(cols):
+        for o in range(cols):
+            same = jnp.where(owner[c] == o, 1.0, 0.0)
+            mask[base + c * cols + o : base + c * cols + o + 1, :] = jnp.full((1, size), same, f32)
 
 
 def add_rims(rows, total, first, second, out):
@@ -409,10 +437,10 @@
     staged = [
         (pltpu.SMEM if k < 3 else pltpu.VMEM)(x.shape, x.dtype) for k, x in enumerate(small)
     ]
-    v, src, first, second, *matrix = call(
+    v, src, first, second, self_in, edge_in, ghosts = call(
         first_kernel,
         [
-            region, region, side, side, (rows * cols * slots + cols * cols, size),
+            region, region, side, side,
             (rows * cols, size, size), (rows * cols * slots, size, size), (cols, size, size),
         ],
         [HBM] * 12,
@@ -424,11 +452,18 @@
                 edge_tiles.reshape(rows * cols * slots, size, size),
             ]
         ],
-        staged
-        + [field]
-        + [pltpu.SemaphoreType.DMA((n,)) for n in (len(small), rows, rows)],
+        staged + [pltpu.SemaphoreType.DMA((n,)) for n in (len(small), rows, rows)],
         limit=10,
     )
+    matrix = [*call(
+        place_kernel,
+        [
+            (rows * cols * slots + cols * cols, size),
+            (rows * cols, size, size), (rows * cols * slots, size, size),
+        ],
+        [SMEM] * 3 + [VMEM] * 2,
+        small[:3] + [self_in, edge_in],
+    ), ghosts]
     total, src, rim1, rim2 = exchange(v, first, second, src)
     part = early(src, total, -1.0)
 

time: 57 us -> 56.8 us (level)
  Pallas kernels: 9.05 us -> 10.1 us
  waiting for transfers between devices: 9.99 us -> 9.34 us
    pallas_call x8 -> x9, Pallas kernels: 8.07 us -> 9.12 us  [call(): pl.pallas_call(functools.partial(kernel, rows, cols, *extra), out_shape=[...]
    ppermute x12, waiting for transfers between devices: 8.23 us -> 7.6 us  [swap(): return lax.ppermute(value, ('slab', 'cross'), pairs)]
  transfers between devices with their start and end apart: 13 -> 13, of which waited for: 7 -> 6; matrix products, arithmetic and copies ran while one was open for 0% -> 0% of each run, Pallas kernels for 4% -> 6%
where the time goes in v6:
time: 56.8 us; the launch traced here: 56.7 us
  starting transfers between devices  36.5 us (64%)
  Pallas kernels  10.1 us (18%)
  waiting for transfers between devices  9.34 us (16%)
  between operations  0.74 us (1%)
    ppermute x12, starting transfers between devices, swap(): return lax.ppermute(value, ('slab', 'cross'), pairs)  23.3 us
    all_to_all x1, starting transfers between devices, per_device(): gathered = lax.all_to_all(sums, ('slab', 'cross'), 0, 0, tiled=True)  13.2 us
    pallas_call x9, Pallas kernels, call(): pl.pallas_call(functools.partial(kernel, rows, cols, *extra), out_shape=[...  9.12 us
    ppermute x12, waiting for transfers between devices, swap(): return lax.ppermute(value, ('slab', 'cross'), pairs)  7.6 us
    all_to_all x1, waiting for transfers between devices, per_device(): gathered = lax.all_to_all(sums, ('slab', 'cross'), 0, 0, tiled=True)  1.74 us
  transfers between devices with their start and end apart: 13, of which 6 were waited for; matrix products, arithmetic and copies ran while one was open for 0% of the time, Pallas kernels for 6%

profile of v6, /device:TPU:1, one launch (start us, length us, event | category | flops | bytes accessed | tf_op | source)
XLA Modules:
  0.0 56.7 jit_solution(7828520544445581708)
XLA Ops:
  0.7 3.5 %shard_map.131 = (f32[40,128]{1,0:T(8,128)S(1)}, f32[40,128]{1,0:T(8,128)S(1)}, f32[16,128]{1,0:T(8,128)S(1)}, f32[16,128]{1,0:T(8,128)S(1)}, f32[16,128,128]{2,...) custom-call(s32[4,4]{1,0:T(4,128)} %count.1, s32[4,4,4]{2,1,0:T(4,128)} %offset.1, s32[4]{0:T(128)} %owner.1, ...), custom_call_target="tpu_custom_call" | custom-call | tf_op jit(solution)/shard_map/pallas_call | solution.py:404
  4.2 2.5 %collective-permute-start = (f32[16,128]{1,0:T(8,128)S(1)}, f32[16,128]{1,0:T(8,128)S(1)}, u32[]{:S(2)}, u32[]{:S(2)}) collective-permute-start(f32[16,128]{1,0:T(8,128)S(1)} %get-tuple-element.39), channel_id=1, source_target_pairs={{0,1},{1,0},{2,3},{3,2},{4,5},{5,4},{6,7},{7,6},{8,9},{9,8},{10,11... | collective-permute-start | bytes 24584 | tf_op jit(solution)/shard_map/ppermute | solution.py:379
  6.7 4.7 %collective-permute-start.1 = (f32[16,128]{1,0:T(8,128)S(1)}, f32[16,128]{1,0:T(8,128)S(1)}, u32[]{:S(2)}, u32[]{:S(2)}) collective-permute-start(f32[16,128]{1,0:T(8,128)S(1)} %get-tuple-element.40), channel_id=1, source_target_pairs={{0,7},{1,2},{2,1},{3,4},{4,3},{5,6},{6,5},{7,0},{8,15},{9,10},{10,... | collective-permute-start | bytes 24584 | tf_op jit(solution)/shard_map/ppermute | solution.py:379
  11.4 0.0 collective-permute-done.refs_1_
  11.4 1.0 %collective-permute-done.1.refs_2_ = f32[16,128]{1,0:T(8,128)S(1)} collective-permute-done((f32[16,128]{1,0:T(8,128)S(1)}, f32[16,128]{1,0:T(8,128)S(1)}, u32[]{:S(2)}, u32[]{:S(2)}) %collective-permute-start.1) | collective-permute-done | bytes 8224 | tf_op jit(solution)/shard_map/ppermute | solution.py:379
  12.4 1.9 %collective-permute-start.2 = (f32[16,128]{1,0:T(8,128)S(1)}, f32[16,128]{1,0:T(8,128)S(1)}, u32[]{:S(2)}, u32[]{:S(2)}) collective-permute-start(f32[16,128]{1,0:T(8,128)S(1)} %get-tuple-element.44), channel_id=1, source_target_pairs={{0,8},{1,9},{2,10},{3,11},{4,12},{5,13},{6,14},{7,15},{8,0},{9,1},... | collective-permute-start | bytes 24584 | tf_op jit(solution)/shard_map/ppermute | solution.py:379
  14.3 1.3 %collective-permute-start.3 = (f32[16,128]{1,0:T(8,128)S(1)}, f32[16,128]{1,0:T(8,128)S(1)}, u32[]{:S(2)}, u32[]{:S(2)}) collective-permute-start(f32[16,128]{1,0:T(8,128)S(1)} %get-tuple-element.45), channel_id=1, source_target_pairs={{0,1},{1,0},{2,3},{3,2},{4,5},{5,4},{6,7},{7,6},{8,16},{9,17},{10,... | collective-permute-start | bytes 24584 | tf_op jit(solution)/shard_map/ppermute | solution.py:379
  15.6 1.1 %shard_map.132 = (f32[80,128]{1,0:T(8,128)S(1)}, f32[16,128,128]{2,1,0:T(8,128)S(1)}, f32[64,128,128]{2,1,0:T(8,128)S(1)}) custom-call(s32[4,4]{1,0:T(4,128)S(1)} %copy-done.1, s32[4,4,4]{2,1,0:T(4,128)S(1)} %copy-done, s32[4]{0:T(128)S(1)} %copy-done.2, f32[16,128,128]{2,1,0:T(8,128)S(1)} %get-tuple-element.32.self_in, ...), custom_call_target="tpu_custom_call" | custom-call | tf_op jit(solution)/shard_map/pallas_call | solution.py:404
  16.7 1.1 %shard_map.134.early = f32[40,128]{1,0:T(8,128)S(1)} custom-call(f32[80,128]{1,0:T(8,128)S(1)} %get-tuple-element.34.mask, f32[16,128,128]{2,1,0:T(8,128)S(1)} %get-tuple-element.35.selfs, f32[64,128,128]{2,1,0:T(8,128)S(1)} %get-tuple-element.36.edges, f32[4,128,128]{2,1,0:T(8,128)S(1)} %get-tuple-element.37.ghosts, ...), custom_call_target="tpu_custom_call" | custom-call | tf_op jit(solution)/shard_map/pallas_call | solution.py:404
  17.8 0.0 collective-permute-done.2.rim1
  17.8 0.0 collective-permute-done.3.rim2
  17.8 0.8 %shard_map.135 = (f32[40,128]{1,0:T(8,128)S(1)}, f32[40,128]{1,0:T(8,128)S(1)}, f32[40,128]{1,0:T(8,128)S(1)}, f32[16,128]{1,0:T(8,128)S(1)}, f32[16,128]{1,0:T(8,128)S(1)}) custom-call(f32[80,128]{1,0:T(8,128)S(1)} %get-tuple-element.34.mask, f32[16,128,128]{2,1,0:T(8,128)S(1)} %get-tuple-element.35.selfs, f32[64,128,128]{2,1,0:T(8,128)S(1)} %get-tuple-element.36.edges, ...), custom_call_target="tpu_custom_call" | custom-call | tf_op jit(solution)/shard_map/pallas_call | solution.py:404
  18.6 0.1 collective-permute-start.4
  18.7 3.0 %collective-permute-start.5 = (f32[16,128]{1,0:T(8,128)S(1)}, f32[16,128]{1,0:T(8,128)S(1)}, u32[]{:S(2)}, u32[]{:S(2)}) collective-permute-start(f32[16,128]{1,0:T(8,128)S(1)} %get-tuple-element.48), channel_id=1, source_target_pairs={{0,7},{1,2},{2,1},{3,4},{4,3},{5,6},{6,5},{7,0},{8,15},{9,10},{10,... | collective-permute-start | bytes 24584 | tf_op jit(solution)/shard_map/ppermute | solution.py:379
  21.8 0.0 collective-permute-done.4.refs_1_
  21.8 1.0 %collective-permute-done.5.refs_2_ = f32[16,128]{1,0:T(8,128)S(1)} collective-permute-done((f32[16,128]{1,0:T(8,128)S(1)}, f32[16,128]{1,0:T(8,128)S(1)}, u32[]{:S(2)}, u32[]{:S(2)}) %collective-permute-start.5) | collective-permute-done | bytes 8224 | tf_op jit(solution)/shard_map/ppermute | solution.py:379
  22.8 1.7 %collective-permute-start.6 = (f32[8,128]{1,0:T(8,128)S(1)}, f32[8,128]{1,0:T(8,128)S(1)}, u32[]{:S(2)}, u32[]{:S(2)}) collective-permute-start(f32[8,128]{1,0:T(8,128)S(1)} %get-tuple-element.52), channel_id=1, source_target_pairs={{0,8},{1,9},{2,10},{3,11},{4,12},{5,13},{6,14},{7,15},{8,0},{9,1},... | collective-permute-start | bytes 12296 | tf_op jit(solution)/shard_map/ppermute | solution.py:379
  24.5 0.3 collective-permute-start.7
  24.8 1.1 %shard_map.137.early = f32[40,128]{1,0:T(8,128)S(1)} custom-call(f32[80,128]{1,0:T(8,128)S(1)} %get-tuple-element.34.mask, f32[16,128,128]{2,1,0:T(8,128)S(1)} %get-tuple-element.35.selfs, f32[64,128,128]{2,1,0:T(8,128)S(1)} %get-tuple-element.36.edges, f32[4,128,128]{2,1,0:T(8,128)S(1)} %get-tuple-element.37.ghosts, ...), custom_call_target="tpu_custom_call" | custom-call | tf_op jit(solution)/shard_map/pallas_call | solution.py:404
  25.9 0.0 collective-permute-done.6.rim1
  25.9 2.0 %collective-permute-done.7.rim2 = f32[8,128]{1,0:T(8,128)S(1)} collective-permute-done((f32[8,128]{1,0:T(8,128)S(1)}, f32[8,128]{1,0:T(8,128)S(1)}, u32[]{:S(2)}, u32[]{:S(2)}) %collective-permute-start.7) | collective-permute-done | bytes 4128 | tf_op jit(solution)/shard_map/ppermute | solution.py:379
  27.8 1.5 %shard_map.138 = (f32[40,128]{1,0:T(8,128)S(1)}, f32[40,128]{1,0:T(8,128)S(1)}, f32[16,128]{1,0:T(8,128)S(1)}, f32[16,128]{1,0:T(8,128)S(1)}, f32[256,128]{1,0:T(8,128)}) custom-call(f32[80,128]{1,0:T(8,128)S(1)} %get-tuple-element.34.mask, f32[16,128,128]{2,1,0:T(8,128)S(1)} %get-tuple-element.35.selfs, f32[64,128,128]{2,1,0:T(8,128)S(1)} %get-tuple-element.36.edges, ...), custom_call_target="tpu_custom_call" | custom-call | tf_op jit(solution)/shard_map/pallas_call | solution.py:404
  29.4 13.2 %all-to-all-start = ((f32[256,1,128]{2,1,0:T(1,128)}), f32[256,1,128]{2,1,0:T(1,128)S(1)}, u32[]{:S(2)}, u32[]{:S(2)}) async-start(f32[256,1,128]{2,1,0:T(1,128)} %bitcast.3), calls=%async_computation | async-start | bytes 262144 | tf_op jit(solution)/shard_map/all_to_all | solution.py:483
  42.6 1.6 %collective-permute-start.8 = (f32[16,128]{1,0:T(8,128)S(1)}, f32[16,128]{1,0:T(8,128)S(1)}, u32[]{:S(2)}, u32[]{:S(2)}) collective-permute-start(f32[16,128]{1,0:T(8,128)S(1)} %get-tuple-element.56), channel_id=1, source_target_pairs={{0,1},{1,0},{2,3},{3,2},{4,5},{5,4},{6,7},{7,6},{8,9},{9,8},{10,11... | collective-permute-start | bytes 24584 | tf_op jit(solution)/shard_map/ppermute | solution.py:379
  44.2 3.7 %collective-permute-start.9 = (f32[16,128]{1,0:T(8,128)S(1)}, f32[16,128]{1,0:T(8,128)S(1)}, u32[]{:S(2)}, u32[]{:S(2)}) collective-permute-start(f32[16,128]{1,0:T(8,128)S(1)} %get-tuple-element.57), channel_id=1, source_target_pairs={{0,7},{1,2},{2,1},{3,4},{4,3},{5,6},{6,5},{7,0},{8,15},{9,10},{10,... | collective-permute-start | bytes 24584 | tf_op jit(solution)/shard_map/ppermute | solution.py:379
  47.9 0.0 collective-permute-done.8.refs_1_
  47.9 1.5 %collective-permute-done.9.refs_2_ = f32[16,128]{1,0:T(8,128)S(1)} collective-permute-done((f32[16,128]{1,0:T(8,128)S(1)}, f32[16,128]{1,0:T(8,128)S(1)}, u32[]{:S(2)}, u32[]{:S(2)}) %collective-permute-start.9) | collective-permute-done | bytes 8224 | tf_op jit(solution)/shard_map/ppermute | solution.py:379
  49.4 1.2 %collective-permute-start.10 = (f32[8,128]{1,0:T(8,128)S(1)}, f32[8,128]{1,0:T(8,128)S(1)}, u32[]{:S(2)}, u32[]{:S(2)}) collective-permute-start(f32[8,128]{1,0:T(8,128)S(1)} %get-tuple-element.59), channel_id=1, source_target_pairs={{0,8},{1,9},{2,10},{3,11},{4,12},{5,13},{6,14},{7,15},{8,0},{9,1},... | collective-permute-start | bytes 12296 | tf_op jit(solution)/shard_map/ppermute | solution.py:379
  50.6 1.2 %collective-permute-start.11 = (f32[8,128]{1,0:T(8,128)S(1)}, f32[8,128]{1,0:T(8,128)S(1)}, u32[]{:S(2)}, u32[]{:S(2)}) collective-permute-start(f32[8,128]{1,0:T(8,128)S(1)} %get-tuple-element.60), channel_id=1, source_target_pairs={{0,1},{1,0},{2,3},{3,2},{4,5},{5,4},{6,7},{7,6},{8,16},{9,17},{10,... | collective-permute-start | bytes 12296 | tf_op jit(solution)/shard_map/ppermute | solution.py:379
  51.9 2.1 %collective-permute-done.11.rim2 = f32[8,128]{1,0:T(8,128)S(1)} collective-permute-done((f32[8,128]{1,0:T(8,128)S(1)}, f32[8,128]{1,0:T(8,128)S(1)}, u32[]{:S(2)}, u32[]{:S(2)}) %collective-permute-start.11) | collective-permute-done | bytes 4128 | tf_op jit(solution)/shard_map/ppermute | solution.py:379
  54.0 1.7 %all-to-all-done = f32[256,1,128]{2,1,0:T(1,128)S(1)} async-done(((f32[256,1,128]{2,1,0:T(1,128)}), f32[256,1,128]{2,1,0:T(1,128)S(1)}, u32[]{:S(2)}, u32[]{:S(2)}) %all-to-all-start) | async-done | bytes 131104 | tf_op jit(solution)/shard_map/all_to_all | solution.py:483
  55.7 1.0 %shard_map.140 = (f32[4,4,128]{2,1,0:T(4,128)}, f32[4,4,128]{2,1,0:T(4,128)}) custom-call(f32[256,128]{1,0:T(8,128)S(1)} %bitcast.6, f32[40,128]{1,0:T(8,128)S(1)} %get-tuple-element.58.total, f32[8,128]{1,0:T(8,128)S(1)} %collective-permute-done.10.rim1, f32[8,128]{1,0:T(8,128)S(1)} %collective-permute-done.11.rim2, f32[40,128]{1,0:T(8,128)S(1)} %get-tuple-element.51.s_ref, ...), custom_call_target="tpu_custom_call" | custom-call | tf_op jit(solution)/shard_map/pallas_call | solution.py:487
  (10 shorter events, 0.1 us)
Async XLA Ops:
  0.6 15.0 %copy-start.2 = (s32[4]{0:T(128)S(1)}, s32[4]{0:T(128)}, u32[]{:S(2)}) copy-start(s32[4]{0:T(128)} %owner.1) | copy-start | bytes 52
  0.6 15.0 %copy-start = (s32[4,4,4]{2,1,0:T(4,128)S(1)}, s32[4,4,4]{2,1,0:T(4,128)}, u32[]{:S(2)}) copy-start(s32[4,4,4]{2,1,0:T(4,128)} %offset.1) | copy-start | bytes 772
  0.7 15.0 %copy-start.1 = (s32[4,4]{1,0:T(4,128)S(1)}, s32[4,4]{1,0:T(4,128)}, u32[]{:S(2)}) copy-start(s32[4,4]{1,0:T(4,128)} %count.1) | copy-start | bytes 196
  4.2 7.2 %collective-permute-start = (f32[16,128]{1,0:T(8,128)S(1)}, f32[16,128]{1,0:T(8,128)S(1)}, u32[]{:S(2)}, u32[]{:S(2)}) collective-permute-start(f32[16,128]{1,0:T(8,128)S(1)} %get-tuple-element.39), channel_id=1, source_target_pairs={{0,1},{1,0},{2,3},{3,2},{4,5},{5,4},{6,7},{7,6},{8,9},{9,8},{10,11... | collective-permute-start | bytes 24584 | tf_op jit(solution)/shard_map/ppermute | solution.py:379
  6.7 5.7 %collective-permute-start.1 = (f32[16,128]{1,0:T(8,128)S(1)}, f32[16,128]{1,0:T(8,128)S(1)}, u32[]{:S(2)}, u32[]{:S(2)}) collective-permute-start(f32[16,128]{1,0:T(8,128)S(1)} %get-tuple-element.40), channel_id=1, source_target_pairs={{0,7},{1,2},{2,1},{3,4},{4,3},{5,6},{6,5},{7,0},{8,15},{9,10},{10,... | collective-permute-start | bytes 24584 | tf_op jit(solution)/shard_map/ppermute | solution.py:379
  12.4 5.4 %collective-permute-start.2 = (f32[16,128]{1,0:T(8,128)S(1)}, f32[16,128]{1,0:T(8,128)S(1)}, u32[]{:S(2)}, u32[]{:S(2)}) collective-permute-start(f32[16,128]{1,0:T(8,128)S(1)} %get-tuple-element.44), channel_id=1, source_target_pairs={{0,8},{1,9},{2,10},{3,11},{4,12},{5,13},{6,14},{7,15},{8,0},{9,1},... | collective-permute-start | bytes 24584 | tf_op jit(solution)/shard_map/ppermute | solution.py:379
  14.3 3.5 %collective-permute-start.3 = (f32[16,128]{1,0:T(8,128)S(1)}, f32[16,128]{1,0:T(8,128)S(1)}, u32[]{:S(2)}, u32[]{:S(2)}) collective-permute-start(f32[16,128]{1,0:T(8,128)S(1)} %get-tuple-element.45), channel_id=1, source_target_pairs={{0,1},{1,0},{2,3},{3,2},{4,5},{5,4},{6,7},{7,6},{8,16},{9,17},{10,... | collective-permute-start | bytes 24584 | tf_op jit(solution)/shard_map/ppermute | solution.py:379
  18.6 3.1 %collective-permute-start.4 = (f32[16,128]{1,0:T(8,128)S(1)}, f32[16,128]{1,0:T(8,128)S(1)}, u32[]{:S(2)}, u32[]{:S(2)}) collective-permute-start(f32[16,128]{1,0:T(8,128)S(1)} %get-tuple-element.47), channel_id=1, source_target_pairs={{0,1},{1,0},{2,3},{3,2},{4,5},{5,4},{6,7},{7,6},{8,9},{9,8},{10,11... | collective-permute-start | bytes 24584 | tf_op jit(solution)/shard_map/ppermute | solution.py:379
  18.7 4.1 %collective-permute-start.5 = (f32[16,128]{1,0:T(8,128)S(1)}, f32[16,128]{1,0:T(8,128)S(1)}, u32[]{:S(2)}, u32[]{:S(2)}) collective-permute-start(f32[16,128]{1,0:T(8,128)S(1)} %get-tuple-element.48), channel_id=1, source_target_pairs={{0,7},{1,2},{2,1},{3,4},{4,3},{5,6},{6,5},{7,0},{8,15},{9,10},{10,... | collective-permute-start | bytes 24584 | tf_op jit(solution)/shard_map/ppermute | solution.py:379
  22.8 3.0 %collective-permute-start.6 = (f32[8,128]{1,0:T(8,128)S(1)}, f32[8,128]{1,0:T(8,128)S(1)}, u32[]{:S(2)}, u32[]{:S(2)}) collective-permute-start(f32[8,128]{1,0:T(8,128)S(1)} %get-tuple-element.52), channel_id=1, source_target_pairs={{0,8},{1,9},{2,10},{3,11},{4,12},{5,13},{6,14},{7,15},{8,0},{9,1},... | collective-permute-start | bytes 12296 | tf_op jit(solution)/shard_map/ppermute | solution.py:379
  24.5 3.3 %collective-permute-start.7 = (f32[8,128]{1,0:T(8,128)S(1)}, f32[8,128]{1,0:T(8,128)S(1)}, u32[]{:S(2)}, u32[]{:S(2)}) collective-permute-start(f32[8,128]{1,0:T(8,128)S(1)} %get-tuple-element.53), channel_id=1, source_target_pairs={{0,1},{1,0},{2,3},{3,2},{4,5},{5,4},{6,7},{7,6},{8,16},{9,17},{10,... | collective-permute-start | bytes 12296 | tf_op jit(solution)/shard_map/ppermute | solution.py:379
  29.4 26.3 %all-to-all-start = ((f32[256,1,128]{2,1,0:T(1,128)}), f32[256,1,128]{2,1,0:T(1,128)S(1)}, u32[]{:S(2)}, u32[]{:S(2)}) async-start(f32[256,1,128]{2,1,0:T(1,128)} %bitcast.3), calls=%async_computation | async-start | bytes 262144 | tf_op jit(solution)/shard_map/all_to_all | solution.py:483
  42.6 5.3 %collective-permute-start.8 = (f32[16,128]{1,0:T(8,128)S(1)}, f32[16,128]{1,0:T(8,128)S(1)}, u32[]{:S(2)}, u32[]{:S(2)}) collective-permute-start(f32[16,128]{1,0:T(8,128)S(1)} %get-tuple-element.56), channel_id=1, source_target_pairs={{0,1},{1,0},{2,3},{3,2},{4,5},{5,4},{6,7},{7,6},{8,9},{9,8},{10,11... | collective-permute-start | bytes 24584 | tf_op jit(solution)/shard_map/ppermute | solution.py:379
  44.2 5.2 %collective-permute-start.9 = (f32[16,128]{1,0:T(8,128)S(1)}, f32[16,128]{1,0:T(8,128)S(1)}, u32[]{:S(2)}, u32[]{:S(2)}) collective-permute-start(f32[16,128]{1,0:T(8,128)S(1)} %get-tuple-element.57), channel_id=1, source_target_pairs={{0,7},{1,2},{2,1},{3,4},{4,3},{5,6},{6,5},{7,0},{8,15},{9,10},{10,... | collective-permute-start | bytes 24584 | tf_op jit(solution)/shard_map/ppermute | solution.py:379
  49.4 2.5 %collective-permute-start.10 = (f32[8,128]{1,0:T(8,128)S(1)}, f32[8,128]{1,0:T(8,128)S(1)}, u32[]{:S(2)}, u32[]{:S(2)}) collective-permute-start(f32[8,128]{1,0:T(8,128)S(1)} %get-tuple-element.59), channel_id=1, source_target_pairs={{0,8},{1,9},{2,10},{3,11},{4,12},{5,13},{6,14},{7,15},{8,0},{9,1},... | collective-permute-start | bytes 12296 | tf_op jit(solution)/shard_map/ppermute | solution.py:379
  50.6 3.3 %collective-permute-start.11 = (f32[8,128]{1,0:T(8,128)S(1)}, f32[8,128]{1,0:T(8,128)S(1)}, u32[]{:S(2)}, u32[]{:S(2)}) collective-permute-start(f32[8,128]{1,0:T(8,128)S(1)} %get-tuple-element.60), channel_id=1, source_target_pairs={{0,1},{1,0},{2,3},{3,2},{4,5},{5,4},{6,7},{7,6},{8,16},{9,17},{10,... | collective-permute-start | bytes 12296 | tf_op jit(solution)/shard_map/ppermute | solution.py:379

commit v7 on v6

--- a/solution.py
+++ b/solution.py
@@ -123,8 +123,11 @@
         part = pl.ds(r * cols, cols)
         pltpu.make_async_copy(self_hbm.at[part], self_in.at[part], self_sem.at[r]).start()
     for r in range(rows):
-        part = pl.ds(r * cols * slots, cols * slots)
-        pltpu.make_async_copy(edge_hbm.at[part], edge_in.at[part], edge_sem.at[r]).start()
+        for h in range(2):
+            part = pl.ds((2 * r + h) * cols * slots // 2, cols * slots // 2)
+            pltpu.make_async_copy(
+                edge_hbm.at[part], edge_in.at[part], edge_sem.at[2 * r + h]
+            ).start()
     count, offset, owner, mirror, gain, vel, acc, grad, dens, weight = staged
     for copy in small:
         copy.wait()
@@ -169,9 +172,13 @@
     for r in range(rows):
         part = pl.ds(r * cols, cols)
         pltpu.make_async_copy(self_hbm.at[part], self_in.at[part], self_sem.at[r]).wait()
-        part = pl.ds(r * cols * slots, cols * slots)
-        pltpu.make_async_copy(edge_hbm.at[part], edge_in.at[part], edge_sem.at[r]).wait()
         for c in range(cols):
+            if c % 2 == 0:
+                h = 2 * c // cols
+                part = pl.ds((2 * r + h) * cols * slots // 2, cols * slots // 2)
+                pltpu.make_async_copy(
+                    edge_hbm.at[part], edge_in.at[part], edge_sem.at[2 * r + h]
+                ).wait()
             block = r * cols + c
             at = r * STRIDE + c + 1
             tile = jnp.where(eye, 0.0, self_in[block])
@@ -452,7 +459,7 @@
                 edge_tiles.reshape(rows * cols * slots, size, size),
             ]
         ],
-        staged + [pltpu.SemaphoreType.DMA((n,)) for n in (len(small), rows, rows)],
+        staged + [pltpu.SemaphoreType.DMA((n,)) for n in (len(small), rows, 2 * rows)],
         limit=10,
     )
     matrix = [*call(

time: 56.8 us -> 57.3 us (level)
  no operation moved by 1% of the time
where the time goes in v7:
time: 57.3 us; the launch traced here: 57.1 us
  starting transfers between devices  36.5 us (64%)
  Pallas kernels  10.6 us (18%)
  waiting for transfers between devices  9.33 us (16%)
  between operations  0.74 us (1%)
    ppermute x12, starting transfers between devices, swap(): return lax.ppermute(value, ('slab', 'cross'), pairs)  23.3 us
    all_to_all x1, starting transfers between devices, per_device(): gathered = lax.all_to_all(sums, ('slab', 'cross'), 0, 0, tiled=True)  13.2 us
    pallas_call x9, Pallas kernels, call(): pl.pallas_call(functools.partial(kernel, rows, cols, *extra), out_shape=[...  9.58 us
    ppermute x12, waiting for transfers between devices, swap(): return lax.ppermute(value, ('slab', 'cross'), pairs)  7.59 us
    all_to_all x1, waiting for transfers between devices, per_device(): gathered = lax.all_to_all(sums, ('slab', 'cross'), 0, 0, tiled=True)  1.74 us
  transfers between devices with their start and end apart: 13, of which 6 were waited for; matrix products, arithmetic and copies ran while one was open for 0% of the time, Pallas kernels for 6%

profile of v7, /device:TPU:1, one launch (start us, length us, event | category | flops | bytes accessed | tf_op | source)
XLA Modules:
  0.0 57.1 jit_solution(4564879217604345987)
XLA Ops:
  0.7 3.9 %shard_map.131 = (f32[40,128]{1,0:T(8,128)S(1)}, f32[40,128]{1,0:T(8,128)S(1)}, f32[16,128]{1,0:T(8,128)S(1)}, f32[16,128]{1,0:T(8,128)S(1)}, f32[16,128,128]{2,...) custom-call(s32[4,4]{1,0:T(4,128)} %count.1, s32[4,4,4]{2,1,0:T(4,128)} %offset.1, s32[4]{0:T(128)} %owner.1, ...), custom_call_target="tpu_custom_call" | custom-call | tf_op jit(solution)/shard_map/pallas_call | solution.py:411
  4.6 2.5 %collective-permute-start = (f32[16,128]{1,0:T(8,128)S(1)}, f32[16,128]{1,0:T(8,128)S(1)}, u32[]{:S(2)}, u32[]{:S(2)}) collective-permute-start(f32[16,128]{1,0:T(8,128)S(1)} %get-tuple-element.39), channel_id=1, source_target_pairs={{0,1},{1,0},{2,3},{3,2},{4,5},{5,4},{6,7},{7,6},{8,9},{9,8},{10,11... | collective-permute-start | bytes 24584 | tf_op jit(solution)/shard_map/ppermute | solution.py:386
  7.2 4.7 %collective-permute-start.1 = (f32[16,128]{1,0:T(8,128)S(1)}, f32[16,128]{1,0:T(8,128)S(1)}, u32[]{:S(2)}, u32[]{:S(2)}) collective-permute-start(f32[16,128]{1,0:T(8,128)S(1)} %get-tuple-element.40), channel_id=1, source_target_pairs={{0,7},{1,2},{2,1},{3,4},{4,3},{5,6},{6,5},{7,0},{8,15},{9,10},{10,... | collective-permute-start | bytes 24584 | tf_op jit(solution)/shard_map/ppermute | solution.py:386
  11.8 0.0 collective-permute-done.refs_1_
  11.8 1.0 %collective-permute-done.1.refs_2_ = f32[16,128]{1,0:T(8,128)S(1)} collective-permute-done((f32[16,128]{1,0:T(8,128)S(1)}, f32[16,128]{1,0:T(8,128)S(1)}, u32[]{:S(2)}, u32[]{:S(2)}) %collective-permute-start.1) | collective-permute-done | bytes 8224 | tf_op jit(solution)/shard_map/ppermute | solution.py:386
  12.9 1.9 %collective-permute-start.2 = (f32[16,128]{1,0:T(8,128)S(1)}, f32[16,128]{1,0:T(8,128)S(1)}, u32[]{:S(2)}, u32[]{:S(2)}) collective-permute-start(f32[16,128]{1,0:T(8,128)S(1)} %get-tuple-element.44), channel_id=1, source_target_pairs={{0,8},{1,9},{2,10},{3,11},{4,12},{5,13},{6,14},{7,15},{8,0},{9,1},... | collective-permute-start | bytes 24584 | tf_op jit(solution)/shard_map/ppermute | solution.py:386
  14.8 1.3 %collective-permute-start.3 = (f32[16,128]{1,0:T(8,128)S(1)}, f32[16,128]{1,0:T(8,128)S(1)}, u32[]{:S(2)}, u32[]{:S(2)}) collective-permute-start(f32[16,128]{1,0:T(8,128)S(1)} %get-tuple-element.45), channel_id=1, source_target_pairs={{0,1},{1,0},{2,3},{3,2},{4,5},{5,4},{6,7},{7,6},{8,16},{9,17},{10,... | collective-permute-start | bytes 24584 | tf_op jit(solution)/shard_map/ppermute | solution.py:386
  16.1 1.1 %shard_map.132 = (f32[80,128]{1,0:T(8,128)S(1)}, f32[16,128,128]{2,1,0:T(8,128)S(1)}, f32[64,128,128]{2,1,0:T(8,128)S(1)}) custom-call(s32[4,4]{1,0:T(4,128)S(1)} %copy-done.1, s32[4,4,4]{2,1,0:T(4,128)S(1)} %copy-done, s32[4]{0:T(128)S(1)} %copy-done.2, f32[16,128,128]{2,1,0:T(8,128)S(1)} %get-tuple-element.32.self_in, ...), custom_call_target="tpu_custom_call" | custom-call | tf_op jit(solution)/shard_map/pallas_call | solution.py:411
  17.2 1.1 %shard_map.134.early = f32[40,128]{1,0:T(8,128)S(1)} custom-call(f32[80,128]{1,0:T(8,128)S(1)} %get-tuple-element.34.mask, f32[16,128,128]{2,1,0:T(8,128)S(1)} %get-tuple-element.35.selfs, f32[64,128,128]{2,1,0:T(8,128)S(1)} %get-tuple-element.36.edges, f32[4,128,128]{2,1,0:T(8,128)S(1)} %get-tuple-element.37.ghosts, ...), custom_call_target="tpu_custom_call" | custom-call | tf_op jit(solution)/shard_map/pallas_call | solution.py:411
  18.3 0.0 collective-permute-done.2.rim1
  18.3 0.0 collective-permute-done.3.rim2
  18.3 0.8 %shard_map.135 = (f32[40,128]{1,0:T(8,128)S(1)}, f32[40,128]{1,0:T(8,128)S(1)}, f32[40,128]{1,0:T(8,128)S(1)}, f32[16,128]{1,0:T(8,128)S(1)}, f32[16,128]{1,0:T(8,128)S(1)}) custom-call(f32[80,128]{1,0:T(8,128)S(1)} %get-tuple-element.34.mask, f32[16,128,128]{2,1,0:T(8,128)S(1)} %get-tuple-element.35.selfs, f32[64,128,128]{2,1,0:T(8,128)S(1)} %get-tuple-element.36.edges, ...), custom_call_target="tpu_custom_call" | custom-call | tf_op jit(solution)/shard_map/pallas_call | solution.py:411
  19.1 0.1 collective-permute-start.4
  19.2 3.0 %collective-permute-start.5 = (f32[16,128]{1,0:T(8,128)S(1)}, f32[16,128]{1,0:T(8,128)S(1)}, u32[]{:S(2)}, u32[]{:S(2)}) collective-permute-start(f32[16,128]{1,0:T(8,128)S(1)} %get-tuple-element.48), channel_id=1, source_target_pairs={{0,7},{1,2},{2,1},{3,4},{4,3},{5,6},{6,5},{7,0},{8,15},{9,10},{10,... | collective-permute-start | bytes 24584 | tf_op jit(solution)/shard_map/ppermute | solution.py:386
  22.2 0.0 collective-permute-done.4.refs_1_
  22.2 1.0 %collective-permute-done.5.refs_2_ = f32[16,128]{1,0:T(8,128)S(1)} collective-permute-done((f32[16,128]{1,0:T(8,128)S(1)}, f32[16,128]{1,0:T(8,128)S(1)}, u32[]{:S(2)}, u32[]{:S(2)}) %collective-permute-start.5) | collective-permute-done | bytes 8224 | tf_op jit(solution)/shard_map/ppermute | solution.py:386
  23.3 1.7 %collective-permute-start.6 = (f32[8,128]{1,0:T(8,128)S(1)}, f32[8,128]{1,0:T(8,128)S(1)}, u32[]{:S(2)}, u32[]{:S(2)}) collective-permute-start(f32[8,128]{1,0:T(8,128)S(1)} %get-tuple-element.52), channel_id=1, source_target_pairs={{0,8},{1,9},{2,10},{3,11},{4,12},{5,13},{6,14},{7,15},{8,0},{9,1},... | collective-permute-start | bytes 12296 | tf_op jit(solution)/shard_map/ppermute | solution.py:386
  25.0 0.3 collective-permute-start.7
  25.3 1.1 %shard_map.137.early = f32[40,128]{1,0:T(8,128)S(1)} custom-call(f32[80,128]{1,0:T(8,128)S(1)} %get-tuple-element.34.mask, f32[16,128,128]{2,1,0:T(8,128)S(1)} %get-tuple-element.35.selfs, f32[64,128,128]{2,1,0:T(8,128)S(1)} %get-tuple-element.36.edges, f32[4,128,128]{2,1,0:T(8,128)S(1)} %get-tuple-element.37.ghosts, ...), custom_call_target="tpu_custom_call" | custom-call | tf_op jit(solution)/shard_map/pallas_call | solution.py:411
  26.3 2.0 %collective-permute-done.7.rim2 = f32[8,128]{1,0:T(8,128)S(1)} collective-permute-done((f32[8,128]{1,0:T(8,128)S(1)}, f32[8,128]{1,0:T(8,128)S(1)}, u32[]{:S(2)}, u32[]{:S(2)}) %collective-permute-start.7) | collective-permute-done | bytes 4128 | tf_op jit(solution)/shard_map/ppermute | solution.py:386
  28.3 1.5 %shard_map.138 = (f32[40,128]{1,0:T(8,128)S(1)}, f32[40,128]{1,0:T(8,128)S(1)}, f32[16,128]{1,0:T(8,128)S(1)}, f32[16,128]{1,0:T(8,128)S(1)}, f32[256,128]{1,0:T(8,128)}) custom-call(f32[80,128]{1,0:T(8,128)S(1)} %get-tuple-element.34.mask, f32[16,128,128]{2,1,0:T(8,128)S(1)} %get-tuple-element.35.selfs, f32[64,128,128]{2,1,0:T(8,128)S(1)} %get-tuple-element.36.edges, ...), custom_call_target="tpu_custom_call" | custom-call | tf_op jit(solution)/shard_map/pallas_call | solution.py:411
  29.8 13.2 %all-to-all-start = ((f32[256,1,128]{2,1,0:T(1,128)}), f32[256,1,128]{2,1,0:T(1,128)S(1)}, u32[]{:S(2)}, u32[]{:S(2)}) async-start(f32[256,1,128]{2,1,0:T(1,128)} %bitcast.3), calls=%async_computation | async-start | bytes 262144 | tf_op jit(solution)/shard_map/all_to_all | solution.py:490
  43.1 1.6 %collective-permute-start.8 = (f32[16,128]{1,0:T(8,128)S(1)}, f32[16,128]{1,0:T(8,128)S(1)}, u32[]{:S(2)}, u32[]{:S(2)}) collective-permute-start(f32[16,128]{1,0:T(8,128)S(1)} %get-tuple-element.56), channel_id=1, source_target_pairs={{0,1},{1,0},{2,3},{3,2},{4,5},{5,4},{6,7},{7,6},{8,9},{9,8},{10,11... | collective-permute-start | bytes 24584 | tf_op jit(solution)/shard_map/ppermute | solution.py:386
  44.6 3.7 %collective-permute-start.9 = (f32[16,128]{1,0:T(8,128)S(1)}, f32[16,128]{1,0:T(8,128)S(1)}, u32[]{:S(2)}, u32[]{:S(2)}) collective-permute-start(f32[16,128]{1,0:T(8,128)S(1)} %get-tuple-element.57), channel_id=1, source_target_pairs={{0,7},{1,2},{2,1},{3,4},{4,3},{5,6},{6,5},{7,0},{8,15},{9,10},{10,... | collective-permute-start | bytes 24584 | tf_op jit(solution)/shard_map/ppermute | solution.py:386
  48.4 0.0 collective-permute-done.8.refs_1_
  48.4 1.5 %collective-permute-done.9.refs_2_ = f32[16,128]{1,0:T(8,128)S(1)} collective-permute-done((f32[16,128]{1,0:T(8,128)S(1)}, f32[16,128]{1,0:T(8,128)S(1)}, u32[]{:S(2)}, u32[]{:S(2)}) %collective-permute-start.9) | collective-permute-done | bytes 8224 | tf_op jit(solution)/shard_map/ppermute | solution.py:386
  49.9 1.2 %collective-permute-start.10 = (f32[8,128]{1,0:T(8,128)S(1)}, f32[8,128]{1,0:T(8,128)S(1)}, u32[]{:S(2)}, u32[]{:S(2)}) collective-permute-start(f32[8,128]{1,0:T(8,128)S(1)} %get-tuple-element.59), channel_id=1, source_target_pairs={{0,8},{1,9},{2,10},{3,11},{4,12},{5,13},{6,14},{7,15},{8,0},{9,1},... | collective-permute-start | bytes 12296 | tf_op jit(solution)/shard_map/ppermute | solution.py:386
  51.1 1.2 %collective-permute-start.11 = (f32[8,128]{1,0:T(8,128)S(1)}, f32[8,128]{1,0:T(8,128)S(1)}, u32[]{:S(2)}, u32[]{:S(2)}) collective-permute-start(f32[8,128]{1,0:T(8,128)S(1)} %get-tuple-element.60), channel_id=1, source_target_pairs={{0,1},{1,0},{2,3},{3,2},{4,5},{5,4},{6,7},{7,6},{8,16},{9,17},{10,... | collective-permute-start | bytes 12296 | tf_op jit(solution)/shard_map/ppermute | solution.py:386
  52.3 0.0 collective-permute-done.10.rim1
  52.3 2.1 %collective-permute-done.11.rim2 = f32[8,128]{1,0:T(8,128)S(1)} collective-permute-done((f32[8,128]{1,0:T(8,128)S(1)}, f32[8,128]{1,0:T(8,128)S(1)}, u32[]{:S(2)}, u32[]{:S(2)}) %collective-permute-start.11) | collective-permute-done | bytes 4128 | tf_op jit(solution)/shard_map/ppermute | solution.py:386
  54.4 1.7 %all-to-all-done = f32[256,1,128]{2,1,0:T(1,128)S(1)} async-done(((f32[256,1,128]{2,1,0:T(1,128)}), f32[256,1,128]{2,1,0:T(1,128)S(1)}, u32[]{:S(2)}, u32[]{:S(2)}) %all-to-all-start) | async-done | bytes 131104 | tf_op jit(solution)/shard_map/all_to_all | solution.py:490
  56.2 1.0 %shard_map.140 = (f32[4,4,128]{2,1,0:T(4,128)}, f32[4,4,128]{2,1,0:T(4,128)}) custom-call(f32[256,128]{1,0:T(8,128)S(1)} %bitcast.6, f32[40,128]{1,0:T(8,128)S(1)} %get-tuple-element.58.total, f32[8,128]{1,0:T(8,128)S(1)} %collective-permute-done.10.rim1, f32[8,128]{1,0:T(8,128)S(1)} %collective-permute-done.11.rim2, f32[40,128]{1,0:T(8,128)S(1)} %get-tuple-element.51.s_ref, ...), custom_call_target="tpu_custom_call" | custom-call | tf_op jit(solution)/shard_map/pallas_call | solution.py:494
  (10 shorter events, 0.1 us)
Async XLA Ops:
  0.6 15.5 %copy-start.2 = (s32[4]{0:T(128)S(1)}, s32[4]{0:T(128)}, u32[]{:S(2)}) copy-start(s32[4]{0:T(128)} %owner.1) | copy-start | bytes 52
  0.6 15.4 %copy-start = (s32[4,4,4]{2,1,0:T(4,128)S(1)}, s32[4,4,4]{2,1,0:T(4,128)}, u32[]{:S(2)}) copy-start(s32[4,4,4]{2,1,0:T(4,128)} %offset.1) | copy-start | bytes 772
  0.7 15.4 %copy-start.1 = (s32[4,4]{1,0:T(4,128)S(1)}, s32[4,4]{1,0:T(4,128)}, u32[]{:S(2)}) copy-start(s32[4,4]{1,0:T(4,128)} %count.1) | copy-start | bytes 196
  4.6 7.2 %collective-permute-start = (f32[16,128]{1,0:T(8,128)S(1)}, f32[16,128]{1,0:T(8,128)S(1)}, u32[]{:S(2)}, u32[]{:S(2)}) collective-permute-start(f32[16,128]{1,0:T(8,128)S(1)} %get-tuple-element.39), channel_id=1, source_target_pairs={{0,1},{1,0},{2,3},{3,2},{4,5},{5,4},{6,7},{7,6},{8,9},{9,8},{10,11... | collective-permute-start | bytes 24584 | tf_op jit(solution)/shard_map/ppermute | solution.py:386
  7.2 5.7 %collective-permute-start.1 = (f32[16,128]{1,0:T(8,128)S(1)}, f32[16,128]{1,0:T(8,128)S(1)}, u32[]{:S(2)}, u32[]{:S(2)}) collective-permute-start(f32[16,128]{1,0:T(8,128)S(1)} %get-tuple-element.40), channel_id=1, source_target_pairs={{0,7},{1,2},{2,1},{3,4},{4,3},{5,6},{6,5},{7,0},{8,15},{9,10},{10,... | collective-permute-start | bytes 24584 | tf_op jit(solution)/shard_map/ppermute | solution.py:386
  12.9 5.4 %collective-permute-start.2 = (f32[16,128]{1,0:T(8,128)S(1)}, f32[16,128]{1,0:T(8,128)S(1)}, u32[]{:S(2)}, u32[]{:S(2)}) collective-permute-start(f32[16,128]{1,0:T(8,128)S(1)} %get-tuple-element.44), channel_id=1, source_target_pairs={{0,8},{1,9},{2,10},{3,11},{4,12},{5,13},{6,14},{7,15},{8,0},{9,1},... | collective-permute-start | bytes 24584 | tf_op jit(solution)/shard_map/ppermute | solution.py:386
  14.8 3.5 %collective-permute-start.3 = (f32[16,128]{1,0:T(8,128)S(1)}, f32[16,128]{1,0:T(8,128)S(1)}, u32[]{:S(2)}, u32[]{:S(2)}) collective-permute-start(f32[16,128]{1,0:T(8,128)S(1)} %get-tuple-element.45), channel_id=1, source_target_pairs={{0,1},{1,0},{2,3},{3,2},{4,5},{5,4},{6,7},{7,6},{8,16},{9,17},{10,... | collective-permute-start | bytes 24584 | tf_op jit(solution)/shard_map/ppermute | solution.py:386
  19.1 3.1 %collective-permute-start.4 = (f32[16,128]{1,0:T(8,128)S(1)}, f32[16,128]{1,0:T(8,128)S(1)}, u32[]{:S(2)}, u32[]{:S(2)}) collective-permute-start(f32[16,128]{1,0:T(8,128)S(1)} %get-tuple-element.47), channel_id=1, source_target_pairs={{0,1},{1,0},{2,3},{3,2},{4,5},{5,4},{6,7},{7,6},{8,9},{9,8},{10,11... | collective-permute-start | bytes 24584 | tf_op jit(solution)/shard_map/ppermute | solution.py:386
  19.2 4.1 %collective-permute-start.5 = (f32[16,128]{1,0:T(8,128)S(1)}, f32[16,128]{1,0:T(8,128)S(1)}, u32[]{:S(2)}, u32[]{:S(2)}) collective-permute-start(f32[16,128]{1,0:T(8,128)S(1)} %get-tuple-element.48), channel_id=1, source_target_pairs={{0,7},{1,2},{2,1},{3,4},{4,3},{5,6},{6,5},{7,0},{8,15},{9,10},{10,... | collective-permute-start | bytes 24584 | tf_op jit(solution)/shard_map/ppermute | solution.py:386
  23.3 3.0 %collective-permute-start.6 = (f32[8,128]{1,0:T(8,128)S(1)}, f32[8,128]{1,0:T(8,128)S(1)}, u32[]{:S(2)}, u32[]{:S(2)}) collective-permute-start(f32[8,128]{1,0:T(8,128)S(1)} %get-tuple-element.52), channel_id=1, source_target_pairs={{0,8},{1,9},{2,10},{3,11},{4,12},{5,13},{6,14},{7,15},{8,0},{9,1},... | collective-permute-start | bytes 12296 | tf_op jit(solution)/shard_map/ppermute | solution.py:386
  25.0 3.3 %collective-permute-start.7 = (f32[8,128]{1,0:T(8,128)S(1)}, f32[8,128]{1,0:T(8,128)S(1)}, u32[]{:S(2)}, u32[]{:S(2)}) collective-permute-start(f32[8,128]{1,0:T(8,128)S(1)} %get-tuple-element.53), channel_id=1, source_target_pairs={{0,1},{1,0},{2,3},{3,2},{4,5},{5,4},{6,7},{7,6},{8,16},{9,17},{10,... | collective-permute-start | bytes 12296 | tf_op jit(solution)/shard_map/ppermute | solution.py:386
  29.8 26.3 %all-to-all-start = ((f32[256,1,128]{2,1,0:T(1,128)}), f32[256,1,128]{2,1,0:T(1,128)S(1)}, u32[]{:S(2)}, u32[]{:S(2)}) async-start(f32[256,1,128]{2,1,0:T(1,128)} %bitcast.3), calls=%async_computation | async-start | bytes 262144 | tf_op jit(solution)/shard_map/all_to_all | solution.py:490
  43.1 5.3 %collective-permute-start.8 = (f32[16,128]{1,0:T(8,128)S(1)}, f32[16,128]{1,0:T(8,128)S(1)}, u32[]{:S(2)}, u32[]{:S(2)}) collective-permute-start(f32[16,128]{1,0:T(8,128)S(1)} %get-tuple-element.56), channel_id=1, source_target_pairs={{0,1},{1,0},{2,3},{3,2},{4,5},{5,4},{6,7},{7,6},{8,9},{9,8},{10,11... | collective-permute-start | bytes 24584 | tf_op jit(solution)/shard_map/ppermute | solution.py:386
  44.6 5.2 %collective-permute-start.9 = (f32[16,128]{1,0:T(8,128)S(1)}, f32[16,128]{1,0:T(8,128)S(1)}, u32[]{:S(2)}, u32[]{:S(2)}) collective-permute-start(f32[16,128]{1,0:T(8,128)S(1)} %get-tuple-element.57), channel_id=1, source_target_pairs={{0,7},{1,2},{2,1},{3,4},{4,3},{5,6},{6,5},{7,0},{8,15},{9,10},{10,... | collective-permute-start | bytes 24584 | tf_op jit(solution)/shard_map/ppermute | solution.py:386
  49.9 2.5 %collective-permute-start.10 = (f32[8,128]{1,0:T(8,128)S(1)}, f32[8,128]{1,0:T(8,128)S(1)}, u32[]{:S(2)}, u32[]{:S(2)}) collective-permute-start(f32[8,128]{1,0:T(8,128)S(1)} %get-tuple-element.59), channel_id=1, source_target_pairs={{0,8},{1,9},{2,10},{3,11},{4,12},{5,13},{6,14},{7,15},{8,0},{9,1},... | collective-permute-start | bytes 12296 | tf_op jit(solution)/shard_map/ppermute | solution.py:386
  51.1 3.3 %collective-permute-start.11 = (f32[8,128]{1,0:T(8,128)S(1)}, f32[8,128]{1,0:T(8,128)S(1)}, u32[]{:S(2)}, u32[]{:S(2)}) collective-permute-start(f32[8,128]{1,0:T(8,128)S(1)} %get-tuple-element.60), channel_id=1, source_target_pairs={{0,1},{1,0},{2,3},{3,2},{4,5},{5,4},{6,7},{7,6},{8,16},{9,17},{10,... | collective-permute-start | bytes 12296 | tf_op jit(solution)/shard_map/ppermute | solution.py:386
